TPU v7x, 32 devices: a whole 2x2x4 slice. The times are simulated.
32 devices in a mesh: groups: 2 (over x), row: 16 (over z, y, core).
Axes of the slice: x: 2, y: 2, z: 4, core: 2. Of those that a mesh axis runs over, the one named last changes fastest.
Arguments:
- object_field: float32 [2, 16384, 384], P(None, ('groups', 'row')), parts along dimension 1, may hold values from -26 to 26
- probe: float32 [2, 2, 256, 256], replicated, may hold values from -4.2 to 4.2
- amplitude: float32 [256, 256, 256], P(('groups', 'row')), parts along dimension 0, may hold values from 0.2 to 27, as said below
- offsets: int32 [256, 2], P(('groups', 'row')), parts along dimension 0, may hold values from 0 to 8191, as said below
Outputs:
- object_grad: float32 [2, 16384, 384], P(None, ('groups', 'row')), parts along dimension 1
- probe_dir: float32 [4, 2, 256, 256], P('groups'), parts along dimension 0
- loss: float32 [2], P('groups'), parts along dimension 0
There are 2 independent parts, one for each index of `groups`. A program takes and returns all parts, laid end to end along the dimension named above; an argument that names none is the same for every part. Nothing has to cross between parts.
Inputs may be any that keep to these rules, and one draw needn't show every extreme that they name: offsets[p, 0] is k * 64 plus a shift below 64 in the rows of device p // 8, with k = p % 8; offsets[p, 1] lies from 0 to 127. `amplitude`: measured amplitudes are positive.
All inputs are finite; a program needn't handle non-finite values.
Results may differ from a plain program's by a relative error of at most 0.0062.
Values sent between devices are 32-bit elements; how exact they have to be, the bound alone decides.
No kernel may reach another device: no remote copies, remote signals or barrier semaphores. Data moves between devices by JAX's collectives and lax.ppermute only.
A program may use at most 128 MiB of HBM per device.

v0:
```python
import math

import jax
import jax.numpy as jnp
from jax import lax
from jax.sharding import PartitionSpec as P


def from_behind(x, axis, by):
    size = lax.axis_size(axis)
    pairs = [(i, i + by) for i in range(size) if 0 <= i + by < size]
    return lax.ppermute(x, axis, pairs)


def dft_tables(size):
    idx = jnp.arange(size, dtype=jnp.int32)
    prod = idx[:, None] * idx[None, :] % size
    angle = prod.astype(jnp.float32) * (2.0 * math.pi / size)
    scale = 1.0 / math.sqrt(size)
    cosine = jnp.cos(angle) * scale
    sine = jnp.sin(angle) * scale
    column = jnp.stack([jnp.stack([cosine, -sine], 1), jnp.stack([sine, cosine], 1)], 0).astype(
        jnp.bfloat16
    )
    rowwise = jnp.stack([jnp.stack([cosine, sine], 1), jnp.stack([-sine, cosine], 1)], 0).astype(
        jnp.bfloat16
    )
    return (column, rowwise)


def window_terms(windows, probe, amplitude, column, rowwise):
    o_re = windows[:, 0][:, None]
    o_im = windows[:, 1][:, None]
    p_re = probe[:, 0][None]
    p_im = probe[:, 1][None]
    wave = jnp.stack([p_re * o_re - p_im * o_im, p_re * o_im + p_im * o_re], 2).astype(jnp.bfloat16)
    half = jnp.einsum("pmcij,cjdk->pmdik", wave, column, preferred_element_type=jnp.float32).astype(
        jnp.bfloat16
    )
    far = jnp.einsum("erdi,pmdil->pmerl", rowwise, half, preferred_element_type=jnp.float32)
    magnitude = jnp.sqrt(jnp.sum(far * far, axis=(1, 2)))
    loss_part = jnp.sum((magnitude - amplitude) ** 2)
    weight = 0.25 * (1.0 - amplitude / jnp.maximum(magnitude, 0.5))
    grad_far = (weight[:, None, None] * far).astype(jnp.bfloat16)
    grad_half = jnp.einsum(
        "erdi,pmerl->pmdil", rowwise, grad_far, preferred_element_type=jnp.float32
    ).astype(jnp.bfloat16)
    grad_wave = jnp.einsum(
        "pmdik,cjdk->pmcij", grad_half, column, preferred_element_type=jnp.float32
    )
    g_re = grad_wave[:, :, 0]
    g_im = grad_wave[:, :, 1]
    win_grad = jnp.stack(
        [jnp.sum(p_re * g_re + p_im * g_im, 1), jnp.sum(p_re * g_im - p_im * g_re, 1)], 1
    )
    probe_grad = jnp.stack(
        [jnp.sum(o_re * g_re + o_im * g_im, 0), jnp.sum(o_re * g_im - o_im * g_re, 0)], 1
    )
    illumination = jnp.sum(windows[:, 0] ** 2 + windows[:, 1] ** 2, 0)
    return (win_grad, probe_grad, illumination, loss_part)


def per_device(object_field, probe, amplitude, offsets):
    tile = object_field.shape[1]
    patch = probe.shape[2]
    count = offsets.shape[0]
    column, rowwise = dft_tables(patch)
    below = from_behind(object_field[:, :patch], "row", -1)
    extended = jnp.concatenate([object_field, below], 1)
    top = lax.axis_index("row") * tile
    rows = offsets[:, 0] - top
    cols = offsets[:, 1]

    def cut(row_start, col_start):
        return lax.dynamic_slice(extended, (jnp.int32(0), row_start, col_start), (2, patch, patch))

    windows = jax.vmap(cut)(rows, cols)
    win_grad, probe_grad, illumination, loss_part = window_terms(
        windows, probe, amplitude, column, rowwise
    )
    loss_total = lax.psum(loss_part, "row")
    grad_ext = jnp.zeros_like(extended)
    for position in range(count):
        start = (jnp.int32(0), rows[position], cols[position])
        current = lax.dynamic_slice(grad_ext, start, (2, patch, patch))
        grad_ext = lax.dynamic_update_slice(grad_ext, current + win_grad[position], start)
    upper = grad_ext[:, :tile]
    lower = grad_ext[:, tile:]
    carried = from_behind(lower, "row", 1)
    object_grad = jnp.concatenate([upper[:, :patch] + carried, upper[:, patch:]], 1)
    probe_sum, illum_sum = lax.psum((probe_grad, illumination), "row")
    probe_dir = probe_sum / jnp.sqrt(illum_sum + 1.0)[None, None]
    total_pixels = count * lax.axis_size("row") * patch * patch
    loss = (loss_total / total_pixels).reshape(1)
    return (object_grad, probe_dir, loss)


def solution(mesh):
    placed = (
        P(None, ("groups", "row"), None),
        P(),
        P(("groups", "row"), None, None),
        P(("groups", "row"), None),
    )
    return jax.shard_map(
        per_device,
        mesh=mesh,
        in_specs=placed,
        out_specs=(P(None, ("groups", "row"), None), P("groups", None, None, None), P("groups")),
        check_vma=False,
    )
```

profile of v0, /device:TPU:0, one launch (start us, length us, event | category | flops | bytes accessed | tf_op | source)
XLA Modules:
  0.0 286.1 jit_solution(10306685527730276282)
XLA Ops:
  54.8 32.5 %while.1 = (s32[]{:T(128)}, f32[2,768,384]{2,1,0:T(8,128)}, s32[8,3]{0,1:T(4,128)S(1)}, f32[8,2,256,256]{3,2,1,0:T(8,128)}, s32[]{:T(128)}) while((s32[]{:T(128)}, f32[2,768,384]{2,1,0:T(8,128)}, s32[8,3]{0,1:T(4,128)S(1)}, f32[8,2,256,256]{3,2,1,0:T(8,128)}, s32[]{:T(128)}) %tuple.55), condition=%wide.while_cond, body=%wide.while_body.sunk | while | flops 2 | bytes 1049717 | solution.py:75
  59.5 3.4 %bitcast_dynamic-update-slice_fusion.2 = f32[8,2,256,256]{3,2,1,0:T(8,128)} fusion(f32[8,2,256,256]{3,2,1,0:T(8,128)} %get-tuple-element.109, s32[]{:T(128)S(6)} %copy.85, f32[2,768,384]{2,1,0:T(8,128)} %get-tuple-element.112, s32[]{:T(128)} %bitcast.212, s32[]{:T(128)} %bitcast.213), kind=kLoop, calls=%fused_computation.clone.1 | loop fusion | bytes 1049604 | tf_op jit(solution)/shard_map/vmap()/gather
  63.5 3.4 %bitcast_dynamic-update-slice_fusion.2 = f32[8,2,256,256]{3,2,1,0:T(8,128)} fusion(f32[8,2,256,256]{3,2,1,0:T(8,128)} %get-tuple-element.109, s32[]{:T(128)S(6)} %copy.85, f32[2,768,384]{2,1,0:T(8,128)} %get-tuple-element.112, s32[]{:T(128)} %bitcast.212, s32[]{:T(128)} %bitcast.213), kind=kLoop, calls=%fused_computation.clone.1 | loop fusion | bytes 1049604 | tf_op jit(solution)/shard_map/vmap()/gather
  67.6 3.4 %bitcast_dynamic-update-slice_fusion.2 = f32[8,2,256,256]{3,2,1,0:T(8,128)} fusion(f32[8,2,256,256]{3,2,1,0:T(8,128)} %get-tuple-element.109, s32[]{:T(128)S(6)} %copy.85, f32[2,768,384]{2,1,0:T(8,128)} %get-tuple-element.112, s32[]{:T(128)} %bitcast.212, s32[]{:T(128)} %bitcast.213), kind=kLoop, calls=%fused_computation.clone.1 | loop fusion | bytes 1049604 | tf_op jit(solution)/shard_map/vmap()/gather
  71.6 3.4 %bitcast_dynamic-update-slice_fusion.2 = f32[8,2,256,256]{3,2,1,0:T(8,128)} fusion(f32[8,2,256,256]{3,2,1,0:T(8,128)} %get-tuple-element.109, s32[]{:T(128)S(6)} %copy.85, f32[2,768,384]{2,1,0:T(8,128)} %get-tuple-element.112, s32[]{:T(128)} %bitcast.212, s32[]{:T(128)} %bitcast.213), kind=kLoop, calls=%fused_computation.clone.1 | loop fusion | bytes 1049604 | tf_op jit(solution)/shard_map/vmap()/gather
  75.7 3.4 %bitcast_dynamic-update-slice_fusion.2 = f32[8,2,256,256]{3,2,1,0:T(8,128)} fusion(f32[8,2,256,256]{3,2,1,0:T(8,128)} %get-tuple-element.109, s32[]{:T(128)S(6)} %copy.85, f32[2,768,384]{2,1,0:T(8,128)} %get-tuple-element.112, s32[]{:T(128)} %bitcast.212, s32[]{:T(128)} %bitcast.213), kind=kLoop, calls=%fused_computation.clone.1 | loop fusion | bytes 1049604 | tf_op jit(solution)/shard_map/vmap()/gather
  79.8 3.4 %bitcast_dynamic-update-slice_fusion.2 = f32[8,2,256,256]{3,2,1,0:T(8,128)} fusion(f32[8,2,256,256]{3,2,1,0:T(8,128)} %get-tuple-element.109, s32[]{:T(128)S(6)} %copy.85, f32[2,768,384]{2,1,0:T(8,128)} %get-tuple-element.112, s32[]{:T(128)} %bitcast.212, s32[]{:T(128)} %bitcast.213), kind=kLoop, calls=%fused_computation.clone.1 | loop fusion | bytes 1049604 | tf_op jit(solution)/shard_map/vmap()/gather
  83.8 3.4 %bitcast_dynamic-update-slice_fusion.2 = f32[8,2,256,256]{3,2,1,0:T(8,128)} fusion(f32[8,2,256,256]{3,2,1,0:T(8,128)} %get-tuple-element.109, s32[]{:T(128)S(6)} %copy.85, f32[2,768,384]{2,1,0:T(8,128)} %get-tuple-element.112, s32[]{:T(128)} %bitcast.212, s32[]{:T(128)} %bitcast.213), kind=kLoop, calls=%fused_computation.clone.1 | loop fusion | bytes 1049604 | tf_op jit(solution)/shard_map/vmap()/gather
  95.4 4.8 %subtract_convert_fusion = (bf16[8,2,1,256,256]{4,3,2,1,0:T(8,128)(2,1)}, bf16[8,2,1,256,256]{4,3,2,1,0:T(8,128)(2,1)}) fusion(f32[8,256,256]{2,1,0:T(8,128)} %slice_bitcast_fusion.2, f32[2,256,256]{2,1,0:T(8,128)S(1)} %get-tuple-element.44, f32[8,256,256]{2,1,0:T(8,128)S(1)} %slice_bitcast_fusion.3, f32[2,256,256]{2,1,0:T(8,128)S(1)} %get-tuple-element.43), kind=kLoop, calls=%fused_computation.40 | loop fusion | flops 8388608 | bytes 9437184 | tf_op jit(solution)/shard_map/convert.8
  102.1 10.0 %fusion = (f32[8,256,256]{1,2,0:T(8,128)}, f32[8,2,256,2,256,1]{4,2,5,3,1,0:T(8,128)}) fusion(bf16[1,256,2,256]{1,3,2,0:T(8,128)(2,1)S(1)} %copy-done.9, bf16[1,256,2,256]{1,3,2,0:T(8,128)(2,1)S(1)} %copy-done.10, bf16[8,2,1,256,256]{4,3,2,1,0:T(8,128)(2,1)} %get-tuple-element.38, bf16[8,2,1,256,256]{4,3,2,1,0:T(8,128)(2,1)} %get-tuple-element.37, ...), kind=kOutput, calls=%fused_computation.19 | convolution fusion | flops 4311220224 | bytes 15728640 | tf_op jit(solution)/shard_map/erdi,pmdil->pmerl/dot_general | solution.py:40
  112.0 4.5 %multiply_reduce_fusion = (f32[]{:T(128)}, f32[8,256,256]{1,2,0:T(8,128)}) fusion(f32[8,256,256]{1,2,0:T(8,128)S(1)} %copy-done.2, f32[8,256,256]{1,2,0:T(8,128)} %get-tuple-element.68), kind=kLoop, calls=%fused_computation.44 | loop fusion | flops 3670015 | bytes 6291460 | tf_op jit(solution)/shard_map/reduce_sum | solution.py:42
  116.6 12.0 %fusion.15 = f32[8,2,2,256,256]{3,4,1,0,2:T(8,128)} fusion(f32[8,2,256,2,256,1]{4,2,5,3,1,0:T(8,128)} %get-tuple-element.69, f32[8,256,256]{1,2,0:T(8,128)} %get-tuple-element.40, bf16[1,256,2,256]{1,3,2,0:T(8,128)(2,1)} %get-tuple-element.46, bf16[1,256,2,256]{1,3,2,0:T(8,128)(2,1)} %get-tuple-element.49, bf16[1,256,2,256]{1,3,0,2:T(8,128)(2,1)} %get-tuple-element.50, ...), kind=kOutput, calls=%fused_computation.41 | convolution fusion | flops 4302569472 | bytes 19922944 | tf_op jit(solution)/shard_map/pmdik,cjdk->pmcij/dot_general | solution.py:48
  128.6 7.2 %add_reduce_fusion = (f32[2,256,256]{1,2,0:T(8,128)}, f32[2,256,256]{1,2,0:T(8,128)}, f32[8,256,256]{1,2,0:T(8,128)S(1)}, f32[8,256,256]{1,2,0:T(8,128)S(1)}) fusion(f32[8,2,2,256,256]{3,4,1,0,2:T(8,128)} %fusion.15, f32[8,256,256]{1,2,0:T(8,128)} %copy.46, f32[8,256,256]{1,2,0:T(8,128)} %copy.45, f32[2,256,256]{1,2,0:T(8,128)S(1)} %copy-done.5, ...), kind=kLoop, calls=%fused_computation.35 | loop fusion | flops 15466496 | bytes 18874368 | tf_op jit(solution)/shard_map/reduce_sum | solution.py:57
  138.7 5.7 %dynamic_update_slice.24 = f32[2,768,384]{1,2,0:T(8,128)} dynamic-update-slice(f32[2,768,384]{1,2,0:T(8,128)} %broadcast_in_dim.2, f32[2,256,256]{1,2,0:T(8,128)S(1)} %fusion.26, s32[]{:T(128)} %constant.15.clone.1, s32[]{:T(128)S(6)} %select_n.109, s32[]{:T(128)S(6)} %select_n.110) | dynamic-update-slice | bytes 1048580 | tf_op jit(solution)/shard_map/dynamic_update_slice | solution.py:86
  145.8 6.6 %dynamic_update_slice.25 = f32[2,768,384]{1,2,0:T(8,128)} dynamic-update-slice(f32[2,768,384]{1,2,0:T(8,128)} %dynamic_update_slice.24, f32[2,256,256]{1,2,0:T(8,128)S(1)} %fusion.29, s32[]{:T(128)} %constant.15.clone.1, s32[]{:T(128)S(6)} %select_n.111, s32[]{:T(128)S(6)} %select_n.112) | dynamic-update-slice | bytes 1048580 | tf_op jit(solution)/shard_map/dynamic_update_slice | solution.py:86
  153.8 6.3 %dynamic_update_slice.26 = f32[2,768,384]{1,2,0:T(8,128)} dynamic-update-slice(f32[2,768,384]{1,2,0:T(8,128)} %dynamic_update_slice.25, f32[2,256,256]{1,2,0:T(8,128)S(1)} %fusion.32, s32[]{:T(128)} %constant.15.clone.1, s32[]{:T(128)S(6)} %select_n.113, s32[]{:T(128)S(6)} %select_n.114) | dynamic-update-slice | bytes 1048580 | tf_op jit(solution)/shard_map/dynamic_update_slice | solution.py:86
  162.5 6.3 %dynamic_update_slice.27 = f32[2,768,384]{1,2,0:T(8,128)} dynamic-update-slice(f32[2,768,384]{1,2,0:T(8,128)} %dynamic_update_slice.26, f32[2,256,256]{1,2,0:T(8,128)} %fusion.35, s32[]{:T(128)} %constant.15.clone.1, s32[]{:T(128)S(6)} %select_n.115, s32[]{:T(128)S(6)} %select_n.116) | dynamic-update-slice | bytes 1048580 | tf_op jit(solution)/shard_map/dynamic_update_slice | solution.py:86
  171.3 6.4 %dynamic_update_slice.28 = f32[2,768,384]{1,2,0:T(8,128)} dynamic-update-slice(f32[2,768,384]{1,2,0:T(8,128)} %dynamic_update_slice.27, f32[2,256,256]{1,2,0:T(8,128)S(1)} %fusion.38, s32[]{:T(128)} %constant.15.clone.1, s32[]{:T(128)S(6)} %select_n.117, s32[]{:T(128)S(6)} %select_n.118) | dynamic-update-slice | bytes 1048580 | tf_op jit(solution)/shard_map/dynamic_update_slice | solution.py:86
  179.1 6.3 %dynamic_update_slice.29 = f32[2,768,384]{1,2,0:T(8,128)} dynamic-update-slice(f32[2,768,384]{1,2,0:T(8,128)} %dynamic_update_slice.28, f32[2,256,256]{1,2,0:T(8,128)S(1)} %fusion.41, s32[]{:T(128)} %constant.15.clone.1, s32[]{:T(128)S(6)} %select_n.119, s32[]{:T(128)S(6)} %select_n.120) | dynamic-update-slice | bytes 1048580 | tf_op jit(solution)/shard_map/dynamic_update_slice | solution.py:86
  186.8 6.4 %dynamic_update_slice.30 = f32[2,768,384]{1,2,0:T(8,128)} dynamic-update-slice(f32[2,768,384]{1,2,0:T(8,128)} %dynamic_update_slice.29, f32[2,256,256]{1,2,0:T(8,128)S(1)} %fusion.24, s32[]{:T(128)} %constant.15.clone.1, s32[]{:T(128)S(6)} %select_n.121, s32[]{:T(128)S(6)} %select_n.122) | dynamic-update-slice | bytes 1048580 | tf_op jit(solution)/shard_map/dynamic_update_slice | solution.py:86
  194.6 6.3 %dynamic_update_slice.31 = f32[2,768,384]{1,2,0:T(8,128)} dynamic-update-slice(f32[2,768,384]{1,2,0:T(8,128)} %dynamic_update_slice.30, f32[2,256,256]{1,2,0:T(8,128)S(1)} %fusion.43, s32[]{:T(128)} %constant.15.clone.1, s32[]{:T(128)S(6)} %select_n.123, s32[]{:T(128)S(6)} %select_n.124) | dynamic-update-slice | bytes 1048580 | tf_op jit(solution)/shard_map/dynamic_update_slice | solution.py:86
  202.1 3.6 %collective-permute-start.1 = (f32[2,256,384]{1,2,0:T(8,128)S(1)}, f32[2,256,384]{1,2,0:T(8,128)}, u32[]{:S(2)}, u32[]{:S(2)}) collective-permute-start(f32[2,256,384]{1,2,0:T(8,128)S(1)} %slice.206), channel_id=1, source_target_pairs={{0,1},{1,2},{2,3},{3,4},{4,5},{5,6},{6,7},{7,8},{8,9},{9,10},{10,1... | collective-permute-start | bytes 2359304 | tf_op jit(solution)/shard_map/ppermute | solution.py:12
  205.7 35.7 %psum.23 = f32[]{:T(128)} all-reduce(f32[]{:T(128)} %get-tuple-element.39), channel_id=1, replica_groups=mesh['groups'=2,'row'=16] {'row'}, use_global_device_ids=true, to_apply=%region_9.10 | all-reduce | flops 1 | bytes 8 | tf_op jit(solution)/shard_map/psum | solution.py:81
  242.0 28.7 %all-reduce.3.cloned.1.call-done = (f32[2,2,256,256]{2,3,0,1:T(8,128)}, f32[256,256]{1,0:T(8,128)}) async-done(((f32[2,2,256,256]{2,3,0,1:T(8,128)}, f32[256,256]{1,0:T(8,128)}), (f32[2,2,256,256]{2,3,0,1:T(8,128)}, f32[256,256]{1,0:T(8,128)})) %all-reduce.3.cloned.1.call-update) | async-done | bytes 1310736 | tf_op jit(solution)/shard_map/psum | solution.py:91
  (84 shorter events, 59.2 us)
Async XLA Ops:
  7.2 26.6 %copy-start.8 = (f32[2,2,256,256]{3,2,1,0:T(8,128)S(1)}, f32[2,2,256,256]{3,2,1,0:T(8,128)}, u32[]{:S(2)}) copy-start(f32[2,2,256,256]{3,2,1,0:T(8,128)} %param.5) | copy-start | bytes 3145732
  7.2 263.5 %all-reduce.3.cloned.1.call-start = ((), (), s32[]{:S(2)}) async-start(), calls=%async_computation | async-start | bytes 2621440 | tf_op jit(solution)/shard_map/psum | solution.py:91
  9.4 42.7 %collective-permute-start = (f32[2,256,384]{2,1,0:T(8,128)}, f32[2,256,384]{2,1,0:T(8,128)}, u32[]{:S(2)}, u32[]{:S(2)}) collective-permute-start(f32[2,256,384]{2,1,0:T(8,128)} %slice.138), channel_id=1, source_target_pairs={{1,0},{2,1},{3,2},{4,3},{5,4},{6,5},{7,6},{8,7},{9,8},{10,9},{11,1... | collective-permute-start | bytes 2359304 | tf_op jit(solution)/shard_map/ppermute | solution.py:12
  35.9 16.2 %copy-start.3 = (f32[2,512,384]{2,1,0:T(8,128)S(1)}, f32[2,512,384]{2,1,0:T(8,128)}, u32[]{:S(2)}) copy-start(f32[2,512,384]{2,1,0:T(8,128)} %param.4) | copy-start | bytes 4718596
  87.3 3.5 %copy-start.1 = (f32[8,2,256,256]{3,2,1,0:T(8,128)S(1)}, f32[8,2,256,256]{3,2,1,0:T(8,128)}, u32[]{:S(2)}) copy-start(f32[8,2,256,256]{3,2,1,0:T(8,128)} %get-tuple-element.10) | copy-start | bytes 12582916
  100.2 1.8 copy-start.9
  100.2 1.8 copy-start.10
  100.2 1.8 copy-start.11
  102.0 10.0 %copy-start.2 = (f32[8,256,256]{1,2,0:T(8,128)S(1)}, f32[8,256,256]{1,2,0:T(8,128)}, u32[]{:S(2)}) copy-start(f32[8,256,256]{1,2,0:T(8,128)} %copy.33) | copy-start | bytes 6291460
  116.6 12.0 %copy-start.4 = (f32[2,256,256]{1,2,0:T(8,128)S(1)}, f32[2,256,256]{1,2,0:T(8,128)}, u32[]{:S(2)}) copy-start(f32[2,256,256]{1,2,0:T(8,128)} %copy.29) | copy-start | bytes 1572868
  116.6 12.0 %copy-start.5 = (f32[2,256,256]{1,2,0:T(8,128)S(1)}, f32[2,256,256]{1,2,0:T(8,128)}, u32[]{:S(2)}) copy-start(f32[2,256,256]{1,2,0:T(8,128)} %copy.37) | copy-start | bytes 1572868
  135.8 1.3 copy-start
  160.1 8.6 %copy-start.6 = (f32[2,256,256]{1,2,0:T(8,128)S(1)}, f32[2,256,256]{1,2,0:T(8,128)}, u32[]{:S(2)}) copy-start(f32[2,256,256]{1,2,0:T(8,128)} %get-tuple-element.17) | copy-start | bytes 1572868
  160.1 8.6 %copy-start.7 = (f32[2,256,256]{1,2,0:T(8,128)S(1)}, f32[2,256,256]{1,2,0:T(8,128)}, u32[]{:S(2)}) copy-start(f32[2,256,256]{1,2,0:T(8,128)} %get-tuple-element.18) | copy-start | bytes 1572868
  202.1 72.4 %collective-permute-start.1 = (f32[2,256,384]{1,2,0:T(8,128)S(1)}, f32[2,256,384]{1,2,0:T(8,128)}, u32[]{:S(2)}, u32[]{:S(2)}) collective-permute-start(f32[2,256,384]{1,2,0:T(8,128)S(1)} %slice.206), channel_id=1, source_target_pairs={{0,1},{1,2},{2,3},{3,4},{4,5},{5,6},{6,7},{7,8},{8,9},{9,10},{10,1... | collective-permute-start | bytes 2359304 | tf_op jit(solution)/shard_map/ppermute | solution.py:12
Sparse Core Ops, SparseCore 0:
  169.9 100.7 all-reduce.2
where the time goes:
time: 289 us; the launch traced here: 286 us
  local copies, waits for them, and re-layouts  106 us (37%)
  between operations  46.1 us (16%)
  other arithmetic  42.8 us (15%)
  blocking collectives  35.7 us (12%)
  waiting for transfers between devices  28.7 us (10%)
  matrix products  22 us (8%)
  starting transfers between devices  4.93 us (2%)
    dynamic_update_slice x8, local copies, waits for them, and re-layouts, per_device(): lax.dynamic_update_slice(grad_ext, current + win_grad[position], start)  50.2 us
    psum x1, blocking collectives, per_device(): loss_total = lax.psum(loss_part, 'row')  35.7 us
    gather x24, local copies, waits for them, and re-layouts  32.5 us
    psum x1, waiting for transfers between devices, per_device(): probe_sum, illum_sum = lax.psum((probe_grad, illumination), 'row')  28.7 us
    dot_general x1, matrix products, window_terms(): jnp.einsum('pmdik,cjdk->pmcij', grad_half, column, preferred_element_type...  12 us
    add x7, other arithmetic, per_device(): current + win_grad[position]  11 us
    dot_general x1, matrix products, window_terms(): jnp.einsum('erdi,pmdil->pmerl', rowwise, half, preferred_element_type=jnp...  9.99 us
    unnamed x27, local copies, waits for them, and re-layouts  7.31 us
  transfers between devices with their start and end apart: 3, of which 1 were waited for; matrix products, arithmetic and copies ran while one was open for 17% of the time, Pallas kernels for 0%

commit v1 on v0

v1 whole, which is shorter than its diff:
```python
import functools
import math

import jax
import jax.numpy as jnp
import ml_dtypes
import numpy as np
from jax import lax
from jax.experimental import pallas as pl
from jax.experimental.pallas import tpu as pltpu
from jax.sharding import PartitionSpec as P

F32, BF16 = jnp.float32, jnp.bfloat16


def dft_tables(size):
    idx = np.arange(size)
    angle = (idx[:, None] * idx[None, :] % size).astype(np.float32) * np.float32(2.0 * math.pi / size)
    scale = np.float32(1.0 / math.sqrt(size))
    return np.stack([np.cos(angle) * scale, np.sin(angle) * scale]).astype(ml_dtypes.bfloat16)


def windows_kernel(first, off_ref, *refs):
    if first:
        top_ref, bottom_ref, probe_ref, amp_ref, table_ref = refs[:5]
        refs = refs[5:]
        grad_ref, pg_ref, loss_ref = refs[:3]
    else:
        top_ref, bottom_ref, probe_ref, amp_ref, table_ref, pg_in, loss_in = refs[:7]
        refs = refs[7:]
        grad_ref, payload_ref = refs[:2]
    ext, win, wave, mid, far, fwd, adj = refs[-7:]
    if not first:
        pg_ref, loss_ref = refs[2:4]
    k = pl.program_id(0)
    n = probe_ref.shape[-1]
    half_rows = top_ref.shape[1]
    width = ext.shape[2]

    @pl.when(k == 0)
    def _():
        grad_ref[...] = jnp.zeros_like(grad_ref)
        if first:
            pg_ref[...] = jnp.zeros_like(pg_ref)
            loss_ref[...] = jnp.zeros_like(loss_ref)
        else:
            pg_ref[...] = pg_in[...]
            loss_ref[...] = loss_in[...]
        ext[:, :half_rows] = top_ref[...]
        ext[:, half_rows:] = bottom_ref[...]
        cosine, sine = table_ref[0], table_ref[1]
        minus = -sine
        fwd[:n, :n] = cosine
        fwd[:n, n:] = minus
        fwd[n:, :n] = sine
        fwd[n:, n:] = cosine
        adj[:n, :n] = cosine
        adj[:n, n:] = sine
        adj[n:, :n] = minus
        adj[n:, n:] = cosine

    r = off_ref[k, 0]
    c = off_ref[k, 1]
    fine = lax.rem(r, 8)
    base = pl.multiple_of(r - fine, 8)
    for d in range(2):
        x = pltpu.roll(ext[d, pl.ds(base, n + 8), :], lax.rem(width - c, width), 1)[:, :n]
        win[d] = pltpu.roll(x, lax.rem(n + 8 - fine, n + 8), 0)[:n]
    pg_ref[4] += win[0] * win[0] + win[1] * win[1]
    for m in range(2):
        p_re, p_im = probe_ref[m, 0], probe_ref[m, 1]
        o_re, o_im = win[0], win[1]
        wave[m * n : (m + 1) * n, :n] = (p_re * o_re - p_im * o_im).astype(BF16)
        wave[m * n : (m + 1) * n, n:] = (p_re * o_im + p_im * o_re).astype(BF16)
    half = jnp.dot(wave[...], fwd[...], preferred_element_type=F32).astype(BF16)
    for m in range(2):
        for d in range(2):
            mid[d * n : (d + 1) * n, m * n : (m + 1) * n] = half[m * n : (m + 1) * n, d * n : (d + 1) * n]
    far[...] = jnp.dot(adj[...], mid[...], preferred_element_type=F32)
    power = jnp.zeros((n, n), F32)
    for e in range(2):
        for m in range(2):
            f = far[e * n : (e + 1) * n, m * n : (m + 1) * n]
            power = power + f * f
    magnitude = jnp.sqrt(power)
    amplitude = amp_ref[0]
    miss = magnitude - amplitude
    loss_ref[...] += jnp.sum((miss * miss).reshape(n // 8, 8, n), 0)
    weight = 0.25 * (1.0 - amplitude / jnp.maximum(magnitude, 0.5))
    for e in range(2):
        for m in range(2):
            part = (slice(e * n, (e + 1) * n), slice(m * n, (m + 1) * n))
            mid[part] = (weight * far[part]).astype(BF16)
    half = jnp.dot(fwd[...], mid[...], preferred_element_type=F32).astype(BF16)
    for m in range(2):
        for d in range(2):
            wave[m * n : (m + 1) * n, d * n : (d + 1) * n] = half[d * n : (d + 1) * n, m * n : (m + 1) * n]
    far[...] = jnp.dot(wave[...], adj[...], preferred_element_type=F32)
    w_re = jnp.zeros((n, n), F32)
    w_im = jnp.zeros((n, n), F32)
    for m in range(2):
        g_re, g_im = far[m * n : (m + 1) * n, :n], far[m * n : (m + 1) * n, n:]
        p_re, p_im = probe_ref[m, 0], probe_ref[m, 1]
        o_re, o_im = win[0], win[1]
        w_re = w_re + p_re * g_re + p_im * g_im
        w_im = w_im + p_re * g_im - p_im * g_re
        pg_ref[2 * m] += o_re * g_re + o_im * g_im
        pg_ref[2 * m + 1] += o_re * g_im - o_im * g_re
    for d, v in ((0, w_re), (1, w_im)):
        v = pltpu.roll(jnp.concatenate([v, jnp.zeros((8, n), F32)], 0), fine, 0)
        v = jnp.concatenate([v, jnp.zeros((n + 8, width - n), F32)], 1)
        grad_ref[d, pl.ds(base, n + 8), :] += pltpu.roll(v, c, 1)

    if not first:

        @pl.when(k == pl.num_programs(0) - 1)
        def _():
            shards = payload_ref.shape[0]
            rows = n // shards
            for s in range(shards):
                for q in range(5):
                    payload_ref[s, q * rows : (q + 1) * rows] = pg_ref[q, s * rows : (s + 1) * rows]
                payload_ref[s, 5 * rows :] = loss_ref[...]


def windows(first, shards, offs, top, bottom, top_block, bottom_block, probe, amplitude, amp_first, table, carried=()):
    count = offs.shape[0]
    n = probe.shape[-1]
    rows, width = n, top.shape[2]

    def whole(*shape):
        return pl.BlockSpec(shape, lambda k, o: (0,) * len(shape))

    in_specs = [
        pl.BlockSpec((2, rows, width), lambda k, o: (0, top_block, 0)),
        pl.BlockSpec((2, rows, width), lambda k, o: (0, bottom_block, 0)),
        whole(*probe.shape),
        pl.BlockSpec((1, n, n), lambda k, o: (amp_first + k, 0, 0)),
        whole(*table.shape),
    ]
    out_specs = [whole(2, 2 * rows, width)]
    out_shape = [jax.ShapeDtypeStruct((2, 2 * rows, width), F32)]
    scratch = []
    if first:
        out_specs += [whole(5, n, n), whole(8, n)]
        out_shape += [jax.ShapeDtypeStruct((5, n, n), F32), jax.ShapeDtypeStruct((8, n), F32)]
    else:
        in_specs += [whole(5, n, n), whole(8, n)]
        shape = (shards, 5 * (n // shards) + 8, n)
        out_specs += [whole(*shape)]
        out_shape += [jax.ShapeDtypeStruct(shape, F32)]
        scratch += [pltpu.VMEM((5, n, n), F32), pltpu.VMEM((8, n), F32)]
    scratch += [
        pltpu.VMEM((2, 2 * rows, width), F32),
        pltpu.VMEM((2, n, n), F32),
        pltpu.VMEM((2 * n, 2 * n), BF16),
        pltpu.VMEM((2 * n, 2 * n), BF16),
        pltpu.VMEM((2 * n, 2 * n), F32),
        pltpu.VMEM((2 * n, 2 * n), BF16),
        pltpu.VMEM((2 * n, 2 * n), BF16),
    ]
    return pl.pallas_call(
        functools.partial(windows_kernel, first),
        grid_spec=pltpu.PrefetchScalarGridSpec(
            num_scalar_prefetch=1,
            grid=(count,),
            in_specs=in_specs,
            out_specs=out_specs,
            scratch_shapes=scratch,
        ),
        out_shape=out_shape,
        compiler_params=pltpu.CompilerParams(vmem_limit_bytes=52 << 20),
        name="near" if first else "across",
    )(offs, top, bottom, probe, amplitude, table, *carried)


def swap(x, bit):
    size = lax.axis_size("row")
    return lax.ppermute(x, "row", [(i, i ^ bit) for i in range(size)])


def per_device(object_field, probe, amplitude, offsets):
    tile = object_field.shape[1]
    n = probe.shape[2]
    count = offsets.shape[0]
    near = count // 2
    size = lax.axis_size("row")
    me = lax.axis_index("row")
    table = jnp.asarray(dft_tables(n))
    below = lax.ppermute(object_field[:, :n], "row", [(i, i - 1) for i in range(1, size)])
    offs = offsets - jnp.stack([me * tile, 0])
    grad_a, pg, loss = windows(
        True, size, offs[:near], object_field, object_field, 0, 1, probe, amplitude, 0, table
    )
    grad_b, x = windows(
        False,
        size,
        offs[near:] - jnp.array([n, 0], jnp.int32),
        object_field,
        below,
        1,
        0,
        probe,
        amplitude,
        near,
        table,
        (pg, loss),
    )
    carried = lax.ppermute(grad_b[:, n:], "row", [(i, i + 1) for i in range(size - 1)])
    bits = [1 << b for b in range(size.bit_length() - 1)]
    order = bits[:2] + bits[2:][::-1]
    for bit in order:
        half = x.shape[0] // 2
        mine = (me // bit) % 2
        keep = jnp.where(mine == 0, x[:half], x[half:])
        send = jnp.where(mine == 0, x[half:], x[:half])
        x = keep + swap(send, bit)
    rows = n // size
    x = x[0]
    loss = jnp.sum(x[5 * rows :]) / (count * size * n * n)
    y = x[: 4 * rows].reshape(4, rows, n) / jnp.sqrt(x[4 * rows : 5 * rows] + 1.0)
    y = y[None]
    for bit in order[::-1]:
        other = swap(y, bit)
        mine = (me // bit) % 2
        y = jnp.where(mine == 0, jnp.concatenate([y, other]), jnp.concatenate([other, y]))
    probe_dir = jnp.transpose(y, (1, 0, 2, 3)).reshape(2, 2, n, n)
    object_grad = jnp.concatenate([grad_a[:, :n] + carried, grad_a[:, n:] + grad_b[:, :n]], 1)
    return (object_grad, probe_dir, loss.reshape(1))


def solution(mesh):
    placed = (
        P(None, ("groups", "row"), None),
        P(),
        P(("groups", "row"), None, None),
        P(("groups", "row"), None),
    )
    return jax.shard_map(
        per_device,
        mesh=mesh,
        in_specs=placed,
        out_specs=(P(None, ("groups", "row"), None), P("groups", None, None, None), P("groups")),
        check_vma=False,
    )
```

time: 289 us -> 95.1 us (0.33)
  local copies, waits for them, and re-layouts: 106 us -> 2.5 us
  between operations: 46.1 us -> 2.61 us
  other arithmetic: 42.8 us -> 4.21 us
  blocking collectives: 35.7 us -> 0 us
  Pallas kernels: 0 us -> 28.9 us
  matrix products: 22 us -> 0 us
  waiting for transfers between devices: 28.7 us -> 39.8 us
  starting transfers between devices: 4.93 us -> 15.6 us
    dynamic_update_slice x8 -> x0, local copies, waits for them, and re-layouts: 50.2 us -> none  [per_device(): lax.dynamic_update_slice(grad_ext, current + win_grad[position], start)]
    ppermute x2 -> x10, waiting for transfers between devices: 0.01 us -> 39.8 us  [the longest x8 39.8 us: swap(): return lax.ppermute(x, 'row', [(i, i ^ bit) for i in range(size)])]
    psum x1 -> x0, blocking collectives: 35.7 us -> none  [per_device(): loss_total = lax.psum(loss_part, 'row')]
    gather x24 -> x0, local copies, waits for them, and re-layouts: 32.5 us -> none
    pallas_call x0 -> x2, Pallas kernels: none -> 28.9 us  [windows(): pl.pallas_call(functools.partial(windows_kernel, first), grid_spec=pltpu....]
    psum x1 -> x0, waiting for transfers between devices: 28.7 us -> none  [per_device(): probe_sum, illum_sum = lax.psum((probe_grad, illumination), 'row')]
    dot_general x2 -> x0, matrix products: 22 us -> none  [the longest x1 12 us: window_terms(): jnp.einsum('pmdik,cjdk->pmcij', grad_half, column, preferred_element_type...]
    reduce_sum x3 -> x1, other arithmetic: 15.1 us -> 0.6 us  [per_device(): loss = jnp.sum(x[5 * rows:]) / (count * size * n * n)]
  transfers between devices with their start and end apart: 3 -> 10, of which waited for: 1 -> 7; matrix products, arithmetic and copies ran while one was open for 17% -> 2% of each run, Pallas kernels for 0% -> 15%
where the time goes in v1:
time: 95.1 us; the launch traced here: 93.7 us
  waiting for transfers between devices  39.8 us (42%)
  Pallas kernels  28.9 us (30%)
  starting transfers between devices  15.6 us (16%)
  other arithmetic  4.21 us (4%)
  between operations  2.61 us (3%)
  local copies, waits for them, and re-layouts  2.5 us (3%)
    ppermute x8, waiting for transfers between devices, swap(): return lax.ppermute(x, 'row', [(i, i ^ bit) for i in range(size)])  39.8 us
    pallas_call x2, Pallas kernels, windows(): pl.pallas_call(functools.partial(windows_kernel, first), grid_spec=pltpu....  28.9 us
    ppermute x8, starting transfers between devices, swap(): return lax.ppermute(x, 'row', [(i, i ^ bit) for i in range(size)])  12.9 us
  transfers between devices with their start and end apart: 10, of which 7 were waited for; matrix products, arithmetic and copies ran while one was open for 2% of the time, Pallas kernels for 15%

profile of v1, /device:TPU:0, one launch (start us, length us, event | category | flops | bytes accessed | tf_op | source)
XLA Modules:
  0.0 93.7 jit_solution(1290212950644338885)
XLA Ops:
  0.7 1.3 %slice.68 = f32[2,256,384]{2,1,0:T(8,128)S(1)} slice(f32[2,512,384]{2,1,0:T(8,128)} %refs_0_.3), slice={[0:2], [0:256], [0:384]} | slice | bytes 1572864 | tf_op jit(solution)/shard_map/slice | solution.py:190
  2.0 1.3 %collective-permute-start = (f32[2,256,384]{2,1,0:T(8,128)S(1)}, f32[2,256,384]{2,1,0:T(8,128)S(1)}, u32[]{:S(2)}, u32[]{:S(2)}) collective-permute-start(f32[2,256,384]{2,1,0:T(8,128)S(1)} %slice.68), channel_id=1, source_target_pairs={{1,0},{2,1},{3,2},{4,3},{5,4},{6,5},{7,6},{8,7},{9,8},{10,9},{11,1... | collective-permute-start | bytes 2359304 | tf_op jit(solution)/shard_map/ppermute | solution.py:190
  3.5 14.0 %near.1 = (f32[2,512,384]{2,1,0:T(8,128)}, f32[5,256,256]{2,1,0:T(8,128)}, f32[8,256]{1,0:T(8,128)S(1)}) custom-call(s32[4,2]{1,0:T(4,128)S(1)} %get-tuple-element.15.off_ref, f32[2,512,384]{2,1,0:T(8,128)} %refs_0_.3, f32[2,512,384]{2,1,0:T(8,128)} %refs_0_.3, f32[2,2,256,256]{3,2,1,0:T(8,128)S(1)} %copy-done, f32[8,256,256]{2,1,0:T(8,128)} %refs_3_.3, ...), custom_call_target="tpu_custom_call" | custom-call | tf_op jit(solution)/shard_map/near/pallas_call | solution.py:162
  17.5 14.9 %across.1 = (f32[2,512,384]{2,1,0:T(8,128)}, f32[16,88,256]{2,1,0:T(8,128)}) custom-call(s32[4,2]{1,0:T(4,128)S(1)} %get-tuple-element.16.off_ref, f32[2,512,384]{2,1,0:T(8,128)} %refs_0_.3, f32[2,256,384]{2,1,0:T(8,128)S(1)} %collective-permute-done.refs_1_, f32[2,2,256,256]{3,2,1,0:T(8,128)} %refs_2_.3, f32[8,256,256]{2,1,0:T(8,128)} %refs_3_.3, ...), custom_call_target="tpu_custom_call" | custom-call | tf_op jit(solution)/shard_map/across/pallas_call | solution.py:162
  32.4 1.5 %slice_select_fusion = f32[8,88,256]{2,1,0:T(8,128)S(1)} fusion(f32[16,88,256]{2,1,0:T(8,128)} %get-tuple-element.12, pred[]{:T(512)S(6)} %eq.29), kind=kLoop, calls=%fused_computation.6 | loop fusion | flops 180224 | bytes 2162689 | tf_op jit(solution)/shard_map/jit(_where)/select_n | solution.py:216
  34.0 1.2 %collective-permute-start.2 = (f32[8,88,256]{2,1,0:T(8,128)S(1)}, f32[8,88,256]{2,1,0:T(8,128)S(1)}, u32[]{:S(2)}, u32[]{:S(2)}) collective-permute-start(f32[8,88,256]{2,1,0:T(8,128)S(1)} %slice_select_fusion), channel_id=1, source_target_pairs={{0,1},{1,0},{2,3},{3,2},{4,5},{5,4},{6,7},{7,6},{8,9},{9,8},{10,11... | collective-permute-start | bytes 2162696 | tf_op jit(solution)/shard_map/ppermute | solution.py:179
  35.2 1.8 %collective-permute-done.2 = f32[8,88,256]{2,1,0:T(8,128)S(1)} collective-permute-done((f32[8,88,256]{2,1,0:T(8,128)S(1)}, f32[8,88,256]{2,1,0:T(8,128)S(1)}, u32[]{:S(2)}, u32[]{:S(2)}) %collective-permute-start.2) | collective-permute-done | bytes 720928 | tf_op jit(solution)/shard_map/ppermute | solution.py:179
  37.2 3.1 %collective-permute-start.3 = (f32[4,88,256]{2,1,0:T(8,128)S(1)}, f32[4,88,256]{2,1,0:T(8,128)S(1)}, u32[]{:S(2)}, u32[]{:S(2)}) collective-permute-start(f32[4,88,256]{2,1,0:T(8,128)S(1)} %slice_select_fusion.1), channel_id=1, source_target_pairs={{0,2},{1,3},{2,0},{3,1},{4,6},{5,7},{6,4},{7,5},{8,10},{9,11},{10,... | collective-permute-start | bytes 1081352 | tf_op jit(solution)/shard_map/ppermute | solution.py:179
  40.3 8.9 %collective-permute-done.3 = f32[4,88,256]{2,1,0:T(8,128)S(1)} collective-permute-done((f32[4,88,256]{2,1,0:T(8,128)S(1)}, f32[4,88,256]{2,1,0:T(8,128)S(1)}, u32[]{:S(2)}, u32[]{:S(2)}) %collective-permute-start.3) | collective-permute-done | bytes 360480 | tf_op jit(solution)/shard_map/ppermute | solution.py:179
  49.3 3.4 %collective-permute-start.4 = (f32[2,88,256]{2,1,0:T(8,128)S(1)}, f32[2,88,256]{2,1,0:T(8,128)S(1)}, u32[]{:S(2)}, u32[]{:S(2)}) collective-permute-start(f32[2,88,256]{2,1,0:T(8,128)S(1)} %slice_select_fusion.2), channel_id=1, source_target_pairs={{0,8},{1,9},{2,10},{3,11},{4,12},{5,13},{6,14},{7,15},{8,0},{9,1},... | collective-permute-start | bytes 540680 | tf_op jit(solution)/shard_map/ppermute | solution.py:179
  52.7 7.9 %collective-permute-done.4 = f32[2,88,256]{2,1,0:T(8,128)S(1)} collective-permute-done((f32[2,88,256]{2,1,0:T(8,128)S(1)}, f32[2,88,256]{2,1,0:T(8,128)S(1)}, u32[]{:S(2)}, u32[]{:S(2)}) %collective-permute-start.4) | collective-permute-done | bytes 180256 | tf_op jit(solution)/shard_map/ppermute | solution.py:179
  60.6 0.8 collective-permute-start.5
  61.4 3.8 %collective-permute-done.5 = f32[1,88,256]{2,1,0:T(8,128)S(1)} collective-permute-done((f32[1,88,256]{2,1,0:T(8,128)S(1)}, f32[1,88,256]{2,1,0:T(8,128)S(1)}, u32[]{:S(2)}, u32[]{:S(2)}) %collective-permute-start.5) | collective-permute-done | bytes 90144 | tf_op jit(solution)/shard_map/ppermute | solution.py:179
  65.3 0.8 collective-permute-start.6
  66.1 1.5 %collective-permute-start.1 = (f32[2,256,384]{2,1,0:T(8,128)S(1)}, f32[2,256,384]{2,1,0:T(8,128)S(1)}, u32[]{:S(2)}, u32[]{:S(2)}) collective-permute-start(f32[2,256,384]{2,1,0:T(8,128)S(1)} %slice.69), channel_id=1, source_target_pairs={{0,1},{1,2},{2,3},{3,4},{4,5},{5,6},{6,7},{7,8},{8,9},{9,10},{10,1... | collective-permute-start | bytes 2359304 | tf_op jit(solution)/shard_map/ppermute | solution.py:209
  67.6 2.0 %collective-permute-done.6 = f32[1,4,16,256]{3,2,1,0:T(8,128)S(1)} collective-permute-done((f32[1,4,16,256]{3,2,1,0:T(8,128)S(1)}, f32[1,4,16,256]{3,2,1,0:T(8,128)S(1)}, u32[]{:S(2)}, u32[]{:S(2)}) %collective-permute-start.6) | collective-permute-done | bytes 65568 | tf_op jit(solution)/shard_map/ppermute | solution.py:179
  69.6 2.4 %collective-permute-start.7 = (f32[2,4,16,256]{3,2,1,0:T(8,128)S(1)}, f32[2,4,16,256]{3,2,1,0:T(8,128)S(1)}, u32[]{:S(2)}, u32[]{:S(2)}) collective-permute-start(f32[2,4,16,256]{3,2,1,0:T(8,128)S(1)} %maximum_select_fusion.3), channel_id=1, source_target_pairs={{0,8},{1,9},{2,10},{3,11},{4,12},{5,13},{6,14},{7,15},{8,0},{9,1},... | collective-permute-start | bytes 393224 | tf_op jit(solution)/shard_map/ppermute | solution.py:179
  72.1 7.5 %collective-permute-done.7 = f32[2,4,16,256]{3,2,1,0:T(8,128)S(1)} collective-permute-done((f32[2,4,16,256]{3,2,1,0:T(8,128)S(1)}, f32[2,4,16,256]{3,2,1,0:T(8,128)S(1)}, u32[]{:S(2)}, u32[]{:S(2)}) %collective-permute-start.7) | collective-permute-done | bytes 131104 | tf_op jit(solution)/shard_map/ppermute | solution.py:179
  79.6 0.8 collective-permute-start.8
  80.4 7.9 %collective-permute-done.8 = f32[4,4,16,256]{3,2,1,0:T(8,128)S(1)} collective-permute-done((f32[4,4,16,256]{3,2,1,0:T(8,128)S(1)}, f32[4,4,16,256]{3,2,1,0:T(8,128)S(1)}, u32[]{:S(2)}, u32[]{:S(2)}) %collective-permute-start.8) | collective-permute-done | bytes 262176 | tf_op jit(solution)/shard_map/ppermute | solution.py:179
  88.3 0.4 collective-permute-start.9
  88.9 1.2 %pad_maximum_fusion = f32[2,512,384]{2,1,0:T(8,128)} fusion(f32[2,256,384]{2,1,0:T(8,128)S(1)} %get-tuple-element.14, f32[2,256,384]{2,1,0:T(8,128)S(1)} %get-tuple-element.13), kind=kLoop, calls=%fused_computation | loop fusion | flops 393216 | bytes 3145728 | tf_op jit(solution)/shard_map/concatenate | solution.py:228
  90.2 0.6 slice_reduce_fusion
  91.6 1.0 %copy.10 = f32[4,16,16,256]{3,2,1,0:T(8,128)} copy(f32[4,16,16,256]{3,2,0,1:T(8,128)S(1)} %fusion) | data formatting | bytes 2097152 | tf_op jit(solution)/shard_map/transpose | solution.py:227
  (37 shorter events, 1.0 us)
Async XLA Ops:
  0.6 2.8 %copy-start.6 = (s32[2]{0:T(128)S(1)}, s32[2]{0:T(128)}, u32[]{:S(2)}) copy-start(s32[2]{0:T(128)} %constant.105) | copy-start | bytes 28
  0.6 2.8 %copy-start.1 = (bf16[2,256,256]{2,1,0:T(8,128)(2,1)S(1)}, bf16[2,256,256]{2,1,0:T(8,128)(2,1)}, u32[]{:S(2)}) copy-start(bf16[2,256,256]{2,1,0:T(8,128)(2,1)} %constant.101.clone.refs_4_) | copy-start | bytes 786436
  0.7 2.6 %copy-start.5 = (s32[8,2]{0,1:T(2,128)S(1)}, s32[8,2]{0,1:T(2,128)}, u32[]{:S(2)}) copy-start(s32[8,2]{0,1:T(2,128)} %param.9) | copy-start | bytes 196
  0.7 2.8 %copy-start = (f32[2,2,256,256]{3,2,1,0:T(8,128)S(1)}, f32[2,2,256,256]{3,2,1,0:T(8,128)}, u32[]{:S(2)}) copy-start(f32[2,2,256,256]{3,2,1,0:T(8,128)} %refs_2_.3) | copy-start | bytes 3145732
  2.0 15.5 %collective-permute-start = (f32[2,256,384]{2,1,0:T(8,128)S(1)}, f32[2,256,384]{2,1,0:T(8,128)S(1)}, u32[]{:S(2)}, u32[]{:S(2)}) collective-permute-start(f32[2,256,384]{2,1,0:T(8,128)S(1)} %slice.68), channel_id=1, source_target_pairs={{1,0},{2,1},{3,2},{4,3},{5,4},{6,5},{7,6},{8,7},{9,8},{10,9},{11,1... | collective-permute-start | bytes 2359304 | tf_op jit(solution)/shard_map/ppermute | solution.py:190
  32.4 4.5 %copy-start.2 = (f32[16,88,256]{2,1,0:T(8,128)S(1)}, f32[16,88,256]{2,1,0:T(8,128)}, u32[]{:S(2)}) copy-start(f32[16,88,256]{2,1,0:T(8,128)} %get-tuple-element.12) | copy-start | bytes 4325380
  34.0 3.0 %collective-permute-start.2 = (f32[8,88,256]{2,1,0:T(8,128)S(1)}, f32[8,88,256]{2,1,0:T(8,128)S(1)}, u32[]{:S(2)}, u32[]{:S(2)}) collective-permute-start(f32[8,88,256]{2,1,0:T(8,128)S(1)} %slice_select_fusion), channel_id=1, source_target_pairs={{0,1},{1,0},{2,3},{3,2},{4,5},{5,4},{6,7},{7,6},{8,9},{9,8},{10,11... | collective-permute-start | bytes 2162696 | tf_op jit(solution)/shard_map/ppermute | solution.py:179
  37.2 12.0 %collective-permute-start.3 = (f32[4,88,256]{2,1,0:T(8,128)S(1)}, f32[4,88,256]{2,1,0:T(8,128)S(1)}, u32[]{:S(2)}, u32[]{:S(2)}) collective-permute-start(f32[4,88,256]{2,1,0:T(8,128)S(1)} %slice_select_fusion.1), channel_id=1, source_target_pairs={{0,2},{1,3},{2,0},{3,1},{4,6},{5,7},{6,4},{7,5},{8,10},{9,11},{10,... | collective-permute-start | bytes 1081352 | tf_op jit(solution)/shard_map/ppermute | solution.py:179
  40.3 25.8 %copy-start.3 = (f32[2,512,384]{2,1,0:T(8,128)S(1)}, f32[2,512,384]{2,1,0:T(8,128)}, u32[]{:S(2)}) copy-start(f32[2,512,384]{2,1,0:T(8,128)} %get-tuple-element.11) | copy-start | bytes 4718596
  49.3 11.2 %collective-permute-start.4 = (f32[2,88,256]{2,1,0:T(8,128)S(1)}, f32[2,88,256]{2,1,0:T(8,128)S(1)}, u32[]{:S(2)}, u32[]{:S(2)}) collective-permute-start(f32[2,88,256]{2,1,0:T(8,128)S(1)} %slice_select_fusion.2), channel_id=1, source_target_pairs={{0,8},{1,9},{2,10},{3,11},{4,12},{5,13},{6,14},{7,15},{8,0},{9,1},... | collective-permute-start | bytes 540680 | tf_op jit(solution)/shard_map/ppermute | solution.py:179
  60.6 4.6 %collective-permute-start.5 = (f32[1,88,256]{2,1,0:T(8,128)S(1)}, f32[1,88,256]{2,1,0:T(8,128)S(1)}, u32[]{:S(2)}, u32[]{:S(2)}) collective-permute-start(f32[1,88,256]{2,1,0:T(8,128)S(1)} %slice_select_fusion.3), channel_id=1, source_target_pairs={{0,4},{1,5},{2,6},{3,7},{4,0},{5,1},{6,2},{7,3},{8,12},{9,13},{10,... | collective-permute-start | bytes 270344 | tf_op jit(solution)/shard_map/ppermute | solution.py:179
  65.3 4.3 %collective-permute-start.6 = (f32[1,4,16,256]{3,2,1,0:T(8,128)S(1)}, f32[1,4,16,256]{3,2,1,0:T(8,128)S(1)}, u32[]{:S(2)}, u32[]{:S(2)}) collective-permute-start(f32[1,4,16,256]{3,2,1,0:T(8,128)S(1)} %broadcast_divide_fusion), channel_id=1, source_target_pairs={{0,4},{1,5},{2,6},{3,7},{4,0},{5,1},{6,2},{7,3},{8,12},{9,13},{10,... | collective-permute-start | bytes 196616 | tf_op jit(solution)/shard_map/ppermute | solution.py:179
  66.1 22.7 %copy-start.4 = (f32[2,512,384]{2,1,0:T(8,128)S(1)}, f32[2,512,384]{2,1,0:T(8,128)}, u32[]{:S(2)}) copy-start(f32[2,512,384]{2,1,0:T(8,128)} %get-tuple-element.8) | copy-start | bytes 4718596
  66.1 22.6 %collective-permute-start.1 = (f32[2,256,384]{2,1,0:T(8,128)S(1)}, f32[2,256,384]{2,1,0:T(8,128)S(1)}, u32[]{:S(2)}, u32[]{:S(2)}) collective-permute-start(f32[2,256,384]{2,1,0:T(8,128)S(1)} %slice.69), channel_id=1, source_target_pairs={{0,1},{1,2},{2,3},{3,4},{4,5},{5,6},{6,7},{7,8},{8,9},{9,10},{10,1... | collective-permute-start | bytes 2359304 | tf_op jit(solution)/shard_map/ppermute | solution.py:209
  69.6 9.9 %collective-permute-start.7 = (f32[2,4,16,256]{3,2,1,0:T(8,128)S(1)}, f32[2,4,16,256]{3,2,1,0:T(8,128)S(1)}, u32[]{:S(2)}, u32[]{:S(2)}) collective-permute-start(f32[2,4,16,256]{3,2,1,0:T(8,128)S(1)} %maximum_select_fusion.3), channel_id=1, source_target_pairs={{0,8},{1,9},{2,10},{3,11},{4,12},{5,13},{6,14},{7,15},{8,0},{9,1},... | collective-permute-start | bytes 393224 | tf_op jit(solution)/shard_map/ppermute | solution.py:179
  79.6 8.7 %collective-permute-start.8 = (f32[4,4,16,256]{3,2,1,0:T(8,128)S(1)}, f32[4,4,16,256]{3,2,1,0:T(8,128)S(1)}, u32[]{:S(2)}, u32[]{:S(2)}) collective-permute-start(f32[4,4,16,256]{3,2,1,0:T(8,128)S(1)} %maximum_select_fusion.2), channel_id=1, source_target_pairs={{0,2},{1,3},{2,0},{3,1},{4,6},{5,7},{6,4},{7,5},{8,10},{9,11},{10,... | collective-permute-start | bytes 786440 | tf_op jit(solution)/shard_map/ppermute | solution.py:179
  88.3 3.1 %collective-permute-start.9 = (f32[8,4,16,256]{3,2,1,0:T(8,128)S(1)}, f32[8,4,16,256]{3,2,1,0:T(8,128)S(1)}, u32[]{:S(2)}, u32[]{:S(2)}) collective-permute-start(f32[8,4,16,256]{3,2,1,0:T(8,128)S(1)} %maximum_select_fusion.1), channel_id=1, source_target_pairs={{0,1},{1,0},{2,3},{3,2},{4,5},{5,4},{6,7},{7,6},{8,9},{9,8},{10,11... | collective-permute-start | bytes 1572872 | tf_op jit(solution)/shard_map/ppermute | solution.py:179

commit v2 on v1

--- a/solution.py
+++ b/solution.py
@@ -28,10 +28,10 @@
     else:
         top_ref, bottom_ref, probe_ref, amp_ref, table_ref, pg_in, loss_in = refs[:7]
         refs = refs[7:]
-        grad_ref, payload_ref = refs[:2]
+        grad_ref, slots = refs[0], refs[1:4]
+        pg_ref, loss_ref = refs[4:6]
     ext, win, wave, mid, far, fwd, adj = refs[-7:]
-    if not first:
-        pg_ref, loss_ref = refs[2:4]
+    shards, rows = pg_ref.shape[1:3]
     k = pl.program_id(0)
     n = probe_ref.shape[-1]
     half_rows = top_ref.shape[1]
@@ -66,7 +66,7 @@
     for d in range(2):
         x = pltpu.roll(ext[d, pl.ds(base, n + 8), :], lax.rem(width - c, width), 1)[:, :n]
         win[d] = pltpu.roll(x, lax.rem(n + 8 - fine, n + 8), 0)[:n]
-    pg_ref[4] += win[0] * win[0] + win[1] * win[1]
+    pg_ref[4] += (win[0] * win[0] + win[1] * win[1]).reshape(shards, rows, n)
     for m in range(2):
         p_re, p_im = probe_ref[m, 0], probe_ref[m, 1]
         o_re, o_im = win[0], win[1]
@@ -104,8 +104,8 @@
         o_re, o_im = win[0], win[1]
         w_re = w_re + p_re * g_re + p_im * g_im
         w_im = w_im + p_re * g_im - p_im * g_re
-        pg_ref[2 * m] += o_re * g_re + o_im * g_im
-        pg_ref[2 * m + 1] += o_re * g_im - o_im * g_re
+        pg_ref[2 * m] += (o_re * g_re + o_im * g_im).reshape(shards, rows, n)
+        pg_ref[2 * m + 1] += (o_re * g_im - o_im * g_re).reshape(shards, rows, n)
     for d, v in ((0, w_re), (1, w_im)):
         v = pltpu.roll(jnp.concatenate([v, jnp.zeros((8, n), F32)], 0), fine, 0)
         v = jnp.concatenate([v, jnp.zeros((n + 8, width - n), F32)], 1)
@@ -115,18 +115,38 @@
 
         @pl.when(k == pl.num_programs(0) - 1)
         def _():
-            shards = payload_ref.shape[0]
-            rows = n // shards
-            for s in range(shards):
+            me = off_ref[off_ref.shape[0] - 1, 0]
+            loss = loss_ref[:, : n // 2] + loss_ref[:, n // 2 :]
+            for d in range(shards):
+                part = slot_of(d, shards)
+                size = shards // 2
+                ref, part = (slots[0], part - size) if part >= size else (slots[2 - part // (size // 2)], part % (size // 2))
+                owner = me ^ d
                 for q in range(5):
-                    payload_ref[s, q * rows : (q + 1) * rows] = pg_ref[q, s * rows : (s + 1) * rows]
-                payload_ref[s, 5 * rows :] = loss_ref[...]
-
-
-def windows(first, shards, offs, top, bottom, top_block, bottom_block, probe, amplitude, amp_first, table, carried=()):
-    count = offs.shape[0]
+                    value = pg_ref[q, owner]
+                    ref[part, 2 * q * rows : (2 * q + 1) * rows] = value[:, : n // 2]
+                    ref[part, (2 * q + 1) * rows : (2 * q + 2) * rows] = value[:, n // 2 :]
+                ref[part, 10 * rows :] = loss
+
+
+def slot_of(d, shards):
+    return (d & 1) * (shards // 2) + (d >> 1 & 1) * (shards // 4) + (d >> 2)
+
+
+def assemble_kernel(me_ref, own_ref, other_ref, out_ref):
+    half, planes, rows, n = own_ref.shape
+    shards = 2 * half
+    for d in range(shards):
+        part = slot_of(d, shards)
+        ref, part = (other_ref, part - half) if part >= half else (own_ref, part)
+        for q in range(planes):
+            out_ref[q, me_ref[0] ^ d] = ref[part, q]
+
+
+def windows(first, shards, count, offs, top, bottom, top_block, bottom_block, probe, amplitude, amp_first, table, carried=()):
     n = probe.shape[-1]
     rows, width = n, top.shape[2]
+    sums = (5, shards, n // shards, n)
 
     def whole(*shape):
         return pl.BlockSpec(shape, lambda k, o: (0,) * len(shape))
@@ -142,14 +162,15 @@
     out_shape = [jax.ShapeDtypeStruct((2, 2 * rows, width), F32)]
     scratch = []
     if first:
-        out_specs += [whole(5, n, n), whole(8, n)]
-        out_shape += [jax.ShapeDtypeStruct((5, n, n), F32), jax.ShapeDtypeStruct((8, n), F32)]
+        out_specs += [whole(*sums), whole(8, n)]
+        out_shape += [jax.ShapeDtypeStruct(sums, F32), jax.ShapeDtypeStruct((8, n), F32)]
     else:
-        in_specs += [whole(5, n, n), whole(8, n)]
-        shape = (shards, 5 * (n // shards) + 8, n)
-        out_specs += [whole(*shape)]
-        out_shape += [jax.ShapeDtypeStruct(shape, F32)]
-        scratch += [pltpu.VMEM((5, n, n), F32), pltpu.VMEM((8, n), F32)]
+        in_specs += [whole(*sums), whole(8, n)]
+        for count_of in (shards // 2, shards // 4, shards // 4):
+            shape = (count_of, 10 * (n // shards) + 8, n // 2)
+            out_specs += [whole(*shape)]
+            out_shape += [jax.ShapeDtypeStruct(shape, F32)]
+        scratch += [pltpu.VMEM(sums, F32), pltpu.VMEM((8, n), F32)]
     scratch += [
         pltpu.VMEM((2, 2 * rows, width), F32),
         pltpu.VMEM((2, n, n), F32),
@@ -174,6 +195,18 @@
     )(offs, top, bottom, probe, amplitude, table, *carried)
 
 
+def assemble(me, own, other):
+    half, planes, rows, n = own.shape
+    whole = pl.BlockSpec(memory_space=pltpu.VMEM)
+    return pl.pallas_call(
+        assemble_kernel,
+        in_specs=[pl.BlockSpec(memory_space=pltpu.SMEM), whole, whole],
+        out_specs=whole,
+        out_shape=jax.ShapeDtypeStruct((planes, 2 * half, rows, n), F32),
+        name="assemble",
+    )(me.reshape(1), own, other)
+
+
 def swap(x, bit):
     size = lax.axis_size("row")
     return lax.ppermute(x, "row", [(i, i ^ bit) for i in range(size)])
@@ -190,12 +223,13 @@
     below = lax.ppermute(object_field[:, :n], "row", [(i, i - 1) for i in range(1, size)])
     offs = offsets - jnp.stack([me * tile, 0])
     grad_a, pg, loss = windows(
-        True, size, offs[:near], object_field, object_field, 0, 1, probe, amplitude, 0, table
-    )
-    grad_b, x = windows(
+        True, size, near, offs[:near], object_field, object_field, 0, 1, probe, amplitude, 0, table
+    )
+    grad_b, away, beside, x = windows(
         False,
         size,
-        offs[near:] - jnp.array([n, 0], jnp.int32),
+        count - near,
+        jnp.concatenate([offs[near:] - jnp.array([n, 0], jnp.int32), jnp.stack([me, 0])[None]]),
         object_field,
         below,
         1,
@@ -207,24 +241,22 @@
         (pg, loss),
     )
     carried = lax.ppermute(grad_b[:, n:], "row", [(i, i + 1) for i in range(size - 1)])
-    bits = [1 << b for b in range(size.bit_length() - 1)]
-    order = bits[:2] + bits[2:][::-1]
-    for bit in order:
-        half = x.shape[0] // 2
-        mine = (me // bit) % 2
-        keep = jnp.where(mine == 0, x[:half], x[half:])
-        send = jnp.where(mine == 0, x[half:], x[:half])
-        x = keep + swap(send, bit)
+    quarter = size // 4
+    away = swap(away, 1)
+    beside = swap(beside + away[quarter:], 2)
+    x = x + away[:quarter] + beside
+    parts = [x[0]] + [swap(x[z], 4 * z) for z in range(1, quarter)]
+    while len(parts) > 1:
+        parts = [a + b for a, b in zip(parts[::2], parts[1::2])]
+    total = parts[0]
     rows = n // size
-    x = x[0]
-    loss = jnp.sum(x[5 * rows :]) / (count * size * n * n)
-    y = x[: 4 * rows].reshape(4, rows, n) / jnp.sqrt(x[4 * rows : 5 * rows] + 1.0)
-    y = y[None]
-    for bit in order[::-1]:
-        other = swap(y, bit)
-        mine = (me // bit) % 2
-        y = jnp.where(mine == 0, jnp.concatenate([y, other]), jnp.concatenate([other, y]))
-    probe_dir = jnp.transpose(y, (1, 0, 2, 3)).reshape(2, 2, n, n)
+    loss = jnp.sum(total[10 * rows :]) / (count * size * n * n)
+    planes = total[: 10 * rows].reshape(5, 2, rows, n // 2)
+    y = planes[:4] / jnp.sqrt(planes[4] + 1.0)
+    y = jnp.concatenate([y[:, 0], y[:, 1]], -1)
+    y = jnp.stack([y] + [swap(y, 4 * z) for z in range(1, quarter)])
+    y = jnp.concatenate([y, swap(y, 2)])
+    probe_dir = assemble(me, y, swap(y, 1)).reshape(2, 2, n, n)
     object_grad = jnp.concatenate([grad_a[:, :n] + carried, grad_a[:, n:] + grad_b[:, :n]], 1)
     return (object_grad, probe_dir, loss.reshape(1))
 

time: 95.1 us -> 85.2 us (0.90); the launches traced: 93.7 us -> 84.9 us
  waiting for transfers between devices: 39.8 us -> 27 us
  starting transfers between devices: 15.6 us -> 18.2 us
  Pallas kernels: 28.9 us -> 31.1 us
  other arithmetic: 4.21 us -> 2.36 us
  local copies, waits for them, and re-layouts: 2.5 us -> 3.64 us
    ppermute x8 -> x10, waiting for transfers between devices: 39.8 us -> 27 us  [swap(): return lax.ppermute(x, 'row', [(i, i ^ bit) for i in range(size)])]
    ppermute x8 -> x10, starting transfers between devices: 12.9 us -> 15.5 us  [swap(): return lax.ppermute(x, 'row', [(i, i ^ bit) for i in range(size)])]
    pallas_call x0 -> x1, Pallas kernels: none -> 2.24 us  [assemble(): pl.pallas_call(assemble_kernel, in_specs=[pl.BlockSpec(memory_space=pltpu...]
    unnamed x15 -> x22, local copies, waits for them, and re-layouts: 0.12 us -> 2.25 us
    select_n x7 -> x0, other arithmetic: 1.7 us -> none  [the longest x4 1.62 us: per_device(): send = jnp.where(mine == 0, x[half:], x[:half])]
    transpose x1 -> x0, local copies, waits for them, and re-layouts: 1.04 us -> none  [per_device(): probe_dir = jnp.transpose(y, (1, 0, 2, 3)).reshape(2, 2, n, n)]
  transfers between devices with their start and end apart: 10 -> 12, of which waited for: 7 -> 7; matrix products, arithmetic and copies ran while one was open for 2% -> 3% of each run, Pallas kernels for 15% -> 17%
where the time goes in v2:
time: 85.2 us; the launch traced here: 84.9 us
  Pallas kernels  31.1 us (37%)
  waiting for transfers between devices  27 us (32%)
  starting transfers between devices  18.2 us (21%)
  local copies, waits for them, and re-layouts  3.64 us (4%)
  between operations  2.63 us (3%)
  other arithmetic  2.36 us (3%)
    pallas_call x2, Pallas kernels, windows(): pl.pallas_call(functools.partial(windows_kernel, first), grid_spec=pltpu....  28.8 us
    ppermute x10, waiting for transfers between devices, swap(): return lax.ppermute(x, 'row', [(i, i ^ bit) for i in range(size)])  27 us
    ppermute x10, starting transfers between devices, swap(): return lax.ppermute(x, 'row', [(i, i ^ bit) for i in range(size)])  15.5 us
    unnamed x22, local copies, waits for them, and re-layouts  2.25 us
    pallas_call x1, Pallas kernels, assemble(): pl.pallas_call(assemble_kernel, in_specs=[pl.BlockSpec(memory_space=pltpu...  2.24 us
  transfers between devices with their start and end apart: 12, of which 7 were waited for; matrix products, arithmetic and copies ran while one was open for 3% of the time, Pallas kernels for 17%

profile of v2, /device:TPU:0, one launch (start us, length us, event | category | flops | bytes accessed | tf_op | source)
XLA Modules:
  0.0 84.9 jit_solution(12789572098566727420)
XLA Ops:
  0.7 1.3 %slice.64 = f32[2,256,384]{2,1,0:T(8,128)S(1)} slice(f32[2,512,384]{2,1,0:T(8,128)} %refs_0_.3), slice={[0:2], [0:256], [0:384]} | slice | bytes 1572864 | tf_op jit(solution)/shard_map/slice | solution.py:223
  2.0 1.3 %collective-permute-start = (f32[2,256,384]{2,1,0:T(8,128)S(1)}, f32[2,256,384]{2,1,0:T(8,128)S(1)}, u32[]{:S(2)}, u32[]{:S(2)}) collective-permute-start(f32[2,256,384]{2,1,0:T(8,128)S(1)} %slice.64), channel_id=1, source_target_pairs={{1,0},{2,1},{3,2},{4,3},{5,4},{6,5},{7,6},{8,7},{9,8},{10,9},{11,1... | collective-permute-start | bytes 2359304 | tf_op jit(solution)/shard_map/ppermute | solution.py:223
  3.5 14.0 %near.1 = (f32[2,512,384]{2,1,0:T(8,128)}, f32[5,16,16,256]{3,2,1,0:T(8,128)}, f32[8,256]{1,0:T(8,128)S(1)}) custom-call(s32[4,2]{1,0:T(4,128)S(1)} %get-tuple-element.26.off_ref, f32[2,512,384]{2,1,0:T(8,128)} %refs_0_.3, f32[2,512,384]{2,1,0:T(8,128)} %refs_0_.3, f32[2,2,256,256]{3,2,1,0:T(8,128)S(1)} %copy-done, f32[8,256,256]{2,1,0:T(8,128)} %refs_3_.3, ...), custom_call_target="tpu_custom_call" | custom-call | tf_op jit(solution)/shard_map/near/pallas_call | solution.py:183
  17.6 0.9 %copy-done.4 = f32[2,256,384]{2,1,0:T(8,128)} copy-done((f32[2,256,384]{2,1,0:T(8,128)}, f32[2,256,384]{2,1,0:T(8,128)S(1)}, u32[]{:S(2)}) %copy-start.4) | copy-done | bytes 786456
  18.5 14.8 %across.1 = (f32[2,512,384]{2,1,0:T(8,128)}, f32[8,168,128]{2,1,0:T(8,128)S(1)}, f32[4,168,128]{2,1,0:T(8,128)S(1)}, f32[4,168,128]{2,1,0:T(8,128)S(1)}) custom-call(s32[5,2]{1,0:T(8,128)S(1)} %pad_add_fusion.off_ref, f32[2,512,384]{2,1,0:T(8,128)} %refs_0_.3, f32[2,256,384]{2,1,0:T(8,128)} %copy-done.4, f32[2,2,256,256]{3,2,1,0:T(8,128)} %refs_2_.3, ...), custom_call_target="tpu_custom_call" | custom-call | tf_op jit(solution)/shard_map/across/pallas_call | solution.py:183
  33.3 1.1 %collective-permute-start.2 = (f32[8,168,128]{2,1,0:T(8,128)S(1)}, f32[8,168,128]{2,1,0:T(8,128)S(1)}, u32[]{:S(2)}, u32[]{:S(2)}) collective-permute-start(f32[8,168,128]{2,1,0:T(8,128)S(1)} %get-tuple-element.15), channel_id=1, source_target_pairs={{0,1},{1,0},{2,3},{3,2},{4,5},{5,4},{6,7},{7,6},{8,9},{9,8},{10,11... | collective-permute-start | bytes 2064392 | tf_op jit(solution)/shard_map/ppermute | solution.py:212
  34.4 1.8 %collective-permute-done.2 = f32[8,168,128]{2,1,0:T(8,128)S(1)} collective-permute-done((f32[8,168,128]{2,1,0:T(8,128)S(1)}, f32[8,168,128]{2,1,0:T(8,128)S(1)}, u32[]{:S(2)}, u32[]{:S(2)}) %collective-permute-start.2) | collective-permute-done | bytes 688160 | tf_op jit(solution)/shard_map/ppermute | solution.py:212
  36.2 3.1 %collective-permute-start.3 = (f32[4,168,128]{2,1,0:T(8,128)S(1)}, f32[4,168,128]{2,1,0:T(8,128)S(1)}, u32[]{:S(2)}, u32[]{:S(2)}) collective-permute-start(f32[4,168,128]{2,1,0:T(8,128)S(1)} %slice_add_fusion.2), channel_id=1, source_target_pairs={{0,2},{1,3},{2,0},{3,1},{4,6},{5,7},{6,4},{7,5},{8,10},{9,11},{10,... | collective-permute-start | bytes 1032200 | tf_op jit(solution)/shard_map/ppermute | solution.py:212
  39.2 8.6 %collective-permute-done.3 = f32[4,168,128]{2,1,0:T(8,128)S(1)} collective-permute-done((f32[4,168,128]{2,1,0:T(8,128)S(1)}, f32[4,168,128]{2,1,0:T(8,128)S(1)}, u32[]{:S(2)}, u32[]{:S(2)}) %collective-permute-start.3) | collective-permute-done | bytes 344096 | tf_op jit(solution)/shard_map/ppermute | solution.py:212
  47.9 4.4 %collective-permute-start.6 = (f32[168,128]{1,0:T(8,128)S(1)}, f32[168,128]{1,0:T(8,128)S(1)}, u32[]{:S(2)}, u32[]{:S(2)}) collective-permute-start(f32[168,128]{1,0:T(8,128)S(1)} %get-tuple-element.19), channel_id=1, source_target_pairs={{0,12},{1,13},{2,14},{3,15},{4,8},{5,9},{6,10},{7,11},{8,4},{9,5},... | collective-permute-start | bytes 258056 | tf_op jit(solution)/shard_map/ppermute | solution.py:212
  52.3 0.6 collective-permute-start.4
  53.0 1.5 %collective-permute-start.1 = (f32[2,256,384]{2,1,0:T(8,128)S(1)}, f32[2,256,384]{2,1,0:T(8,128)S(1)}, u32[]{:S(2)}, u32[]{:S(2)}) collective-permute-start(f32[2,256,384]{2,1,0:T(8,128)S(1)} %slice.65), channel_id=1, source_target_pairs={{0,1},{1,2},{2,3},{3,4},{4,5},{5,6},{6,7},{7,8},{8,9},{9,10},{10,1... | collective-permute-start | bytes 2359304 | tf_op jit(solution)/shard_map/ppermute | solution.py:243
  54.5 1.2 %collective-permute-done.6 = f32[168,128]{1,0:T(8,128)S(1)} collective-permute-done((f32[168,128]{1,0:T(8,128)S(1)}, f32[168,128]{1,0:T(8,128)S(1)}, u32[]{:S(2)}, u32[]{:S(2)}) %collective-permute-start.6) | collective-permute-done | bytes 86048 | tf_op jit(solution)/shard_map/ppermute | solution.py:212
  55.7 3.3 %collective-permute-done.5 = f32[168,128]{1,0:T(8,128)S(1)} collective-permute-done((f32[168,128]{1,0:T(8,128)S(1)}, f32[168,128]{1,0:T(8,128)S(1)}, u32[]{:S(2)}, u32[]{:S(2)}) %collective-permute-start.5) | collective-permute-done | bytes 86048 | tf_op jit(solution)/shard_map/ppermute | solution.py:212
  59.1 0.9 %collective-permute-start.8 = (f32[4,16,256]{2,1,0:T(8,128)S(1)}, f32[4,16,256]{2,1,0:T(8,128)S(1)}, u32[]{:S(2)}, u32[]{:S(2)}) collective-permute-start(f32[4,16,256]{2,1,0:T(8,128)S(1)} %get-tuple-element.23), channel_id=1, source_target_pairs={{0,8},{1,9},{2,10},{3,11},{4,12},{5,13},{6,14},{7,15},{8,0},{9,1},... | collective-permute-start | bytes 196616 | tf_op jit(solution)/shard_map/ppermute | solution.py:212
  60.0 2.4 %collective-permute-start.7 = (f32[4,16,256]{2,1,0:T(8,128)S(1)}, f32[4,16,256]{2,1,0:T(8,128)S(1)}, u32[]{:S(2)}, u32[]{:S(2)}) collective-permute-start(f32[4,16,256]{2,1,0:T(8,128)S(1)} %get-tuple-element.23), channel_id=1, source_target_pairs={{0,4},{1,5},{2,6},{3,7},{4,0},{5,1},{6,2},{7,3},{8,12},{9,13},{10,... | collective-permute-start | bytes 196616 | tf_op jit(solution)/shard_map/ppermute | solution.py:212
  62.4 1.2 %collective-permute-start.9 = (f32[4,16,256]{2,1,0:T(8,128)S(1)}, f32[4,16,256]{2,1,0:T(8,128)S(1)}, u32[]{:S(2)}, u32[]{:S(2)}) collective-permute-start(f32[4,16,256]{2,1,0:T(8,128)S(1)} %get-tuple-element.23), channel_id=1, source_target_pairs={{0,12},{1,13},{2,14},{3,15},{4,8},{5,9},{6,10},{7,11},{8,4},{9,5},... | collective-permute-start | bytes 196616 | tf_op jit(solution)/shard_map/ppermute | solution.py:212
  63.6 2.1 %collective-permute-done.8 = f32[4,16,256]{2,1,0:T(8,128)S(1)} collective-permute-done((f32[4,16,256]{2,1,0:T(8,128)S(1)}, f32[4,16,256]{2,1,0:T(8,128)S(1)}, u32[]{:S(2)}, u32[]{:S(2)}) %collective-permute-start.8) | collective-permute-done | bytes 65568 | tf_op jit(solution)/shard_map/ppermute | solution.py:212
  65.7 2.7 %collective-permute-done.9 = f32[4,16,256]{2,1,0:T(8,128)S(1)} collective-permute-done((f32[4,16,256]{2,1,0:T(8,128)S(1)}, f32[4,16,256]{2,1,0:T(8,128)S(1)}, u32[]{:S(2)}, u32[]{:S(2)}) %collective-permute-start.9) | collective-permute-done | bytes 65568 | tf_op jit(solution)/shard_map/ppermute | solution.py:212
  68.5 1.7 %collective-permute-start.10 = (f32[4,4,16,256]{3,2,1,0:T(8,128)S(1)}, f32[4,4,16,256]{3,2,1,0:T(8,128)S(1)}, u32[]{:S(2)}, u32[]{:S(2)}) collective-permute-start(f32[4,4,16,256]{3,2,1,0:T(8,128)S(1)} %pad_maximum_fusion.1), channel_id=1, source_target_pairs={{0,2},{1,3},{2,0},{3,1},{4,6},{5,7},{6,4},{7,5},{8,10},{9,11},{10,... | collective-permute-start | bytes 786440 | tf_op jit(solution)/shard_map/ppermute | solution.py:212
  70.2 7.2 %collective-permute-done.10 = f32[4,4,16,256]{3,2,1,0:T(8,128)S(1)} collective-permute-done((f32[4,4,16,256]{3,2,1,0:T(8,128)S(1)}, f32[4,4,16,256]{3,2,1,0:T(8,128)S(1)}, u32[]{:S(2)}, u32[]{:S(2)}) %collective-permute-start.10) | collective-permute-done | bytes 262176 | tf_op jit(solution)/shard_map/ppermute | solution.py:212
  78.3 1.2 %pad_maximum_fusion = f32[2,512,384]{2,1,0:T(8,128)} fusion(f32[2,256,384]{2,1,0:T(8,128)S(1)} %get-tuple-element.18, f32[2,256,384]{2,1,0:T(8,128)S(1)} %get-tuple-element.17), kind=kLoop, calls=%fused_computation | loop fusion | flops 393216 | bytes 3145728 | tf_op jit(solution)/shard_map/concatenate | solution.py:260
  80.8 0.8 copy-done.6
  81.6 2.2 %assemble.1 = f32[4,16,16,256]{3,2,1,0:T(8,128)} custom-call(s32[1]{0:T(128)} %bitcast.1.me_ref, f32[8,4,16,256]{3,2,1,0:T(8,128)} %copy-done.5, f32[8,4,16,256]{3,2,1,0:T(8,128)} %copy-done.6), custom_call_target="tpu_custom_call" | custom-call | tf_op jit(solution)/shard_map/assemble/pallas_call | solution.py:201
  (47 shorter events, 2.0 us)
Async XLA Ops:
  0.6 2.8 %copy-start.8 = (s32[2]{0:T(128)S(1)}, s32[2]{0:T(128)}, u32[]{:S(2)}) copy-start(s32[2]{0:T(128)} %constant.23) | copy-start | bytes 28
  0.6 2.8 %copy-start.1 = (bf16[2,256,256]{2,1,0:T(8,128)(2,1)S(1)}, bf16[2,256,256]{2,1,0:T(8,128)(2,1)}, u32[]{:S(2)}) copy-start(bf16[2,256,256]{2,1,0:T(8,128)(2,1)} %constant.19.clone.refs_4_) | copy-start | bytes 786436
  0.7 2.6 %copy-start.7 = (s32[8,2]{0,1:T(2,128)S(1)}, s32[8,2]{0,1:T(2,128)}, u32[]{:S(2)}) copy-start(s32[8,2]{0,1:T(2,128)} %param.9) | copy-start | bytes 196
  0.7 2.8 %copy-start = (f32[2,2,256,256]{3,2,1,0:T(8,128)S(1)}, f32[2,2,256,256]{3,2,1,0:T(8,128)}, u32[]{:S(2)}) copy-start(f32[2,2,256,256]{3,2,1,0:T(8,128)} %refs_2_.3) | copy-start | bytes 3145732
  2.0 15.6 %collective-permute-start = (f32[2,256,384]{2,1,0:T(8,128)S(1)}, f32[2,256,384]{2,1,0:T(8,128)S(1)}, u32[]{:S(2)}, u32[]{:S(2)}) collective-permute-start(f32[2,256,384]{2,1,0:T(8,128)S(1)} %slice.64), channel_id=1, source_target_pairs={{1,0},{2,1},{3,2},{4,3},{5,4},{6,5},{7,6},{8,7},{9,8},{10,9},{11,1... | collective-permute-start | bytes 2359304 | tf_op jit(solution)/shard_map/ppermute | solution.py:223
  17.6 0.9 %copy-start.4 = (f32[2,256,384]{2,1,0:T(8,128)}, f32[2,256,384]{2,1,0:T(8,128)S(1)}, u32[]{:S(2)}) copy-start(f32[2,256,384]{2,1,0:T(8,128)S(1)} %collective-permute-done.refs_1_) | copy-start | bytes 2359300
  33.3 19.7 %copy-start.2 = (f32[2,512,384]{2,1,0:T(8,128)S(1)}, f32[2,512,384]{2,1,0:T(8,128)}, u32[]{:S(2)}) copy-start(f32[2,512,384]{2,1,0:T(8,128)} %get-tuple-element.13) | copy-start | bytes 4718596
  33.3 2.9 %collective-permute-start.2 = (f32[8,168,128]{2,1,0:T(8,128)S(1)}, f32[8,168,128]{2,1,0:T(8,128)S(1)}, u32[]{:S(2)}, u32[]{:S(2)}) collective-permute-start(f32[8,168,128]{2,1,0:T(8,128)S(1)} %get-tuple-element.15), channel_id=1, source_target_pairs={{0,1},{1,0},{2,3},{3,2},{4,5},{5,4},{6,7},{7,6},{8,9},{9,8},{10,11... | collective-permute-start | bytes 2064392 | tf_op jit(solution)/shard_map/ppermute | solution.py:212
  36.2 11.6 %collective-permute-start.3 = (f32[4,168,128]{2,1,0:T(8,128)S(1)}, f32[4,168,128]{2,1,0:T(8,128)S(1)}, u32[]{:S(2)}, u32[]{:S(2)}) collective-permute-start(f32[4,168,128]{2,1,0:T(8,128)S(1)} %slice_add_fusion.2), channel_id=1, source_target_pairs={{0,2},{1,3},{2,0},{3,1},{4,6},{5,7},{6,4},{7,5},{8,10},{9,11},{10,... | collective-permute-start | bytes 1032200 | tf_op jit(solution)/shard_map/ppermute | solution.py:212
  47.9 7.8 %collective-permute-start.6 = (f32[168,128]{1,0:T(8,128)S(1)}, f32[168,128]{1,0:T(8,128)S(1)}, u32[]{:S(2)}, u32[]{:S(2)}) collective-permute-start(f32[168,128]{1,0:T(8,128)S(1)} %get-tuple-element.19), channel_id=1, source_target_pairs={{0,12},{1,13},{2,14},{3,15},{4,8},{5,9},{6,10},{7,11},{8,4},{9,5},... | collective-permute-start | bytes 258056 | tf_op jit(solution)/shard_map/ppermute | solution.py:212
  52.3 6.7 %collective-permute-start.5 = (f32[168,128]{1,0:T(8,128)S(1)}, f32[168,128]{1,0:T(8,128)S(1)}, u32[]{:S(2)}, u32[]{:S(2)}) collective-permute-start(f32[168,128]{1,0:T(8,128)S(1)} %get-tuple-element.20), channel_id=1, source_target_pairs={{0,8},{1,9},{2,10},{3,11},{4,12},{5,13},{6,14},{7,15},{8,0},{9,1},... | collective-permute-start | bytes 258056 | tf_op jit(solution)/shard_map/ppermute | solution.py:212
  52.3 6.7 %collective-permute-start.4 = (f32[168,128]{1,0:T(8,128)S(1)}, f32[168,128]{1,0:T(8,128)S(1)}, u32[]{:S(2)}, u32[]{:S(2)}) collective-permute-start(f32[168,128]{1,0:T(8,128)S(1)} %get-tuple-element.21), channel_id=1, source_target_pairs={{0,4},{1,5},{2,6},{3,7},{4,0},{5,1},{6,2},{7,3},{8,12},{9,13},{10,... | collective-permute-start | bytes 258056 | tf_op jit(solution)/shard_map/ppermute | solution.py:212
  53.0 24.7 %copy-start.3 = (f32[2,512,384]{2,1,0:T(8,128)S(1)}, f32[2,512,384]{2,1,0:T(8,128)}, u32[]{:S(2)}) copy-start(f32[2,512,384]{2,1,0:T(8,128)} %get-tuple-element.10) | copy-start | bytes 4718596
  53.0 24.6 %collective-permute-start.1 = (f32[2,256,384]{2,1,0:T(8,128)S(1)}, f32[2,256,384]{2,1,0:T(8,128)S(1)}, u32[]{:S(2)}, u32[]{:S(2)}) collective-permute-start(f32[2,256,384]{2,1,0:T(8,128)S(1)} %slice.65), channel_id=1, source_target_pairs={{0,1},{1,2},{2,3},{3,4},{4,5},{5,6},{6,7},{7,8},{8,9},{9,10},{10,1... | collective-permute-start | bytes 2359304 | tf_op jit(solution)/shard_map/ppermute | solution.py:243
  59.1 6.6 %collective-permute-start.8 = (f32[4,16,256]{2,1,0:T(8,128)S(1)}, f32[4,16,256]{2,1,0:T(8,128)S(1)}, u32[]{:S(2)}, u32[]{:S(2)}) collective-permute-start(f32[4,16,256]{2,1,0:T(8,128)S(1)} %get-tuple-element.23), channel_id=1, source_target_pairs={{0,8},{1,9},{2,10},{3,11},{4,12},{5,13},{6,14},{7,15},{8,0},{9,1},... | collective-permute-start | bytes 196616 | tf_op jit(solution)/shard_map/ppermute | solution.py:212
  60.0 5.7 %collective-permute-start.7 = (f32[4,16,256]{2,1,0:T(8,128)S(1)}, f32[4,16,256]{2,1,0:T(8,128)S(1)}, u32[]{:S(2)}, u32[]{:S(2)}) collective-permute-start(f32[4,16,256]{2,1,0:T(8,128)S(1)} %get-tuple-element.23), channel_id=1, source_target_pairs={{0,4},{1,5},{2,6},{3,7},{4,0},{5,1},{6,2},{7,3},{8,12},{9,13},{10,... | collective-permute-start | bytes 196616 | tf_op jit(solution)/shard_map/ppermute | solution.py:212
  62.4 6.1 %collective-permute-start.9 = (f32[4,16,256]{2,1,0:T(8,128)S(1)}, f32[4,16,256]{2,1,0:T(8,128)S(1)}, u32[]{:S(2)}, u32[]{:S(2)}) collective-permute-start(f32[4,16,256]{2,1,0:T(8,128)S(1)} %get-tuple-element.23), channel_id=1, source_target_pairs={{0,12},{1,13},{2,14},{3,15},{4,8},{5,9},{6,10},{7,11},{8,4},{9,5},... | collective-permute-start | bytes 196616 | tf_op jit(solution)/shard_map/ppermute | solution.py:212
  68.5 9.0 %collective-permute-start.10 = (f32[4,4,16,256]{3,2,1,0:T(8,128)S(1)}, f32[4,4,16,256]{3,2,1,0:T(8,128)S(1)}, u32[]{:S(2)}, u32[]{:S(2)}) collective-permute-start(f32[4,4,16,256]{3,2,1,0:T(8,128)S(1)} %pad_maximum_fusion.1), channel_id=1, source_target_pairs={{0,2},{1,3},{2,0},{3,1},{4,6},{5,7},{6,4},{7,5},{8,10},{9,11},{10,... | collective-permute-start | bytes 786440 | tf_op jit(solution)/shard_map/ppermute | solution.py:212
  77.4 0.8 copy-start.5
  77.5 3.3 %collective-permute-start.11 = (f32[8,4,16,256]{3,2,1,0:T(8,128)S(1)}, f32[8,4,16,256]{3,2,1,0:T(8,128)S(1)}, u32[]{:S(2)}, u32[]{:S(2)}) collective-permute-start(f32[8,4,16,256]{3,2,1,0:T(8,128)S(1)} %constant_dynamic-update-slice_fusion.own_ref), channel_id=1, source_target_pairs={{0,1},{1,0},{2,3},{3,2},{4,5},{5,4},{6,7},{7,6},{8,9},{9,8},{10,11... | collective-permute-start | bytes 1572872 | tf_op jit(solution)/shard_map/ppermute | solution.py:212
  80.8 0.8 copy-start.6

commit v3 on v0

v3 whole, which is shorter than its diff:
```python
import functools
import math

import jax
import jax.numpy as jnp
import ml_dtypes
import numpy as np
from jax import lax
from jax.experimental import pallas as pl
from jax.experimental.pallas import tpu as pltpu
from jax.sharding import PartitionSpec as P

F32, BF16 = jnp.float32, jnp.bfloat16
LANES = 128
GROUP = 2
VMEM_MIB = 30


def dft_tables(n):
    h = n // 2
    idx = np.arange(n)
    angle = (idx[:, None] * idx[None, :] % n).astype(np.float32) * np.float32(2.0 * math.pi / n)
    scale = np.float32(1.0 / math.sqrt(n))
    c, s = np.cos(angle) * scale, np.sin(angle) * scale
    near = np.arange(h)
    even, odd = 2 * near, 2 * near + 1
    turned = 2 * ((near + h // 2) % h) + 1

    def column(k):
        a, b = c[np.ix_(near, k)], s[np.ix_(near, k)]
        return np.block([[a, -b], [b, a]])

    def row(r):
        a, b = c[np.ix_(r, near)], s[np.ix_(r, near)]
        return np.block([[a, b], [-b, a]])

    tables = [column(even), column(turned), row(even), row(odd)]
    return np.stack(tables + [tables[1].T, tables[3].T]).astype(ml_dtypes.bfloat16)


def windows_kernel(first, amp_first, off_ref, *refs):
    object_ref, probe_hbm, amp_hbm, tab_hbm = refs[:4]
    if first:
        grad_out, pg_out, loss_out = refs[4:7]
    else:
        below_ref, grad_in, pg_in, loss_in, grad_out, low_out, keep_out, away_out, keep_ref, away_ref = refs[4:14]
    ext, grad, pg_ref, loss_ref, probe_ref, tab, amp_s, win_s, lhs_s, hs_s, far_s, sems = refs[-12:]
    shards, rows = pg_ref.shape[1:3]
    k = pl.program_id(0)
    n = probe_ref.shape[-1]
    h = n // 2
    width = ext.shape[2]
    below_row = 0 if first else n
    lane = lax.broadcasted_iota(jnp.int32, (1, 1, LANES), 2)
    sub = lax.broadcasted_iota(jnp.int32, (1, 8, 1), 1)

    def amplitude_copies(group):
        at = amp_first + group * GROUP
        return [
            pltpu.make_async_copy(
                amp_hbm.at[pl.ds(at, GROUP), :, pl.ds(q * LANES, LANES)], amp_s.at[group, q], sems.at[8 + 2 * group + q]
            )
            for q in range(2)
        ]

    if first:
        windows_in = [(object_ref, ext)]
        sums_in = []
    else:
        windows_in = [(object_ref.at[:, pl.ds(n, n)], ext.at[:, pl.ds(0, n)]), (below_ref, ext.at[:, pl.ds(n, n)])]
        sums_in = [(grad_in, grad.at[:, pl.ds(0, 2 * n)]), (pg_in, pg_ref), (loss_in, loss_ref)]
    windows_in = [*windows_in, (probe_hbm, probe_ref)]
    windows_in = [pltpu.make_async_copy(a, b, sems.at[i]) for i, (a, b) in enumerate(windows_in)]
    table_in = pltpu.make_async_copy(tab_hbm, tab, sems.at[3])
    sums_in = [pltpu.make_async_copy(a, b, sems.at[4 + i]) for i, (a, b) in enumerate(sums_in)]

    @pl.when(k == 0)
    def _():
        for copy in (*windows_in, table_in, *amplitude_copies(0), *amplitude_copies(1), *sums_in):
            copy.start()
        if first:
            grad[...] = jnp.zeros_like(grad)
            pg_ref[...] = jnp.zeros_like(pg_ref)
            loss_ref[...] = jnp.zeros_like(loss_ref)
        else:
            grad[:, 2 * n :] = jnp.zeros((2, n, width), F32)
        for copy in (*windows_in, table_in, *sums_in):
            copy.wait()

    for copy in amplitude_copies(k):
        copy.wait()

    def dot(a, b):
        return jnp.dot(a, b, preferred_element_type=F32)

    places = []
    for g in range(GROUP):
        r, c = off_ref[amp_first + k * GROUP + g, 0] - below_row, off_ref[amp_first + k * GROUP + g, 1]
        fine = lax.rem(r, 8)
        places.append((pl.multiple_of(r - fine, 8), fine, c))

    def load(g):
        base, fine, c = places[g]
        win = win_s.at[g]
        in_lane, in_sub = lane < LANES - c, sub < 8 - fine
        back_lane, back_sub = lax.rem(LANES - c, LANES), lax.rem(8 - fine, 8)
        for d in range(2):
            x = ext[d, pl.ds(base, n + 8), :].reshape(n // 8 + 1, 8, width)
            t = [pltpu.roll(x[:, :, LANES * q : LANES * (q + 1)], back_lane, 2) for q in range(3)]
            for q in range(2):
                y = pltpu.roll(jnp.where(in_lane, t[q], t[q + 1]), back_sub, 1)
                win[d, :, LANES * q : LANES * (q + 1)] = jnp.where(in_sub, y[:-1], y[1:]).reshape(n, LANES)

    def wave(g):
        win, lhs = win_s.at[g], lhs_s.at[g]
        for m in range(2):
            parts = []
            for j in range(2):
                js = slice(j * h, (j + 1) * h)
                p_re, p_im = probe_ref[m, 0, :, js], probe_ref[m, 1, :, js]
                o_re, o_im = win[0, :, js], win[1, :, js]
                parts.append((p_re * o_re - p_im * o_im, p_re * o_im + p_im * o_re))
            for d in range(2):
                at = (slice(m * n, (m + 1) * n), slice(d * h, (d + 1) * h))
                lhs[(0, *at)] = (parts[0][d] + parts[1][d]).astype(BF16)
                lhs[(1, *at)] = (parts[0][d] - parts[1][d]).astype(BF16)

    def columns(g):
        lhs, hs = lhs_s.at[g], hs_s.at[g]
        for p in range(2):
            v = dot(lhs[p], tab[p])
            for m in range(2):
                top, bottom = v[m * n : m * n + h], v[m * n + h : (m + 1) * n]
                for u, z in ((0, top + bottom), (1, top - bottom)):
                    for d in range(2):
                        at = (u, slice(d * h, (d + 1) * h), slice((2 * m + p) * h, (2 * m + p + 1) * h))
                        hs[at] = z[:, d * h : (d + 1) * h].astype(BF16)

    def down(g):
        hs, far = hs_s.at[g], far_s.at[g]
        for u in range(2):
            far[u] = dot(tab[2 + u], hs[u])

    idx = lax.broadcasted_iota(jnp.int32, (h, LANES), 1)
    lower = idx < LANES // 2
    pick_lo = jnp.where(lower, 2 * idx, 2 * idx - (LANES - 1))
    pick_hi = jnp.where(lower, 2 * idx + 1, 2 * idx - LANES)

    def weigh(g):
        hs, far = hs_s.at[g], far_s.at[g]
        total = jnp.zeros((8, n), F32)
        for u in range(2):
            lo = jnp.take_along_axis(amp_s[k, 0, g, pl.ds(u, h, stride=2), :], pick_lo, 1)
            hi = jnp.take_along_axis(amp_s[k, 1, g, pl.ds(u, h, stride=2), :], pick_hi, 1)
            amplitude = jnp.concatenate([jnp.where(lower, lo, hi), jnp.where(lower, hi, lo)], 1)
            power = None
            for e in range(2):
                for m in range(2):
                    f = far[u, e * h : (e + 1) * h, m * n : (m + 1) * n]
                    power = f * f if power is None else power + f * f
            magnitude = jnp.sqrt(power)
            miss = magnitude - amplitude
            total = total + jnp.sum((miss * miss).reshape(h // 8, 8, n), 0)
            weight = 0.25 * (1.0 - amplitude / jnp.maximum(magnitude, 0.5))
            for e in range(2):
                for m in range(2):
                    at = (u, slice(e * h, (e + 1) * h), slice(m * n, (m + 1) * n))
                    hs[at] = (weight * far[at]).astype(BF16)
        loss_ref[...] += total

    def up(g):
        lhs, hs = lhs_s.at[g], hs_s.at[g]
        a, b = dot(tab[0], hs[0]), dot(tab[5], hs[1])
        for j, z in ((0, a + b), (1, a - b)):
            for m in range(2):
                for p in range(2):
                    for d in range(2):
                        at = (p, slice(m * n + j * h, m * n + (j + 1) * h), slice(d * h, (d + 1) * h))
                        lhs[at] = z[d * h : (d + 1) * h, (2 * m + p) * h : (2 * m + p + 1) * h].astype(BF16)

    def columns_back(g):
        lhs, far = lhs_s.at[g], far_s.at[g]
        a, b = dot(lhs[0], tab[2]), dot(lhs[1], tab[4])
        for j, z in ((0, a + b), (1, a - b)):
            far[j] = jnp.concatenate([z[:n], z[n:]], 1)

    def sums():
        for j in range(2):
            js = slice(j * h, (j + 1) * h)
            for m in range(2):
                s_re = s_im = None
                for g in range(GROUP):
                    g_re, g_im = far_s[g, j, :, m * n : m * n + h], far_s[g, j, :, m * n + h : (m + 1) * n]
                    o_re, o_im = win_s[g, 0, :, js], win_s[g, 1, :, js]
                    a, b = o_re * g_re + o_im * g_im, o_re * g_im - o_im * g_re
                    s_re, s_im = (a, b) if s_re is None else (s_re + a, s_im + b)
                pg_ref[2 * m, :, :, js] += s_re.reshape(shards, rows, h)
                pg_ref[2 * m + 1, :, :, js] += s_im.reshape(shards, rows, h)
            s = None
            for g in range(GROUP):
                o_re, o_im = win_s[g, 0, :, js], win_s[g, 1, :, js]
                v = o_re * o_re + o_im * o_im
                s = v if s is None else s + v
            pg_ref[4, :, :, js] += s.reshape(shards, rows, h)

    def scatter(g):
        base, fine, c = places[g]
        far = far_s.at[g]
        from_sub, from_lane = sub >= fine, lane >= c
        t = [[], []]
        for j in range(2):
            js = slice(j * h, (j + 1) * h)
            w = [None, None]
            for m in range(2):
                g_re, g_im = far[j, :, m * n : m * n + h], far[j, :, m * n + h : (m + 1) * n]
                p_re, p_im = probe_ref[m, 0, :, js], probe_ref[m, 1, :, js]
                v = (p_re * g_re + p_im * g_im, p_re * g_im - p_im * g_re)
                w = [x if y is None else x + y for x, y in zip(v, w)]
            for d in range(2):
                y = pltpu.roll(w[d].reshape(n // 8, 8, LANES), fine, 1)
                z = jnp.zeros((1, 8, LANES), F32)
                y = jnp.where(from_sub, jnp.concatenate([y, z], 0), jnp.concatenate([z, y], 0))
                t[d].append(pltpu.roll(y, c, 2))
        for d in range(2):
            a, b = t[d]
            out = [jnp.where(from_lane, a, 0.0), jnp.where(from_lane, b, a), jnp.where(from_lane, 0.0, b)]
            for q in range(3):
                grad[d, pl.ds(base + below_row, n + 8), LANES * q : LANES * (q + 1)] += out[q].reshape(n + 8, LANES)

    for stage in (load, wave, columns, down, weigh, up, columns_back):
        for g in range(GROUP):
            stage(g)
    sums()
    for g in range(GROUP):
        scatter(g)

    @pl.when(k == pl.num_programs(0) - 1)
    def _():
        if first:
            out = [(grad, grad_out), (pg_ref, pg_out), (loss_ref, loss_out)]
            out = [pltpu.make_async_copy(a, b, sems.at[i]) for i, (a, b) in enumerate(out)]
            for copy in out:
                copy.start()
            for copy in out:
                copy.wait()
            return
        out = [(grad.at[:, pl.ds(2 * n, n)], low_out), (grad.at[:, pl.ds(0, 2 * n)], grad_out), (away_ref, away_out), (keep_ref, keep_out)]
        out = [pltpu.make_async_copy(a, b, sems.at[i]) for i, (a, b) in enumerate(out)]
        out[0].start()
        out[1].start()
        me = off_ref[off_ref.shape[0] - 1, 0]
        loss = loss_ref[:, : n // 2] + loss_ref[:, n // 2 :]
        for core in (1, 0):
            ref = away_ref if core else keep_ref
            for slot in range(shards // 2):
                owner = owner_of(me, core, slot, shards)
                for q in range(5):
                    value = pg_ref[q, owner]
                    ref[slot, 2 * q * rows : (2 * q + 1) * rows] = value[:, : n // 2]
                    ref[slot, (2 * q + 1) * rows : (2 * q + 2) * rows] = value[:, n // 2 :]
                ref[slot, 10 * rows :] = loss
            out[3 - core].start()
        for copy in out:
            copy.wait()


def owner_of(me, core, slot, size):
    z = lax.rem(me // 4 + slot % (size // 4), size // 4)
    return z * 4 + ((me & 3) ^ (core + 2 * (slot // (size // 4))))


def windows(first, shards, count, offs, object_field, probe, amplitude, amp_first, table, carried=()):
    n = probe.shape[-1]
    width = object_field.shape[2]
    sums = (5, shards, n // shards, n)
    hbm, anywhere = pl.BlockSpec(memory_space=pltpu.HBM), pl.BlockSpec(memory_space=pl.ANY)
    inputs = (object_field, probe, amplitude, table, *carried)
    scratch = []
    if first:
        shapes = [(2, 2 * n, width), sums, (8, n)]
    else:
        slots = (shards // 2, 10 * (n // shards) + 8, n // 2)
        shapes = [(2, 2 * n, width), (2, n, width), slots, slots]
        scratch += [pltpu.VMEM(slots, F32)] * 2
    scratch += [
        pltpu.VMEM((2, 2 * n, width), F32),
        pltpu.VMEM((2, 2 * n if first else 3 * n, width), F32),
        pltpu.VMEM(sums, F32),
        pltpu.VMEM((8, n), F32),
        pltpu.VMEM(probe.shape, F32),
        pltpu.VMEM(table.shape, BF16),
        pltpu.VMEM((count // GROUP, 2, GROUP, n, LANES), F32),
        pltpu.VMEM((GROUP, 2, n, n), F32),
        pltpu.VMEM((GROUP, 2, 2 * n, n), BF16),
        pltpu.VMEM((GROUP, 2, n, 2 * n), BF16),
        pltpu.VMEM((GROUP, 2, n, 2 * n), F32),
        pltpu.SemaphoreType.DMA((12,)),
    ]
    return pl.pallas_call(
        functools.partial(windows_kernel, first, amp_first),
        grid_spec=pltpu.PrefetchScalarGridSpec(
            num_scalar_prefetch=1,
            grid=(count // GROUP,),
            in_specs=[anywhere] * len(inputs),
            out_specs=[anywhere] * len(shapes),
            scratch_shapes=scratch,
        ),
        out_shape=[jax.ShapeDtypeStruct(s, F32) for s in shapes],
        compiler_params=pltpu.CompilerParams(vmem_limit_bytes=VMEM_MIB << 20),
        name="near" if first else "across",
    )(offs, *inputs)


def assemble_kernel(scale, me_ref, own_ref, other_ref, losses_ref, out_ref, loss_ref, stage, sem):
    half, planes, rows, n = own_ref.shape
    quarter = losses_ref.shape[0]
    me = me_ref[0]
    copies = []
    for core, ref in enumerate((own_ref, other_ref)):
        for slot in range(half):
            owner = owner_of(me, core, slot, 2 * half)
            copies.append(pltpu.make_async_copy(ref.at[slot], stage.at[:, owner], sem.at[len(copies)]))
    for copy in copies:
        copy.start()
    loss = jnp.zeros(losses_ref.shape[1:], F32)
    for z in range(quarter):
        loss = loss + losses_ref[lax.rem(me // 4 + quarter - z, quarter)]
    loss_ref[0] = jnp.sum(loss) * scale
    for copy in copies:
        copy.wait()
    out = pltpu.make_async_copy(stage, out_ref, sem.at[0])
    out.start()
    out.wait()


def assemble(me, own, other, losses, scale):
    half, planes, rows, n = own.shape
    shape = (planes, 2 * half, rows, n)
    anywhere = pl.BlockSpec(memory_space=pl.ANY)
    return pl.pallas_call(
        functools.partial(assemble_kernel, scale),
        in_specs=[pl.BlockSpec(memory_space=pltpu.SMEM), anywhere, anywhere, pl.BlockSpec(memory_space=pltpu.VMEM)],
        out_specs=[pl.BlockSpec(memory_space=pltpu.HBM), pl.BlockSpec(memory_space=pltpu.SMEM)],
        out_shape=[jax.ShapeDtypeStruct(shape, F32), jax.ShapeDtypeStruct((1,), F32)],
        scratch_shapes=[pltpu.VMEM(shape, F32), pltpu.SemaphoreType.DMA((2 * half,))],
        name="assemble",
    )(me.reshape(1), own, other, losses)


def swap(x, bit):
    size = lax.axis_size("row")
    return lax.ppermute(x, "row", [(i, i ^ bit) for i in range(size)])


def shift(x, by):
    size = lax.axis_size("row")
    return lax.ppermute(x, "row", [(i, (i + by) % size) for i in range(size)])


def tree(parts):
    while len(parts) > 1:
        parts = [sum(parts[i + 1 : i + 2], parts[i]) for i in range(0, len(parts), 2)]
    return parts[0]


def per_device(object_field, probe, amplitude, offsets):
    tile = object_field.shape[1]
    n = probe.shape[2]
    count = offsets.shape[0]
    near = count // 2
    size = lax.axis_size("row")
    me = lax.axis_index("row")
    table = jnp.asarray(dft_tables(n))
    below = lax.ppermute(object_field[:, :n], "row", [(i, i - 1) for i in range(1, size)])
    offs = jnp.concatenate([offsets - jnp.stack([me * tile, 0]), jnp.stack([me, 0])[None]])
    grad, pg, loss = windows(True, size, near, offs, object_field, probe, amplitude, 0, table)
    grad, low, keep, away = windows(
        False, size, count - near, offs, object_field, probe, amplitude, near, table, (below, grad, pg, loss)
    )
    hop = lax.ppermute(low, "row", [(i, i + 4) for i in range(3, size - 4, 4)])
    rows = n // size
    quarter = size // 4
    away = swap(away, 1)
    beside = swap(keep[quarter:] + away[quarter:], 2)
    x = keep[:quarter] + away[:quarter] + beside
    hop, x = lax.optimization_barrier((hop, x))
    carried = jnp.where(me % 4 == 3, hop, low)
    carried = lax.ppermute(carried, "row", [(i, i - 3 if i % 4 == 3 else i + 1) for i in range(size)])
    parts = [x[0]] + [shift(x[z], 4 * z) for z in range(1, quarter)]
    total = tree(parts)
    losses = jnp.stack([p[10 * rows :] for p in parts])
    planes = total[: 10 * rows].reshape(5, 2, rows, n // 2)
    y = planes[:4] / jnp.sqrt(planes[4] + 1.0)
    y = jnp.concatenate([y[:, 0], y[:, 1]], -1)
    others = [shift(y, -4 * z) for z in range(1, quarter)]
    object_grad = grad.at[:, :n].add(carried)
    object_grad, y = lax.optimization_barrier((object_grad, y))
    y = jnp.stack([y] + others)
    y = jnp.concatenate([y, swap(y, 2)])
    probe_dir, loss = assemble(me, y, swap(y, 1), losses, 1.0 / (count * size * n * n))
    probe_dir = probe_dir.reshape(2, 2, n, n)
    return (object_grad, probe_dir, loss)


def solution(mesh):
    placed = (
        P(None, ("groups", "row"), None),
        P(),
        P(("groups", "row"), None, None),
        P(("groups", "row"), None),
    )
    return jax.shard_map(
        per_device,
        mesh=mesh,
        in_specs=placed,
        out_specs=(P(None, ("groups", "row"), None), P("groups", None, None, None), P("groups")),
        check_vma=False,
    )
```

time: 289 us -> 74.6 us (0.26)
  local copies, waits for them, and re-layouts: 106 us -> 6.26 us
  between operations: 46.1 us -> 0.91 us
  other arithmetic: 42.8 us -> 2.21 us
  blocking collectives: 35.7 us -> 0 us
  matrix products: 22 us -> 0 us
  Pallas kernels: 0 us -> 19.4 us
  starting transfers between devices: 4.93 us -> 18.7 us
    dynamic_update_slice x8 -> x0, local copies, waits for them, and re-layouts: 50.2 us -> none  [per_device(): lax.dynamic_update_slice(grad_ext, current + win_grad[position], start)]
    psum x1 -> x0, blocking collectives: 35.7 us -> none  [per_device(): loss_total = lax.psum(loss_part, 'row')]
    gather x24 -> x0, local copies, waits for them, and re-layouts: 32.5 us -> none
    psum x1 -> x0, waiting for transfers between devices: 28.7 us -> none  [per_device(): probe_sum, illum_sum = lax.psum((probe_grad, illumination), 'row')]
    ppermute x2 -> x13, waiting for transfers between devices: 0.01 us -> 26.7 us  [the longest x4 16.3 us: swap(): return lax.ppermute(x, 'row', [(i, i ^ bit) for i in range(size)])]
    dot_general x2 -> x0, matrix products: 22 us -> none  [the longest x1 12 us: window_terms(): jnp.einsum('pmdik,cjdk->pmcij', grad_half, column, preferred_element_type...]
    pallas_call x0 -> x3, Pallas kernels: none -> 19.4 us  [the longest x2 15.8 us: windows(): pl.pallas_call(functools.partial(windows_kernel, first, amp_first), grid_...]
    reduce_sum x3 -> x0, other arithmetic: 15.1 us -> none  [the longest x1 7.21 us: window_terms(): jnp.sum(o_re * g_re + o_im * g_im, 0)]
  transfers between devices with their start and end apart: 3 -> 13, of which waited for: 1 -> 8; matrix products, arithmetic and copies ran while one was open for 17% -> 3% of each run, Pallas kernels for 0% -> 10%
where the time goes in v3:
time: 74.6 us; the launch traced here: 74.2 us
  waiting for transfers between devices  26.7 us (36%)
  Pallas kernels  19.4 us (26%)
  starting transfers between devices  18.7 us (25%)
  local copies, waits for them, and re-layouts  6.26 us (8%)
  other arithmetic  2.21 us (3%)
  between operations  0.91 us (1%)
    ppermute x4, waiting for transfers between devices, swap(): return lax.ppermute(x, 'row', [(i, i ^ bit) for i in range(size)])  16.3 us
    pallas_call x2, Pallas kernels, windows(): pl.pallas_call(functools.partial(windows_kernel, first, amp_first), grid_...  15.8 us
    ppermute x6, starting transfers between devices, shift(): return lax.ppermute(x, 'row', [(i, (i + by) % size) for i in range(size)])  11 us
    ppermute x6, waiting for transfers between devices, shift(): return lax.ppermute(x, 'row', [(i, (i + by) % size) for i in range(size)])  9.76 us
    ppermute x4, starting transfers between devices, swap(): return lax.ppermute(x, 'row', [(i, i ^ bit) for i in range(size)])  5.66 us
    unnamed x25, local copies, waits for them, and re-layouts  4.89 us
    pallas_call x1, Pallas kernels, assemble(): pl.pallas_call(functools.partial(assemble_kernel, scale), in_specs=[pl.Bl...  3.58 us
  transfers between devices with their start and end apart: 13, of which 8 were waited for; matrix products, arithmetic and copies ran while one was open for 3% of the time, Pallas kernels for 10%

profile of v3, /device:TPU:0, one launch (start us, length us, event | category | flops | bytes accessed | tf_op | source)
XLA Modules:
  0.0 74.2 jit_solution(7128235398520493563)
XLA Ops:
  0.6 1.3 %slice.84 = f32[2,256,384]{2,1,0:T(8,128)S(1)} slice(f32[2,512,384]{2,1,0:T(8,128)} %refs_0_.3), slice={[0:2], [0:256], [0:384]} | slice | bytes 1572864 | tf_op jit(solution)/shard_map/slice | solution.py:374
  2.0 1.3 %collective-permute-start = (f32[2,256,384]{2,1,0:T(8,128)S(1)}, f32[2,256,384]{2,1,0:T(8,128)S(1)}, u32[]{:S(2)}, u32[]{:S(2)}) collective-permute-start(f32[2,256,384]{2,1,0:T(8,128)S(1)} %slice.84), channel_id=1, source_target_pairs={{1,0},{2,1},{3,2},{4,3},{5,4},{6,5},{7,6},{8,7},{9,8},{10,9},{11,1... | collective-permute-start | bytes 2359304 | tf_op jit(solution)/shard_map/ppermute | solution.py:374
  3.5 1.6 %copy-done.1 = f32[8,256,256]{2,1,0:T(8,128)S(1)} copy-done((f32[8,256,256]{2,1,0:T(8,128)S(1)}, f32[8,256,256]{2,1,0:T(8,128)}, u32[]{:S(2)}) %copy-start.1) | copy-done | bytes 2097176
  5.1 1.2 %copy-done.2 = f32[2,2,256,256]{3,2,1,0:T(8,128)S(1)} copy-done((f32[2,2,256,256]{3,2,1,0:T(8,128)S(1)}, f32[2,2,256,256]{3,2,1,0:T(8,128)}, u32[]{:S(2)}) %copy-start.2) | copy-done | bytes 1048600
  6.4 1.1 %copy-done.3 = bf16[6,256,256]{2,1,0:T(8,128)(2,1)S(1)} copy-done((bf16[6,256,256]{2,1,0:T(8,128)(2,1)S(1)}, bf16[6,256,256]{2,1,0:T(8,128)(2,1)}, u32[]{:S(2)}) %copy-start.3) | copy-done | bytes 786456
  7.5 7.3 %near.1 = (f32[2,512,384]{2,1,0:T(8,128)S(1)}, f32[5,16,16,256]{3,2,1,0:T(8,128)S(1)}, f32[8,256]{1,0:T(8,128)S(1)}) custom-call(s32[9,2]{1,0:T(8,128)S(1)} %pad_add_fusion.off_ref, f32[2,512,384]{2,1,0:T(8,128)S(1)} %copy-done, f32[2,2,256,256]{3,2,1,0:T(8,128)S(1)} %copy-done.2, f32[8,256,256]{2,1,0:T(8,128)S(1)} %copy-done.1, ...), custom_call_target="tpu_custom_call" | custom-call | tf_op jit(solution)/shard_map/near/pallas_call | solution.py:299
  14.8 8.5 %across.1 = (f32[2,512,384]{2,1,0:T(8,128)}, f32[2,256,384]{2,1,0:T(8,128)S(1)}, f32[8,168,128]{2,1,0:T(8,128)S(1)}, f32[8,168,128]{2,1,0:T(8,128)S(1)}) custom-call(s32[9,2]{1,0:T(8,128)S(1)} %pad_add_fusion.off_ref, f32[2,512,384]{2,1,0:T(8,128)S(1)} %copy-done, f32[2,2,256,256]{3,2,1,0:T(8,128)S(1)} %copy-done.2, f32[8,256,256]{2,1,0:T(8,128)S(1)} %copy-done.1, ...), custom_call_target="tpu_custom_call" | custom-call | tf_op jit(solution)/shard_map/across/pallas_call | solution.py:299
  23.3 1.8 %collective-permute-start.2 = (f32[8,168,128]{2,1,0:T(8,128)S(1)}, f32[8,168,128]{2,1,0:T(8,128)S(1)}, u32[]{:S(2)}, u32[]{:S(2)}) collective-permute-start(f32[8,168,128]{2,1,0:T(8,128)S(1)} %get-tuple-element.34), channel_id=1, source_target_pairs={{0,1},{1,0},{2,3},{3,2},{4,5},{5,4},{6,7},{7,6},{8,9},{9,8},{10,11... | collective-permute-start | bytes 2064392 | tf_op jit(solution)/shard_map/ppermute | solution.py:352
  25.9 1.1 %collective-permute-done.2 = f32[8,168,128]{2,1,0:T(8,128)S(1)} collective-permute-done((f32[8,168,128]{2,1,0:T(8,128)S(1)}, f32[8,168,128]{2,1,0:T(8,128)S(1)}, u32[]{:S(2)}, u32[]{:S(2)}) %collective-permute-start.2) | collective-permute-done | bytes 688160 | tf_op jit(solution)/shard_map/ppermute | solution.py:352
  27.0 2.3 %collective-permute-start.3 = (f32[4,168,128]{2,1,0:T(8,128)S(1)}, f32[4,168,128]{2,1,0:T(8,128)S(1)}, u32[]{:S(2)}, u32[]{:S(2)}) collective-permute-start(f32[4,168,128]{2,1,0:T(8,128)S(1)} %slice_add_fusion), channel_id=1, source_target_pairs={{0,2},{1,3},{2,0},{3,1},{4,6},{5,7},{6,4},{7,5},{8,10},{9,11},{10,... | collective-permute-start | bytes 1032200 | tf_op jit(solution)/shard_map/ppermute | solution.py:352
  29.3 8.0 %collective-permute-done.3 = f32[4,168,128]{2,1,0:T(8,128)S(1)} collective-permute-done((f32[4,168,128]{2,1,0:T(8,128)S(1)}, f32[4,168,128]{2,1,0:T(8,128)S(1)}, u32[]{:S(2)}, u32[]{:S(2)}) %collective-permute-start.3) | collective-permute-done | bytes 344096 | tf_op jit(solution)/shard_map/ppermute | solution.py:352
  37.3 1.0 %fusion = f32[4,168,128]{2,1,0:T(8,128)S(1)} fusion(f32[4,168,128]{2,1,0:T(8,128)S(1)} %collective-permute-done.3, f32[8,168,128]{2,1,0:T(8,128)S(1)} %collective-permute-done.2, f32[8,168,128]{2,1,0:T(8,128)} %copy-done.4), kind=kLoop, calls=%fused_computation.4 | loop fusion | flops 172032 | bytes 1376256 | tf_op jit(solution)/shard_map/add | solution.py:385
  38.4 5.0 %collective-permute-start.7 = (f32[168,128]{1,0:T(8,128)S(1)}, f32[168,128]{1,0:T(8,128)S(1)}, u32[]{:S(2)}, u32[]{:S(2)}) collective-permute-start(f32[168,128]{1,0:T(8,128)S(1)} %get-tuple-element.41), channel_id=1, source_target_pairs={{0,12},{1,13},{2,14},{3,15},{4,0},{5,1},{6,2},{7,3},{8,4},{9,5},{1... | collective-permute-start | bytes 258056 | tf_op jit(solution)/shard_map/ppermute | solution.py:357
  43.4 1.5 %collective-permute-start.5 = (f32[168,128]{1,0:T(8,128)S(1)}, f32[168,128]{1,0:T(8,128)S(1)}, u32[]{:S(2)}, u32[]{:S(2)}) collective-permute-start(f32[168,128]{1,0:T(8,128)S(1)} %get-tuple-element.43), channel_id=1, source_target_pairs={{0,4},{1,5},{2,6},{3,7},{4,8},{5,9},{6,10},{7,11},{8,12},{9,13},{1... | collective-permute-start | bytes 258056 | tf_op jit(solution)/shard_map/ppermute | solution.py:357
  45.0 1.3 %collective-permute-done.7 = f32[168,128]{1,0:T(8,128)S(1)} collective-permute-done((f32[168,128]{1,0:T(8,128)S(1)}, f32[168,128]{1,0:T(8,128)S(1)}, u32[]{:S(2)}, u32[]{:S(2)}) %collective-permute-start.7) | collective-permute-done | bytes 86048 | tf_op jit(solution)/shard_map/ppermute | solution.py:357
  46.4 4.8 %collective-permute-done.6 = f32[168,128]{1,0:T(8,128)S(1)} collective-permute-done((f32[168,128]{1,0:T(8,128)S(1)}, f32[168,128]{1,0:T(8,128)S(1)}, u32[]{:S(2)}, u32[]{:S(2)}) %collective-permute-start.6) | collective-permute-done | bytes 86048 | tf_op jit(solution)/shard_map/ppermute | solution.py:357
  51.3 1.6 %collective-permute-start.8 = (f32[4,16,256]{2,1,0:T(8,128)S(1)}, f32[4,16,256]{2,1,0:T(8,128)S(1)}, u32[]{:S(2)}, u32[]{:S(2)}) collective-permute-start(f32[4,16,256]{2,1,0:T(8,128)S(1)} %pad_maximum_fusion.1), channel_id=1, source_target_pairs={{0,12},{1,13},{2,14},{3,15},{4,0},{5,1},{6,2},{7,3},{8,4},{9,5},{1... | collective-permute-start | bytes 196616 | tf_op jit(solution)/shard_map/ppermute | solution.py:357
  52.9 0.9 %collective-permute-start.9 = (f32[4,16,256]{2,1,0:T(8,128)S(1)}, f32[4,16,256]{2,1,0:T(8,128)S(1)}, u32[]{:S(2)}, u32[]{:S(2)}) collective-permute-start(f32[4,16,256]{2,1,0:T(8,128)S(1)} %pad_maximum_fusion.1), channel_id=1, source_target_pairs={{0,8},{1,9},{2,10},{3,11},{4,12},{5,13},{6,14},{7,15},{8,0},{9,1},... | collective-permute-start | bytes 196616 | tf_op jit(solution)/shard_map/ppermute | solution.py:357
  53.8 1.9 %collective-permute-start.10 = (f32[4,16,256]{2,1,0:T(8,128)S(1)}, f32[4,16,256]{2,1,0:T(8,128)S(1)}, u32[]{:S(2)}, u32[]{:S(2)}) collective-permute-start(f32[4,16,256]{2,1,0:T(8,128)S(1)} %pad_maximum_fusion.1), channel_id=1, source_target_pairs={{0,4},{1,5},{2,6},{3,7},{4,8},{5,9},{6,10},{7,11},{8,12},{9,13},{1... | collective-permute-start | bytes 196616 | tf_op jit(solution)/shard_map/ppermute | solution.py:357
  56.6 3.6 %collective-permute-done.9 = f32[4,16,256]{2,1,0:T(8,128)S(1)} collective-permute-done((f32[4,16,256]{2,1,0:T(8,128)S(1)}, f32[4,16,256]{2,1,0:T(8,128)S(1)}, u32[]{:S(2)}, u32[]{:S(2)}) %collective-permute-start.9) | collective-permute-done | bytes 65568 | tf_op jit(solution)/shard_map/ppermute | solution.py:357
  60.3 1.4 %collective-permute-start.11 = (f32[4,4,16,256]{3,2,1,0:T(8,128)S(1)}, f32[4,4,16,256]{3,2,1,0:T(8,128)S(1)}, u32[]{:S(2)}, u32[]{:S(2)}) collective-permute-start(f32[4,4,16,256]{3,2,1,0:T(8,128)S(1)} %pad_maximum_fusion), channel_id=1, source_target_pairs={{0,2},{1,3},{2,0},{3,1},{4,6},{5,7},{6,4},{7,5},{8,10},{9,11},{10,... | collective-permute-start | bytes 786440 | tf_op jit(solution)/shard_map/ppermute | solution.py:352
  61.8 6.0 %collective-permute-done.11 = f32[4,4,16,256]{3,2,1,0:T(8,128)S(1)} collective-permute-done((f32[4,4,16,256]{3,2,1,0:T(8,128)S(1)}, f32[4,4,16,256]{3,2,1,0:T(8,128)S(1)}, u32[]{:S(2)}, u32[]{:S(2)}) %collective-permute-start.11) | collective-permute-done | bytes 262176 | tf_op jit(solution)/shard_map/ppermute | solution.py:352
  68.6 1.2 %collective-permute-done.12.other_ref = f32[8,4,16,256]{3,2,1,0:T(8,128)S(1)} collective-permute-done((f32[8,4,16,256]{3,2,1,0:T(8,128)S(1)}, f32[8,4,16,256]{3,2,1,0:T(8,128)S(1)}, u32[]{:S(2)}, u32[]{:S(2)}) %collective-permute-start.12) | collective-permute-done | bytes 524320 | tf_op jit(solution)/shard_map/ppermute | solution.py:352
  70.6 3.6 %assemble.1 = (f32[4,16,16,256]{3,2,1,0:T(8,128)}, f32[1]{0:T(128)}) custom-call(s32[1]{0:T(128)} %bitcast.1.me_ref, f32[8,4,16,256]{3,2,1,0:T(8,128)} %copy-done.5, f32[8,4,16,256]{3,2,1,0:T(8,128)} %copy-done.6, f32[4,8,128]{2,1,0:T(8,128)} %pad_maximum_fusion.2.losses_ref), custom_call_target="tpu_custom_call" | custom-call | tf_op jit(solution)/shard_map/assemble/pallas_call | solution.py:340
  (53 shorter events, 3.7 us)
Async XLA Ops:
  0.6 2.9 %copy-start = (f32[2,512,384]{2,1,0:T(8,128)S(1)}, f32[2,512,384]{2,1,0:T(8,128)}, u32[]{:S(2)}) copy-start(f32[2,512,384]{2,1,0:T(8,128)} %refs_0_.3) | copy-start | bytes 4718596
  0.6 2.6 %copy-start.9 = (s32[8,2]{0,1:T(2,128)S(1)}, s32[8,2]{0,1:T(2,128)}, u32[]{:S(2)}) copy-start(s32[8,2]{0,1:T(2,128)} %param.10) | copy-start | bytes 196
  2.0 12.8 %collective-permute-start = (f32[2,256,384]{2,1,0:T(8,128)S(1)}, f32[2,256,384]{2,1,0:T(8,128)S(1)}, u32[]{:S(2)}, u32[]{:S(2)}) collective-permute-start(f32[2,256,384]{2,1,0:T(8,128)S(1)} %slice.84), channel_id=1, source_target_pairs={{1,0},{2,1},{3,2},{4,3},{5,4},{6,5},{7,6},{8,7},{9,8},{10,9},{11,1... | collective-permute-start | bytes 2359304 | tf_op jit(solution)/shard_map/ppermute | solution.py:374
  3.5 1.6 %copy-start.1 = (f32[8,256,256]{2,1,0:T(8,128)S(1)}, f32[8,256,256]{2,1,0:T(8,128)}, u32[]{:S(2)}) copy-start(f32[8,256,256]{2,1,0:T(8,128)} %refs_2_.3) | copy-start | bytes 6291460
  5.1 1.2 %copy-start.2 = (f32[2,2,256,256]{3,2,1,0:T(8,128)S(1)}, f32[2,2,256,256]{3,2,1,0:T(8,128)}, u32[]{:S(2)}) copy-start(f32[2,2,256,256]{3,2,1,0:T(8,128)} %refs_1_.3) | copy-start | bytes 3145732
  6.4 1.1 %copy-start.3 = (bf16[6,256,256]{2,1,0:T(8,128)(2,1)S(1)}, bf16[6,256,256]{2,1,0:T(8,128)(2,1)}, u32[]{:S(2)}) copy-start(bf16[6,256,256]{2,1,0:T(8,128)(2,1)} %constant.51.clone.refs_3_) | copy-start | bytes 2359300
  23.3 3.6 %copy-start.4 = (f32[8,168,128]{2,1,0:T(8,128)}, f32[8,168,128]{2,1,0:T(8,128)S(1)}, u32[]{:S(2)}) copy-start(f32[8,168,128]{2,1,0:T(8,128)S(1)} %get-tuple-element.33) | copy-start | bytes 2064388
  23.3 3.6 %collective-permute-start.2 = (f32[8,168,128]{2,1,0:T(8,128)S(1)}, f32[8,168,128]{2,1,0:T(8,128)S(1)}, u32[]{:S(2)}, u32[]{:S(2)}) collective-permute-start(f32[8,168,128]{2,1,0:T(8,128)S(1)} %get-tuple-element.34), channel_id=1, source_target_pairs={{0,1},{1,0},{2,3},{3,2},{4,5},{5,4},{6,7},{7,6},{8,9},{9,8},{10,11... | collective-permute-start | bytes 2064392 | tf_op jit(solution)/shard_map/ppermute | solution.py:352
  25.2 13.2 %collective-permute-start.1 = (f32[2,256,384]{2,1,0:T(8,128)S(1)}, f32[2,256,384]{2,1,0:T(8,128)S(1)}, u32[]{:S(2)}, u32[]{:S(2)}) collective-permute-start(f32[2,256,384]{2,1,0:T(8,128)S(1)} %get-tuple-element.32), channel_id=1, source_target_pairs={{3,7},{7,11},{11,15},{19,23},{23,27},{27,31}} | collective-permute-start | bytes 2359304 | tf_op jit(solution)/shard_map/ppermute | solution.py:380
  27.0 10.4 %collective-permute-start.3 = (f32[4,168,128]{2,1,0:T(8,128)S(1)}, f32[4,168,128]{2,1,0:T(8,128)S(1)}, u32[]{:S(2)}, u32[]{:S(2)}) collective-permute-start(f32[4,168,128]{2,1,0:T(8,128)S(1)} %slice_add_fusion), channel_id=1, source_target_pairs={{0,2},{1,3},{2,0},{3,1},{4,6},{5,7},{6,4},{7,5},{8,10},{9,11},{10,... | collective-permute-start | bytes 1032200 | tf_op jit(solution)/shard_map/ppermute | solution.py:352
  38.4 8.0 %collective-permute-start.7 = (f32[168,128]{1,0:T(8,128)S(1)}, f32[168,128]{1,0:T(8,128)S(1)}, u32[]{:S(2)}, u32[]{:S(2)}) collective-permute-start(f32[168,128]{1,0:T(8,128)S(1)} %get-tuple-element.41), channel_id=1, source_target_pairs={{0,12},{1,13},{2,14},{3,15},{4,0},{5,1},{6,2},{7,3},{8,4},{9,5},{1... | collective-permute-start | bytes 258056 | tf_op jit(solution)/shard_map/ppermute | solution.py:357
  43.4 7.8 %collective-permute-start.6 = (f32[168,128]{1,0:T(8,128)S(1)}, f32[168,128]{1,0:T(8,128)S(1)}, u32[]{:S(2)}, u32[]{:S(2)}) collective-permute-start(f32[168,128]{1,0:T(8,128)S(1)} %get-tuple-element.42), channel_id=1, source_target_pairs={{0,8},{1,9},{2,10},{3,11},{4,12},{5,13},{6,14},{7,15},{8,0},{9,1},... | collective-permute-start | bytes 258056 | tf_op jit(solution)/shard_map/ppermute | solution.py:357
  43.4 13.1 %copy-start.7 = (f32[2,512,384]{2,1,0:T(8,128)S(1)}, f32[2,512,384]{2,1,0:T(8,128)}, u32[]{:S(2)}) copy-start(f32[2,512,384]{2,1,0:T(8,128)} %get-tuple-element.31) | copy-start | bytes 4718596
  43.4 7.8 %collective-permute-start.5 = (f32[168,128]{1,0:T(8,128)S(1)}, f32[168,128]{1,0:T(8,128)S(1)}, u32[]{:S(2)}, u32[]{:S(2)}) collective-permute-start(f32[168,128]{1,0:T(8,128)S(1)} %get-tuple-element.43), channel_id=1, source_target_pairs={{0,4},{1,5},{2,6},{3,7},{4,8},{5,9},{6,10},{7,11},{8,12},{9,13},{1... | collective-permute-start | bytes 258056 | tf_op jit(solution)/shard_map/ppermute | solution.py:357
  45.0 11.5 %collective-permute-start.4 = (f32[2,256,384]{2,1,0:T(8,128)S(1)}, f32[2,256,384]{2,1,0:T(8,128)S(1)}, u32[]{:S(2)}, u32[]{:S(2)}) collective-permute-start(f32[2,256,384]{2,1,0:T(8,128)S(1)} %broadcast_select_fusion), channel_id=1, source_target_pairs={{0,1},{1,2},{2,3},{3,0},{4,5},{5,6},{6,7},{7,4},{8,9},{9,10},{10,1... | collective-permute-start | bytes 2359304 | tf_op jit(solution)/shard_map/ppermute | solution.py:388
  51.3 5.4 %collective-permute-start.8 = (f32[4,16,256]{2,1,0:T(8,128)S(1)}, f32[4,16,256]{2,1,0:T(8,128)S(1)}, u32[]{:S(2)}, u32[]{:S(2)}) collective-permute-start(f32[4,16,256]{2,1,0:T(8,128)S(1)} %pad_maximum_fusion.1), channel_id=1, source_target_pairs={{0,12},{1,13},{2,14},{3,15},{4,0},{5,1},{6,2},{7,3},{8,4},{9,5},{1... | collective-permute-start | bytes 196616 | tf_op jit(solution)/shard_map/ppermute | solution.py:357
  52.9 7.4 %collective-permute-start.9 = (f32[4,16,256]{2,1,0:T(8,128)S(1)}, f32[4,16,256]{2,1,0:T(8,128)S(1)}, u32[]{:S(2)}, u32[]{:S(2)}) collective-permute-start(f32[4,16,256]{2,1,0:T(8,128)S(1)} %pad_maximum_fusion.1), channel_id=1, source_target_pairs={{0,8},{1,9},{2,10},{3,11},{4,12},{5,13},{6,14},{7,15},{8,0},{9,1},... | collective-permute-start | bytes 196616 | tf_op jit(solution)/shard_map/ppermute | solution.py:357
  53.8 6.5 %collective-permute-start.10 = (f32[4,16,256]{2,1,0:T(8,128)S(1)}, f32[4,16,256]{2,1,0:T(8,128)S(1)}, u32[]{:S(2)}, u32[]{:S(2)}) collective-permute-start(f32[4,16,256]{2,1,0:T(8,128)S(1)} %pad_maximum_fusion.1), channel_id=1, source_target_pairs={{0,4},{1,5},{2,6},{3,7},{4,8},{5,9},{6,10},{7,11},{8,12},{9,13},{1... | collective-permute-start | bytes 196616 | tf_op jit(solution)/shard_map/ppermute | solution.py:357
  56.6 17.6 %copy-start.8 = (f32[2,512,384]{2,1,0:T(8,128)}, f32[2,512,384]{2,1,0:T(8,128)S(1)}, u32[]{:S(2)}) copy-start(f32[2,512,384]{2,1,0:T(8,128)S(1)} %add_dynamic-update-slice_fusion) | copy-start | bytes 4718596
  60.3 7.4 %collective-permute-start.11 = (f32[4,4,16,256]{3,2,1,0:T(8,128)S(1)}, f32[4,4,16,256]{3,2,1,0:T(8,128)S(1)}, u32[]{:S(2)}, u32[]{:S(2)}) collective-permute-start(f32[4,4,16,256]{3,2,1,0:T(8,128)S(1)} %pad_maximum_fusion), channel_id=1, source_target_pairs={{0,2},{1,3},{2,0},{3,1},{4,6},{5,7},{6,4},{7,5},{8,10},{9,11},{10,... | collective-permute-start | bytes 786440 | tf_op jit(solution)/shard_map/ppermute | solution.py:352
  67.8 2.0 %copy-start.5 = (f32[8,4,16,256]{3,2,1,0:T(8,128)}, f32[8,4,16,256]{3,2,1,0:T(8,128)S(1)}, u32[]{:S(2)}) copy-start(f32[8,4,16,256]{3,2,1,0:T(8,128)S(1)} %constant_dynamic-update-slice_fusion.own_ref) | copy-start | bytes 1572868
  67.8 2.0 %collective-permute-start.12 = (f32[8,4,16,256]{3,2,1,0:T(8,128)S(1)}, f32[8,4,16,256]{3,2,1,0:T(8,128)S(1)}, u32[]{:S(2)}, u32[]{:S(2)}) collective-permute-start(f32[8,4,16,256]{3,2,1,0:T(8,128)S(1)} %constant_dynamic-update-slice_fusion.own_ref), channel_id=1, source_target_pairs={{0,1},{1,0},{2,3},{3,2},{4,5},{5,4},{6,7},{7,6},{8,9},{9,8},{10,11... | collective-permute-start | bytes 1572872 | tf_op jit(solution)/shard_map/ppermute | solution.py:352
  69.8 0.8 %copy-start.6 = (f32[8,4,16,256]{3,2,1,0:T(8,128)}, f32[8,4,16,256]{3,2,1,0:T(8,128)S(1)}, u32[]{:S(2)}) copy-start(f32[8,4,16,256]{3,2,1,0:T(8,128)S(1)} %collective-permute-done.12.other_ref) | copy-start | bytes 1572868

commit v4 on v3

--- a/solution.py
+++ b/solution.py
@@ -306,45 +306,64 @@
             scratch_shapes=scratch,
         ),
         out_shape=[jax.ShapeDtypeStruct(s, F32) for s in shapes],
-        compiler_params=pltpu.CompilerParams(vmem_limit_bytes=VMEM_MIB << 20),
+        compiler_params=pltpu.CompilerParams(vmem_limit_bytes=(48 if first else 20) << 20),
         name="near" if first else "across",
     )(offs, *inputs)
 
 
-def assemble_kernel(scale, me_ref, own_ref, other_ref, losses_ref, out_ref, loss_ref, stage, sem):
-    half, planes, rows, n = own_ref.shape
-    quarter = losses_ref.shape[0]
+def place_kernel(nears, scale, me_ref, *refs):
+    pieces, refs = refs[: len(nears)], refs[len(nears) :]
+    if scale:
+        losses_ref, out_ref, loss_ref, stage, sem = refs
+    else:
+        unused, out_ref, stage, sem = refs
+    quarter, planes, rows, n = pieces[0].shape
     me = me_ref[0]
-    copies = []
-    for core, ref in enumerate((own_ref, other_ref)):
-        for slot in range(half):
-            owner = owner_of(me, core, slot, 2 * half)
-            copies.append(pltpu.make_async_copy(ref.at[slot], stage.at[:, owner], sem.at[len(copies)]))
+    copies = [pltpu.make_async_copy(piece, stage.at[i], sem.at[i, quarter]) for i, piece in enumerate(pieces)]
     for copy in copies:
         copy.start()
-    loss = jnp.zeros(losses_ref.shape[1:], F32)
-    for z in range(quarter):
-        loss = loss + losses_ref[lax.rem(me // 4 + quarter - z, quarter)]
-    loss_ref[0] = jnp.sum(loss) * scale
-    for copy in copies:
+    if scale:
+        loss = jnp.zeros(losses_ref.shape[1:], F32)
+        for z in range(quarter):
+            loss = loss + losses_ref[lax.rem(me // 4 + quarter - z, quarter)]
+        loss_ref[0] = jnp.sum(loss) * scale
+    out = []
+    for i, near in enumerate(nears):
+        copies[i].wait()
+        for z in range(quarter):
+            owner = owner_of(me, near, z, 4 * quarter)
+            out.append(pltpu.make_async_copy(stage.at[i, z], out_ref.at[:, owner], sem.at[i, z]))
+            out[-1].start()
+    for copy in out:
         copy.wait()
-    out = pltpu.make_async_copy(stage, out_ref, sem.at[0])
-    out.start()
-    out.wait()
-
-
-def assemble(me, own, other, losses, scale):
-    half, planes, rows, n = own.shape
-    shape = (planes, 2 * half, rows, n)
-    anywhere = pl.BlockSpec(memory_space=pl.ANY)
+
+
+def place(me, nears, pieces, losses=None, scale=None, base=None):
+    quarter, planes, rows, n = pieces[0].shape
+    shape = (planes, 4 * quarter, rows, n)
+    anywhere, hbm = pl.BlockSpec(memory_space=pl.ANY), pl.BlockSpec(memory_space=pltpu.HBM)
+    smem = pl.BlockSpec(memory_space=pltpu.SMEM)
+    in_specs = [smem] + [anywhere] * len(pieces)
+    out_specs, out_shape, aliases = [hbm], [jax.ShapeDtypeStruct(shape, F32)], {}
+    if scale:
+        in_specs, last = in_specs + [pl.BlockSpec(memory_space=pltpu.VMEM)], losses
+        out_specs, out_shape = out_specs + [smem], out_shape + [jax.ShapeDtypeStruct((1,), F32)]
+    else:
+        in_specs, last = in_specs + [hbm], base
+        aliases = {1 + len(pieces): 0}
     return pl.pallas_call(
-        functools.partial(assemble_kernel, scale),
-        in_specs=[pl.BlockSpec(memory_space=pltpu.SMEM), anywhere, anywhere, pl.BlockSpec(memory_space=pltpu.VMEM)],
-        out_specs=[pl.BlockSpec(memory_space=pltpu.HBM), pl.BlockSpec(memory_space=pltpu.SMEM)],
-        out_shape=[jax.ShapeDtypeStruct(shape, F32), jax.ShapeDtypeStruct((1,), F32)],
-        scratch_shapes=[pltpu.VMEM(shape, F32), pltpu.SemaphoreType.DMA((2 * half,))],
-        name="assemble",
-    )(me.reshape(1), own, other, losses)
+        functools.partial(place_kernel, nears, scale),
+        in_specs=in_specs,
+        out_specs=out_specs,
+        out_shape=out_shape,
+        scratch_shapes=[
+            pltpu.VMEM((len(nears), *pieces[0].shape), F32),
+            pltpu.SemaphoreType.DMA((len(nears), quarter + 1)),
+        ],
+        input_output_aliases=aliases,
+        compiler_params=pltpu.CompilerParams(vmem_limit_bytes=4 << 20),
+        name="place",
+    )(me.reshape(1), *pieces, last)
 
 
 def swap(x, bit):
@@ -392,12 +411,15 @@
     planes = total[: 10 * rows].reshape(5, 2, rows, n // 2)
     y = planes[:4] / jnp.sqrt(planes[4] + 1.0)
     y = jnp.concatenate([y[:, 0], y[:, 1]], -1)
-    others = [shift(y, -4 * z) for z in range(1, quarter)]
+    y = jnp.stack([y] + [shift(y, -4 * z) for z in range(1, quarter)])
+    sibling = swap(y, 1)
+    beside = swap(y, 2)
+    probe_dir, loss = place(me, (0, 1), (y, sibling), losses, 1.0 / (count * size * n * n))
     object_grad = grad.at[:, :n].add(carried)
-    object_grad, y = lax.optimization_barrier((object_grad, y))
-    y = jnp.stack([y] + others)
-    y = jnp.concatenate([y, swap(y, 2)])
-    probe_dir, loss = assemble(me, y, swap(y, 1), losses, 1.0 / (count * size * n * n))
+    probe_dir, object_grad, beside = lax.optimization_barrier((probe_dir, object_grad, beside))
+    sibling = swap(beside, 1)
+    (probe_dir,) = place(me, (2,), (beside,), base=probe_dir)
+    (probe_dir,) = place(me, (3,), (sibling,), base=probe_dir)
     probe_dir = probe_dir.reshape(2, 2, n, n)
     return (object_grad, probe_dir, loss)
 

time: 74.6 us -> 70.3 us (0.942)
  local copies, waits for them, and re-layouts: 6.26 us -> 2.56 us
  other arithmetic: 2.21 us -> 1.3 us
  Pallas kernels: 19.4 us -> 20.2 us
    unnamed x25 -> x15, local copies, waits for them, and re-layouts: 4.89 us -> 1.24 us
    ppermute x4 -> x5, starting transfers between devices: 5.66 us -> 7.26 us  [swap(): return lax.ppermute(x, 'row', [(i, i ^ bit) for i in range(size)])]
    ppermute x6, starting transfers between devices: 11 us -> 9.41 us  [shift(): return lax.ppermute(x, 'row', [(i, (i + by) % size) for i in range(size)])]
    pallas_call x2, Pallas kernels: 15.8 us -> 17.2 us  [windows(): pl.pallas_call(functools.partial(windows_kernel, first, amp_first), grid_...]
    ppermute x6, waiting for transfers between devices: 9.76 us -> 10.9 us  [shift(): return lax.ppermute(x, 'row', [(i, (i + by) % size) for i in range(size)])]
    add x1, other arithmetic: 1.03 us -> 0.05 us  [per_device(): x = keep[:quarter] + away[:quarter] + beside]
    ppermute x4 -> x5, waiting for transfers between devices: 16.3 us -> 15.5 us  [swap(): return lax.ppermute(x, 'row', [(i, i ^ bit) for i in range(size)])]
    pallas_call x1 -> x3, Pallas kernels: 3.58 us -> 3.07 us  [place(): pl.pallas_call(functools.partial(place_kernel, nears, scale), in_specs=in...]
  transfers between devices with their start and end apart: 13 -> 14, of which waited for: 8 -> 8; matrix products, arithmetic and copies ran while one was open for 3% -> 2% of each run, Pallas kernels for 10% -> 16%
where the time goes in v4:
time: 70.3 us; the launch traced here: 70.2 us
  waiting for transfers between devices  26.4 us (38%)
  Pallas kernels  20.2 us (29%)
  starting transfers between devices  18.7 us (27%)
  local copies, waits for them, and re-layouts  2.56 us (4%)
  other arithmetic  1.3 us (2%)
  between operations  0.92 us (1%)
    pallas_call x2, Pallas kernels, windows(): pl.pallas_call(functools.partial(windows_kernel, first, amp_first), grid_...  17.2 us
    ppermute x5, waiting for transfers between devices, swap(): return lax.ppermute(x, 'row', [(i, i ^ bit) for i in range(size)])  15.5 us
    ppermute x6, waiting for transfers between devices, shift(): return lax.ppermute(x, 'row', [(i, (i + by) % size) for i in range(size)])  10.9 us
    ppermute x6, starting transfers between devices, shift(): return lax.ppermute(x, 'row', [(i, (i + by) % size) for i in range(size)])  9.41 us
    ppermute x5, starting transfers between devices, swap(): return lax.ppermute(x, 'row', [(i, i ^ bit) for i in range(size)])  7.26 us
    pallas_call x3, Pallas kernels, place(): pl.pallas_call(functools.partial(place_kernel, nears, scale), in_specs=in...  3.07 us
  transfers between devices with their start and end apart: 14, of which 8 were waited for; matrix products, arithmetic and copies ran while one was open for 2% of the time, Pallas kernels for 16%

profile of v4, /device:TPU:0, one launch (start us, length us, event | category | flops | bytes accessed | tf_op | source)
XLA Modules:
  0.0 70.2 jit_solution(5913524759731681167)
XLA Ops:
  0.7 1.3 %slice.84 = f32[2,256,384]{2,1,0:T(8,128)S(1)} slice(f32[2,512,384]{2,1,0:T(8,128)} %refs_0_.3), slice={[0:2], [0:256], [0:384]} | slice | bytes 1572864 | tf_op jit(solution)/shard_map/slice | solution.py:393
  1.9 1.3 %collective-permute-start = (f32[2,256,384]{2,1,0:T(8,128)S(1)}, f32[2,256,384]{2,1,0:T(8,128)S(1)}, u32[]{:S(2)}, u32[]{:S(2)}) collective-permute-start(f32[2,256,384]{2,1,0:T(8,128)S(1)} %slice.84), channel_id=1, source_target_pairs={{1,0},{2,1},{3,2},{4,3},{5,4},{6,5},{7,6},{8,7},{9,8},{10,9},{11,1... | collective-permute-start | bytes 2359304 | tf_op jit(solution)/shard_map/ppermute | solution.py:393
  3.5 1.1 %copy-done.3 = bf16[6,256,256]{2,1,0:T(8,128)(2,1)S(1)} copy-done((bf16[6,256,256]{2,1,0:T(8,128)(2,1)S(1)}, bf16[6,256,256]{2,1,0:T(8,128)(2,1)}, u32[]{:S(2)}) %copy-start.3) | copy-done | bytes 786456
  4.6 8.7 %near.1 = (f32[2,512,384]{2,1,0:T(8,128)S(1)}, f32[5,16,16,256]{3,2,1,0:T(8,128)S(1)}, f32[8,256]{1,0:T(8,128)S(1)}) custom-call(s32[9,2]{1,0:T(8,128)S(1)} %pad_add_fusion.off_ref, f32[2,512,384]{2,1,0:T(8,128)} %refs_0_.3, f32[2,2,256,256]{3,2,1,0:T(8,128)S(1)} %copy-done.2, f32[8,256,256]{2,1,0:T(8,128)} %refs_2_.3, bf16[6,256,256]{2,1,0:T(8,128)(2,1)S(1)} %copy-done.3), custom_call_target="tpu_custom_call" | custom-call | tf_op jit(solution)/shard_map/near/pallas_call | solution.py:299
  13.4 8.5 %across.1 = (f32[2,512,384]{2,1,0:T(8,128)}, f32[2,256,384]{2,1,0:T(8,128)S(1)}, f32[8,168,128]{2,1,0:T(8,128)S(1)}, f32[8,168,128]{2,1,0:T(8,128)S(1)}) custom-call(s32[9,2]{1,0:T(8,128)S(1)} %pad_add_fusion.off_ref, f32[2,512,384]{2,1,0:T(8,128)S(1)} %copy-done, f32[2,2,256,256]{3,2,1,0:T(8,128)S(1)} %copy-done.2, f32[8,256,256]{2,1,0:T(8,128)S(1)} %copy-done.1, ...), custom_call_target="tpu_custom_call" | custom-call | tf_op jit(solution)/shard_map/across/pallas_call | solution.py:299
  21.9 3.3 %collective-permute-start.2 = (f32[8,168,128]{2,1,0:T(8,128)S(1)}, f32[8,168,128]{2,1,0:T(8,128)S(1)}, u32[]{:S(2)}, u32[]{:S(2)}) collective-permute-start(f32[8,168,128]{2,1,0:T(8,128)S(1)} %get-tuple-element.34), channel_id=1, source_target_pairs={{0,1},{1,0},{2,3},{3,2},{4,5},{5,4},{6,7},{7,6},{8,9},{9,8},{10,11... | collective-permute-start | bytes 2064392 | tf_op jit(solution)/shard_map/ppermute | solution.py:371
  25.9 1.1 %collective-permute-done.2 = f32[8,168,128]{2,1,0:T(8,128)S(1)} collective-permute-done((f32[8,168,128]{2,1,0:T(8,128)S(1)}, f32[8,168,128]{2,1,0:T(8,128)S(1)}, u32[]{:S(2)}, u32[]{:S(2)}) %collective-permute-start.2) | collective-permute-done | bytes 688160 | tf_op jit(solution)/shard_map/ppermute | solution.py:371
  26.9 0.8 %slice_add_fusion = f32[4,168,128]{2,1,0:T(8,128)} fusion(f32[8,168,128]{2,1,0:T(8,128)S(1)} %collective-permute-done.2, f32[8,168,128]{2,1,0:T(8,128)S(1)} %get-tuple-element.33), kind=kLoop, calls=%fused_computation.2 | loop fusion | flops 86016 | bytes 1032192 | tf_op jit(solution)/shard_map/add | solution.py:403
  27.7 2.3 %collective-permute-start.3 = (f32[4,168,128]{2,1,0:T(8,128)}, f32[4,168,128]{2,1,0:T(8,128)S(1)}, u32[]{:S(2)}, u32[]{:S(2)}) collective-permute-start(f32[4,168,128]{2,1,0:T(8,128)} %slice_add_fusion), channel_id=1, source_target_pairs={{0,2},{1,3},{2,0},{3,1},{4,6},{5,7},{6,4},{7,5},{8,10},{9,11},{10,... | collective-permute-start | bytes 1032200 | tf_op jit(solution)/shard_map/ppermute | solution.py:371
  30.0 8.3 %collective-permute-done.3 = f32[4,168,128]{2,1,0:T(8,128)S(1)} collective-permute-done((f32[4,168,128]{2,1,0:T(8,128)}, f32[4,168,128]{2,1,0:T(8,128)S(1)}, u32[]{:S(2)}, u32[]{:S(2)}) %collective-permute-start.3) | collective-permute-done | bytes 344096 | tf_op jit(solution)/shard_map/ppermute | solution.py:371
  38.4 3.5 %collective-permute-start.6 = (f32[168,128]{1,0:T(8,128)S(1)}, f32[168,128]{1,0:T(8,128)S(1)}, u32[]{:S(2)}, u32[]{:S(2)}) collective-permute-start(f32[168,128]{1,0:T(8,128)S(1)} %get-tuple-element.43), channel_id=1, source_target_pairs={{0,12},{1,13},{2,14},{3,15},{4,0},{5,1},{6,2},{7,3},{8,4},{9,5},{1... | collective-permute-start | bytes 258056 | tf_op jit(solution)/shard_map/ppermute | solution.py:376
  41.9 1.6 %collective-permute-start.4 = (f32[168,128]{1,0:T(8,128)S(1)}, f32[168,128]{1,0:T(8,128)S(1)}, u32[]{:S(2)}, u32[]{:S(2)}) collective-permute-start(f32[168,128]{1,0:T(8,128)S(1)} %get-tuple-element.45), channel_id=1, source_target_pairs={{0,4},{1,5},{2,6},{3,7},{4,8},{5,9},{6,10},{7,11},{8,12},{9,13},{1... | collective-permute-start | bytes 258056 | tf_op jit(solution)/shard_map/ppermute | solution.py:376
  43.8 1.2 %collective-permute-done.6 = f32[168,128]{1,0:T(8,128)S(1)} collective-permute-done((f32[168,128]{1,0:T(8,128)S(1)}, f32[168,128]{1,0:T(8,128)S(1)}, u32[]{:S(2)}, u32[]{:S(2)}) %collective-permute-start.6) | collective-permute-done | bytes 86048 | tf_op jit(solution)/shard_map/ppermute | solution.py:376
  45.0 5.1 %collective-permute-done.5 = f32[168,128]{1,0:T(8,128)S(1)} collective-permute-done((f32[168,128]{1,0:T(8,128)S(1)}, f32[168,128]{1,0:T(8,128)S(1)}, u32[]{:S(2)}, u32[]{:S(2)}) %collective-permute-start.5) | collective-permute-done | bytes 86048 | tf_op jit(solution)/shard_map/ppermute | solution.py:376
  50.2 1.4 %collective-permute-start.7 = (f32[4,16,256]{2,1,0:T(8,128)S(1)}, f32[4,16,256]{2,1,0:T(8,128)S(1)}, u32[]{:S(2)}, u32[]{:S(2)}) collective-permute-start(f32[4,16,256]{2,1,0:T(8,128)S(1)} %get-tuple-element.47), channel_id=1, source_target_pairs={{0,12},{1,13},{2,14},{3,15},{4,0},{5,1},{6,2},{7,3},{8,4},{9,5},{1... | collective-permute-start | bytes 196616 | tf_op jit(solution)/shard_map/ppermute | solution.py:376
  51.6 0.9 %collective-permute-start.8 = (f32[4,16,256]{2,1,0:T(8,128)S(1)}, f32[4,16,256]{2,1,0:T(8,128)S(1)}, u32[]{:S(2)}, u32[]{:S(2)}) collective-permute-start(f32[4,16,256]{2,1,0:T(8,128)S(1)} %get-tuple-element.47), channel_id=1, source_target_pairs={{0,8},{1,9},{2,10},{3,11},{4,12},{5,13},{6,14},{7,15},{8,0},{9,1},... | collective-permute-start | bytes 196616 | tf_op jit(solution)/shard_map/ppermute | solution.py:376
  52.5 1.9 %collective-permute-start.9 = (f32[4,16,256]{2,1,0:T(8,128)S(1)}, f32[4,16,256]{2,1,0:T(8,128)S(1)}, u32[]{:S(2)}, u32[]{:S(2)}) collective-permute-start(f32[4,16,256]{2,1,0:T(8,128)S(1)} %get-tuple-element.47), channel_id=1, source_target_pairs={{0,4},{1,5},{2,6},{3,7},{4,8},{5,9},{6,10},{7,11},{8,12},{9,13},{1... | collective-permute-start | bytes 196616 | tf_op jit(solution)/shard_map/ppermute | solution.py:376
  54.5 4.5 %collective-permute-done.8 = f32[4,16,256]{2,1,0:T(8,128)S(1)} collective-permute-done((f32[4,16,256]{2,1,0:T(8,128)S(1)}, f32[4,16,256]{2,1,0:T(8,128)S(1)}, u32[]{:S(2)}, u32[]{:S(2)}) %collective-permute-start.8) | collective-permute-done | bytes 65568 | tf_op jit(solution)/shard_map/ppermute | solution.py:376
  59.1 1.6 %collective-permute-start.12 = (f32[4,4,16,256]{3,2,1,0:T(8,128)S(1)}, f32[4,4,16,256]{3,2,1,0:T(8,128)S(1)}, u32[]{:S(2)}, u32[]{:S(2)}) collective-permute-start(f32[4,4,16,256]{3,2,1,0:T(8,128)S(1)} %pad_maximum_fusion.refs_0_), channel_id=1, source_target_pairs={{0,2},{1,3},{2,0},{3,1},{4,6},{5,7},{6,4},{7,5},{8,10},{9,11},{10,... | collective-permute-start | bytes 786440 | tf_op jit(solution)/shard_map/ppermute | solution.py:371
  60.7 1.6 %place.3 = (f32[4,16,16,256]{3,2,1,0:T(8,128)}, f32[1]{0:T(128)}) custom-call(s32[1]{0:T(128)} %bitcast.me_ref, f32[4,4,16,256]{3,2,1,0:T(8,128)S(1)} %pad_maximum_fusion.refs_0_, f32[4,4,16,256]{3,2,1,0:T(8,128)S(1)} %collective-permute-done.10.refs_1_, f32[4,8,128]{2,1,0:T(8,128)S(1)} %pad_maximum_fusion.2.refs_2_), custom_call_target="tpu_custom_call" | custom-call | tf_op jit(solution)/shard_map/place/pallas_call | solution.py:354
  62.5 5.4 %collective-permute-done.12.refs_0_ = f32[4,4,16,256]{3,2,1,0:T(8,128)S(1)} collective-permute-done((f32[4,4,16,256]{3,2,1,0:T(8,128)S(1)}, f32[4,4,16,256]{3,2,1,0:T(8,128)S(1)}, u32[]{:S(2)}, u32[]{:S(2)}) %collective-permute-start.12) | collective-permute-done | bytes 262176 | tf_op jit(solution)/shard_map/ppermute | solution.py:371
  67.9 0.8 %place.4.refs_1_ = f32[4,16,16,256]{3,2,1,0:T(8,128)} custom-call(s32[1]{0:T(128)} %bitcast.me_ref, f32[4,4,16,256]{3,2,1,0:T(8,128)S(1)} %collective-permute-done.12.refs_0_, f32[4,16,16,256]{3,2,1,0:T(8,128)} %get-tuple-element.41.refs_1_), custom_call_target="tpu_custom_call", output_to_operand_aliasing={{}: (2, {})} | custom-call | tf_op jit(solution)/shard_map/place/pallas_call | solution.py:354
  68.6 0.8 %collective-permute-done.13.refs_0_ = f32[4,4,16,256]{3,2,1,0:T(8,128)S(1)} collective-permute-done((f32[4,4,16,256]{3,2,1,0:T(8,128)S(1)}, f32[4,4,16,256]{3,2,1,0:T(8,128)S(1)}, u32[]{:S(2)}, u32[]{:S(2)}) %collective-permute-start.13) | collective-permute-done | bytes 262176 | tf_op jit(solution)/shard_map/ppermute | solution.py:371
  69.4 0.8 %place.5 = f32[4,16,16,256]{3,2,1,0:T(8,128)} custom-call(s32[1]{0:T(128)} %bitcast.me_ref, f32[4,4,16,256]{3,2,1,0:T(8,128)S(1)} %collective-permute-done.13.refs_0_, f32[4,16,16,256]{3,2,1,0:T(8,128)} %place.4.refs_1_), custom_call_target="tpu_custom_call", output_to_operand_aliasing={{}: (2, {})} | custom-call | tf_op jit(solution)/shard_map/place/pallas_call | solution.py:354
  (46 shorter events, 1.6 us)
Async XLA Ops:
  0.6 2.6 %copy-start.6 = (s32[8,2]{0,1:T(2,128)S(1)}, s32[8,2]{0,1:T(2,128)}, u32[]{:S(2)}) copy-start(s32[8,2]{0,1:T(2,128)} %param.10) | copy-start | bytes 196
  0.6 2.9 %copy-start.2 = (f32[2,2,256,256]{3,2,1,0:T(8,128)S(1)}, f32[2,2,256,256]{3,2,1,0:T(8,128)}, u32[]{:S(2)}) copy-start(f32[2,2,256,256]{3,2,1,0:T(8,128)} %refs_1_.3) | copy-start | bytes 3145732
  1.9 11.4 %collective-permute-start = (f32[2,256,384]{2,1,0:T(8,128)S(1)}, f32[2,256,384]{2,1,0:T(8,128)S(1)}, u32[]{:S(2)}, u32[]{:S(2)}) collective-permute-start(f32[2,256,384]{2,1,0:T(8,128)S(1)} %slice.84), channel_id=1, source_target_pairs={{1,0},{2,1},{3,2},{4,3},{5,4},{6,5},{7,6},{8,7},{9,8},{10,9},{11,1... | collective-permute-start | bytes 2359304 | tf_op jit(solution)/shard_map/ppermute | solution.py:393
  3.5 1.1 %copy-start.3 = (bf16[6,256,256]{2,1,0:T(8,128)(2,1)S(1)}, bf16[6,256,256]{2,1,0:T(8,128)(2,1)}, u32[]{:S(2)}) copy-start(bf16[6,256,256]{2,1,0:T(8,128)(2,1)} %constant.51.clone.refs_3_) | copy-start | bytes 2359300
  4.6 8.7 %copy-start = (f32[2,512,384]{2,1,0:T(8,128)S(1)}, f32[2,512,384]{2,1,0:T(8,128)}, u32[]{:S(2)}) copy-start(f32[2,512,384]{2,1,0:T(8,128)} %refs_0_.3) | copy-start | bytes 4718596
  4.6 8.7 %copy-start.1 = (f32[8,256,256]{2,1,0:T(8,128)S(1)}, f32[8,256,256]{2,1,0:T(8,128)}, u32[]{:S(2)}) copy-start(f32[8,256,256]{2,1,0:T(8,128)} %refs_2_.3) | copy-start | bytes 6291460
  21.9 5.1 %collective-permute-start.2 = (f32[8,168,128]{2,1,0:T(8,128)S(1)}, f32[8,168,128]{2,1,0:T(8,128)S(1)}, u32[]{:S(2)}, u32[]{:S(2)}) collective-permute-start(f32[8,168,128]{2,1,0:T(8,128)S(1)} %get-tuple-element.34), channel_id=1, source_target_pairs={{0,1},{1,0},{2,3},{3,2},{4,5},{5,4},{6,7},{7,6},{8,9},{9,8},{10,11... | collective-permute-start | bytes 2064392 | tf_op jit(solution)/shard_map/ppermute | solution.py:371
  25.1 13.2 %collective-permute-start.1 = (f32[2,256,384]{2,1,0:T(8,128)S(1)}, f32[2,256,384]{2,1,0:T(8,128)S(1)}, u32[]{:S(2)}, u32[]{:S(2)}) collective-permute-start(f32[2,256,384]{2,1,0:T(8,128)S(1)} %get-tuple-element.32), channel_id=1, source_target_pairs={{3,7},{7,11},{11,15},{19,23},{23,27},{27,31}} | collective-permute-start | bytes 2359304 | tf_op jit(solution)/shard_map/ppermute | solution.py:399
  27.7 10.6 %collective-permute-start.3 = (f32[4,168,128]{2,1,0:T(8,128)}, f32[4,168,128]{2,1,0:T(8,128)S(1)}, u32[]{:S(2)}, u32[]{:S(2)}) collective-permute-start(f32[4,168,128]{2,1,0:T(8,128)} %slice_add_fusion), channel_id=1, source_target_pairs={{0,2},{1,3},{2,0},{3,1},{4,6},{5,7},{6,4},{7,5},{8,10},{9,11},{10,... | collective-permute-start | bytes 1032200 | tf_op jit(solution)/shard_map/ppermute | solution.py:371
  38.4 6.5 %collective-permute-start.6 = (f32[168,128]{1,0:T(8,128)S(1)}, f32[168,128]{1,0:T(8,128)S(1)}, u32[]{:S(2)}, u32[]{:S(2)}) collective-permute-start(f32[168,128]{1,0:T(8,128)S(1)} %get-tuple-element.43), channel_id=1, source_target_pairs={{0,12},{1,13},{2,14},{3,15},{4,0},{5,1},{6,2},{7,3},{8,4},{9,5},{1... | collective-permute-start | bytes 258056 | tf_op jit(solution)/shard_map/ppermute | solution.py:376
  41.9 8.2 %collective-permute-start.5 = (f32[168,128]{1,0:T(8,128)S(1)}, f32[168,128]{1,0:T(8,128)S(1)}, u32[]{:S(2)}, u32[]{:S(2)}) collective-permute-start(f32[168,128]{1,0:T(8,128)S(1)} %get-tuple-element.44), channel_id=1, source_target_pairs={{0,8},{1,9},{2,10},{3,11},{4,12},{5,13},{6,14},{7,15},{8,0},{9,1},... | collective-permute-start | bytes 258056 | tf_op jit(solution)/shard_map/ppermute | solution.py:376
  41.9 8.2 %collective-permute-start.4 = (f32[168,128]{1,0:T(8,128)S(1)}, f32[168,128]{1,0:T(8,128)S(1)}, u32[]{:S(2)}, u32[]{:S(2)}) collective-permute-start(f32[168,128]{1,0:T(8,128)S(1)} %get-tuple-element.45), channel_id=1, source_target_pairs={{0,4},{1,5},{2,6},{3,7},{4,8},{5,9},{6,10},{7,11},{8,12},{9,13},{1... | collective-permute-start | bytes 258056 | tf_op jit(solution)/shard_map/ppermute | solution.py:376
  43.7 18.6 %copy-start.4 = (f32[2,512,384]{2,1,0:T(8,128)S(1)}, f32[2,512,384]{2,1,0:T(8,128)}, u32[]{:S(2)}) copy-start(f32[2,512,384]{2,1,0:T(8,128)} %get-tuple-element.37) | copy-start | bytes 4718596
  43.7 18.6 %collective-permute-start.11 = (f32[2,256,384]{2,1,0:T(8,128)S(1)}, f32[2,256,384]{2,1,0:T(8,128)S(1)}, u32[]{:S(2)}, u32[]{:S(2)}) collective-permute-start(f32[2,256,384]{2,1,0:T(8,128)S(1)} %broadcast_select_fusion), channel_id=1, source_target_pairs={{0,1},{1,2},{2,3},{3,0},{4,5},{5,6},{6,7},{7,4},{8,9},{9,10},{10,1... | collective-permute-start | bytes 2359304 | tf_op jit(solution)/shard_map/ppermute | solution.py:407
  50.2 4.3 %collective-permute-start.7 = (f32[4,16,256]{2,1,0:T(8,128)S(1)}, f32[4,16,256]{2,1,0:T(8,128)S(1)}, u32[]{:S(2)}, u32[]{:S(2)}) collective-permute-start(f32[4,16,256]{2,1,0:T(8,128)S(1)} %get-tuple-element.47), channel_id=1, source_target_pairs={{0,12},{1,13},{2,14},{3,15},{4,0},{5,1},{6,2},{7,3},{8,4},{9,5},{1... | collective-permute-start | bytes 196616 | tf_op jit(solution)/shard_map/ppermute | solution.py:376
  51.6 7.4 %collective-permute-start.8 = (f32[4,16,256]{2,1,0:T(8,128)S(1)}, f32[4,16,256]{2,1,0:T(8,128)S(1)}, u32[]{:S(2)}, u32[]{:S(2)}) collective-permute-start(f32[4,16,256]{2,1,0:T(8,128)S(1)} %get-tuple-element.47), channel_id=1, source_target_pairs={{0,8},{1,9},{2,10},{3,11},{4,12},{5,13},{6,14},{7,15},{8,0},{9,1},... | collective-permute-start | bytes 196616 | tf_op jit(solution)/shard_map/ppermute | solution.py:376
  52.5 6.5 %collective-permute-start.9 = (f32[4,16,256]{2,1,0:T(8,128)S(1)}, f32[4,16,256]{2,1,0:T(8,128)S(1)}, u32[]{:S(2)}, u32[]{:S(2)}) collective-permute-start(f32[4,16,256]{2,1,0:T(8,128)S(1)} %get-tuple-element.47), channel_id=1, source_target_pairs={{0,4},{1,5},{2,6},{3,7},{4,8},{5,9},{6,10},{7,11},{8,12},{9,13},{1... | collective-permute-start | bytes 196616 | tf_op jit(solution)/shard_map/ppermute | solution.py:376
  59.0 1.7 %collective-permute-start.10 = (f32[4,4,16,256]{3,2,1,0:T(8,128)S(1)}, f32[4,4,16,256]{3,2,1,0:T(8,128)S(1)}, u32[]{:S(2)}, u32[]{:S(2)}) collective-permute-start(f32[4,4,16,256]{3,2,1,0:T(8,128)S(1)} %pad_maximum_fusion.refs_0_), channel_id=1, source_target_pairs={{0,1},{1,0},{2,3},{3,2},{4,5},{5,4},{6,7},{7,6},{8,9},{9,8},{10,11... | collective-permute-start | bytes 786440 | tf_op jit(solution)/shard_map/ppermute | solution.py:371
  59.1 8.7 %collective-permute-start.12 = (f32[4,4,16,256]{3,2,1,0:T(8,128)S(1)}, f32[4,4,16,256]{3,2,1,0:T(8,128)S(1)}, u32[]{:S(2)}, u32[]{:S(2)}) collective-permute-start(f32[4,4,16,256]{3,2,1,0:T(8,128)S(1)} %pad_maximum_fusion.refs_0_), channel_id=1, source_target_pairs={{0,2},{1,3},{2,0},{3,1},{4,6},{5,7},{6,4},{7,5},{8,10},{9,11},{10,... | collective-permute-start | bytes 786440 | tf_op jit(solution)/shard_map/ppermute | solution.py:371
  62.5 7.7 %copy-start.5 = (f32[2,512,384]{2,1,0:T(8,128)}, f32[2,512,384]{2,1,0:T(8,128)S(1)}, u32[]{:S(2)}) copy-start(f32[2,512,384]{2,1,0:T(8,128)S(1)} %add_dynamic-update-slice_fusion) | copy-start | bytes 4718596
  67.9 1.5 %collective-permute-start.13 = (f32[4,4,16,256]{3,2,1,0:T(8,128)S(1)}, f32[4,4,16,256]{3,2,1,0:T(8,128)S(1)}, u32[]{:S(2)}, u32[]{:S(2)}) collective-permute-start(f32[4,4,16,256]{3,2,1,0:T(8,128)S(1)} %collective-permute-done.12.refs_0_), channel_id=1, source_target_pairs={{0,1},{1,0},{2,3},{3,2},{4,5},{5,4},{6,7},{7,6},{8,9},{9,8},{10,11... | collective-permute-start | bytes 786440 | tf_op jit(solution)/shard_map/ppermute | solution.py:371

commit v5 on v4

--- a/solution.py
+++ b/solution.py
@@ -400,26 +400,29 @@
     rows = n // size
     quarter = size // 4
     away = swap(away, 1)
-    beside = swap(keep[quarter:] + away[quarter:], 2)
-    x = keep[:quarter] + away[:quarter] + beside
+    beside = swap(keep[quarter + 1 :] + away[quarter + 1 :], 2)
+    x = keep[1:quarter] + away[1:quarter] + beside
     hop, x = lax.optimization_barrier((hop, x))
+    own = keep[0] + away[0] + swap(keep[quarter] + away[quarter], 2)
     carried = jnp.where(me % 4 == 3, hop, low)
     carried = lax.ppermute(carried, "row", [(i, i - 3 if i % 4 == 3 else i + 1) for i in range(size)])
-    parts = [x[0]] + [shift(x[z], 4 * z) for z in range(1, quarter)]
+    parts = [own] + [shift(x[z - 1], 4 * z) for z in range(1, quarter)]
     total = tree(parts)
     losses = jnp.stack([p[10 * rows :] for p in parts])
     planes = total[: 10 * rows].reshape(5, 2, rows, n // 2)
     y = planes[:4] / jnp.sqrt(planes[4] + 1.0)
     y = jnp.concatenate([y[:, 0], y[:, 1]], -1)
-    y = jnp.stack([y] + [shift(y, -4 * z) for z in range(1, quarter)])
+    others = jnp.stack([shift(y, -4 * z) for z in range(1, quarter)])
+    first = swap(y, 2)
+    y = jnp.concatenate([y[None], others])
     sibling = swap(y, 1)
-    beside = swap(y, 2)
-    probe_dir, loss = place(me, (0, 1), (y, sibling), losses, 1.0 / (count * size * n * n))
+    beside = jnp.concatenate([first[None], swap(others, 2)])
+    probe_dir, loss = place(me, (0,), (y,), losses, 1.0 / (count * size * n * n))
     object_grad = grad.at[:, :n].add(carried)
     probe_dir, object_grad, beside = lax.optimization_barrier((probe_dir, object_grad, beside))
-    sibling = swap(beside, 1)
-    (probe_dir,) = place(me, (2,), (beside,), base=probe_dir)
-    (probe_dir,) = place(me, (3,), (sibling,), base=probe_dir)
+    farther = swap(beside, 1)
+    (probe_dir,) = place(me, (1, 2), (sibling, beside), base=probe_dir)
+    (probe_dir,) = place(me, (3,), (farther,), base=probe_dir)
     probe_dir = probe_dir.reshape(2, 2, n, n)
     return (object_grad, probe_dir, loss)
 

time: 70.3 us -> 67.3 us (0.957)
  waiting for transfers between devices: 26.4 us -> 20.1 us
  starting transfers between devices: 18.7 us -> 22.4 us
    ppermute x5 -> x7, waiting for transfers between devices: 15.5 us -> 10.9 us  [swap(): return lax.ppermute(x, 'row', [(i, i ^ bit) for i in range(size)])]
    ppermute x5 -> x7, starting transfers between devices: 7.26 us -> 9.83 us  [swap(): return lax.ppermute(x, 'row', [(i, i ^ bit) for i in range(size)])]
    ppermute x6, waiting for transfers between devices: 10.9 us -> 9.22 us  [shift(): return lax.ppermute(x, 'row', [(i, (i + by) % size) for i in range(size)])]
    ppermute x6, starting transfers between devices: 9.41 us -> 10.5 us  [shift(): return lax.ppermute(x, 'row', [(i, (i + by) % size) for i in range(size)])]
    add x2 -> x3, other arithmetic: 0.82 us -> 0.08 us  [the longest x1 0.04 us: per_device(): x = keep[1:quarter] + away[1:quarter] + beside]
  transfers between devices with their start and end apart: 14 -> 16, of which waited for: 8 -> 7; matrix products, arithmetic and copies ran while one was open for 2% -> 1% of each run, Pallas kernels for 16% -> 17%
where the time goes in v5:
time: 67.3 us; the launch traced here: 67 us
  starting transfers between devices  22.4 us (33%)
  Pallas kernels  20.4 us (30%)
  waiting for transfers between devices  20.1 us (30%)
  local copies, waits for them, and re-layouts  2.56 us (4%)
  between operations  0.95 us (1%)
    pallas_call x2, Pallas kernels, windows(): pl.pallas_call(functools.partial(windows_kernel, first, amp_first), grid_...  17.1 us
    ppermute x7, waiting for transfers between devices, swap(): return lax.ppermute(x, 'row', [(i, i ^ bit) for i in range(size)])  10.9 us
    ppermute x6, starting transfers between devices, shift(): return lax.ppermute(x, 'row', [(i, (i + by) % size) for i in range(size)])  10.5 us
    ppermute x7, starting transfers between devices, swap(): return lax.ppermute(x, 'row', [(i, i ^ bit) for i in range(size)])  9.83 us
    ppermute x6, waiting for transfers between devices, shift(): return lax.ppermute(x, 'row', [(i, (i + by) % size) for i in range(size)])  9.22 us
    pallas_call x3, Pallas kernels, place(): pl.pallas_call(functools.partial(place_kernel, nears, scale), in_specs=in...  3.26 us
  transfers between devices with their start and end apart: 16, of which 7 were waited for; matrix products, arithmetic and copies ran while one was open for 1% of the time, Pallas kernels for 17%

profile of v5, /device:TPU:0, one launch (start us, length us, event | category | flops | bytes accessed | tf_op | source)
XLA Modules:
  0.0 67.0 jit_solution(10773618131532896720)
XLA Ops:
  0.7 1.3 %slice.91 = f32[2,256,384]{2,1,0:T(8,128)S(1)} slice(f32[2,512,384]{2,1,0:T(8,128)} %refs_0_.3), slice={[0:2], [0:256], [0:384]} | slice | bytes 1572864 | tf_op jit(solution)/shard_map/slice | solution.py:393
  1.9 1.3 %collective-permute-start = (f32[2,256,384]{2,1,0:T(8,128)S(1)}, f32[2,256,384]{2,1,0:T(8,128)S(1)}, u32[]{:S(2)}, u32[]{:S(2)}) collective-permute-start(f32[2,256,384]{2,1,0:T(8,128)S(1)} %slice.91), channel_id=1, source_target_pairs={{1,0},{2,1},{3,2},{4,3},{5,4},{6,5},{7,6},{8,7},{9,8},{10,9},{11,1... | collective-permute-start | bytes 2359304 | tf_op jit(solution)/shard_map/ppermute | solution.py:393
  3.5 1.1 %copy-done.3 = bf16[6,256,256]{2,1,0:T(8,128)(2,1)S(1)} copy-done((bf16[6,256,256]{2,1,0:T(8,128)(2,1)S(1)}, bf16[6,256,256]{2,1,0:T(8,128)(2,1)}, u32[]{:S(2)}) %copy-start.3) | copy-done | bytes 786456
  4.6 8.7 %near.1 = (f32[2,512,384]{2,1,0:T(8,128)S(1)}, f32[5,16,16,256]{3,2,1,0:T(8,128)S(1)}, f32[8,256]{1,0:T(8,128)S(1)}) custom-call(s32[9,2]{1,0:T(8,128)S(1)} %pad_add_fusion.off_ref, f32[2,512,384]{2,1,0:T(8,128)} %refs_0_.3, f32[2,2,256,256]{3,2,1,0:T(8,128)S(1)} %copy-done.2, f32[8,256,256]{2,1,0:T(8,128)} %refs_2_.3, bf16[6,256,256]{2,1,0:T(8,128)(2,1)S(1)} %copy-done.3), custom_call_target="tpu_custom_call" | custom-call | tf_op jit(solution)/shard_map/near/pallas_call | solution.py:299
  13.4 8.4 %across.1 = (f32[2,512,384]{2,1,0:T(8,128)}, f32[2,256,384]{2,1,0:T(8,128)S(1)}, f32[8,168,128]{2,1,0:T(8,128)S(1)}, f32[8,168,128]{2,1,0:T(8,128)S(1)}) custom-call(s32[9,2]{1,0:T(8,128)S(1)} %pad_add_fusion.off_ref, f32[2,512,384]{2,1,0:T(8,128)S(1)} %copy-done, f32[2,2,256,256]{3,2,1,0:T(8,128)S(1)} %copy-done.2, f32[8,256,256]{2,1,0:T(8,128)S(1)} %copy-done.1, ...), custom_call_target="tpu_custom_call" | custom-call | tf_op jit(solution)/shard_map/across/pallas_call | solution.py:299
  21.8 3.4 %collective-permute-start.1 = (f32[8,168,128]{2,1,0:T(8,128)S(1)}, f32[8,168,128]{2,1,0:T(8,128)S(1)}, u32[]{:S(2)}, u32[]{:S(2)}) collective-permute-start(f32[8,168,128]{2,1,0:T(8,128)S(1)} %get-tuple-element.33), channel_id=1, source_target_pairs={{0,1},{1,0},{2,3},{3,2},{4,5},{5,4},{6,7},{7,6},{8,9},{9,8},{10,11... | collective-permute-start | bytes 2064392 | tf_op jit(solution)/shard_map/ppermute | solution.py:371
  25.2 0.7 %collective-permute-start.3 = (f32[2,256,384]{2,1,0:T(8,128)S(1)}, f32[2,256,384]{2,1,0:T(8,128)S(1)}, u32[]{:S(2)}, u32[]{:S(2)}) collective-permute-start(f32[2,256,384]{2,1,0:T(8,128)S(1)} %get-tuple-element.34), channel_id=1, source_target_pairs={{3,7},{7,11},{11,15},{19,23},{23,27},{27,31}} | collective-permute-start | bytes 2359304 | tf_op jit(solution)/shard_map/ppermute | solution.py:399
  25.9 1.1 %collective-permute-done.1 = f32[8,168,128]{2,1,0:T(8,128)S(1)} collective-permute-done((f32[8,168,128]{2,1,0:T(8,128)S(1)}, f32[8,168,128]{2,1,0:T(8,128)S(1)}, u32[]{:S(2)}, u32[]{:S(2)}) %collective-permute-start.1) | collective-permute-done | bytes 688160 | tf_op jit(solution)/shard_map/ppermute | solution.py:371
  27.0 2.2 %collective-permute-start.4 = (f32[3,168,128]{2,1,0:T(8,128)S(1)}, f32[3,168,128]{2,1,0:T(8,128)S(1)}, u32[]{:S(2)}, u32[]{:S(2)}) collective-permute-start(f32[3,168,128]{2,1,0:T(8,128)S(1)} %slice_add_fusion), channel_id=1, source_target_pairs={{0,2},{1,3},{2,0},{3,1},{4,6},{5,7},{6,4},{7,5},{8,10},{9,11},{10,... | collective-permute-start | bytes 774152 | tf_op jit(solution)/shard_map/ppermute | solution.py:371
  29.3 6.0 %collective-permute-done.4 = f32[3,168,128]{2,1,0:T(8,128)S(1)} collective-permute-done((f32[3,168,128]{2,1,0:T(8,128)S(1)}, f32[3,168,128]{2,1,0:T(8,128)S(1)}, u32[]{:S(2)}, u32[]{:S(2)}) %collective-permute-start.4) | collective-permute-done | bytes 258080 | tf_op jit(solution)/shard_map/ppermute | solution.py:371
  35.4 2.1 %collective-permute-start.5 = (f32[168,128]{1,0:T(8,128)S(1)}, f32[168,128]{1,0:T(8,128)S(1)}, u32[]{:S(2)}, u32[]{:S(2)}) collective-permute-start(f32[168,128]{1,0:T(8,128)S(1)} %get-tuple-element.45), channel_id=1, source_target_pairs={{0,4},{1,5},{2,6},{3,7},{4,8},{5,9},{6,10},{7,11},{8,12},{9,13},{1... | collective-permute-start | bytes 258056 | tf_op jit(solution)/shard_map/ppermute | solution.py:376
  37.5 2.9 %collective-permute-start.6 = (f32[168,128]{1,0:T(8,128)S(1)}, f32[168,128]{1,0:T(8,128)S(1)}, u32[]{:S(2)}, u32[]{:S(2)}) collective-permute-start(f32[168,128]{1,0:T(8,128)S(1)} %get-tuple-element.47), channel_id=1, source_target_pairs={{0,8},{1,9},{2,10},{3,11},{4,12},{5,13},{6,14},{7,15},{8,0},{9,1},... | collective-permute-start | bytes 258056 | tf_op jit(solution)/shard_map/ppermute | solution.py:376
  40.4 1.6 %collective-permute-start.7 = (f32[168,128]{1,0:T(8,128)S(1)}, f32[168,128]{1,0:T(8,128)S(1)}, u32[]{:S(2)}, u32[]{:S(2)}) collective-permute-start(f32[168,128]{1,0:T(8,128)S(1)} %get-tuple-element.46), channel_id=1, source_target_pairs={{0,12},{1,13},{2,14},{3,15},{4,0},{5,1},{6,2},{7,3},{8,4},{9,5},{1... | collective-permute-start | bytes 258056 | tf_op jit(solution)/shard_map/ppermute | solution.py:376
  42.2 1.0 %collective-permute-done.5 = f32[168,128]{1,0:T(8,128)S(1)} collective-permute-done((f32[168,128]{1,0:T(8,128)S(1)}, f32[168,128]{1,0:T(8,128)S(1)}, u32[]{:S(2)}, u32[]{:S(2)}) %collective-permute-start.5) | collective-permute-done | bytes 86048 | tf_op jit(solution)/shard_map/ppermute | solution.py:376
  43.2 3.8 %collective-permute-done.6 = f32[168,128]{1,0:T(8,128)S(1)} collective-permute-done((f32[168,128]{1,0:T(8,128)S(1)}, f32[168,128]{1,0:T(8,128)S(1)}, u32[]{:S(2)}, u32[]{:S(2)}) %collective-permute-start.6) | collective-permute-done | bytes 86048 | tf_op jit(solution)/shard_map/ppermute | solution.py:376
  47.1 3.1 %collective-permute-start.8 = (f32[4,16,256]{2,1,0:T(8,128)S(1)}, f32[4,16,256]{2,1,0:T(8,128)S(1)}, u32[]{:S(2)}, u32[]{:S(2)}) collective-permute-start(f32[4,16,256]{2,1,0:T(8,128)S(1)} %get-tuple-element.49), channel_id=1, source_target_pairs={{0,12},{1,13},{2,14},{3,15},{4,0},{5,1},{6,2},{7,3},{8,4},{9,5},{1... | collective-permute-start | bytes 196616 | tf_op jit(solution)/shard_map/ppermute | solution.py:376
  50.2 0.8 %collective-permute-start.9 = (f32[4,16,256]{2,1,0:T(8,128)S(1)}, f32[4,16,256]{2,1,0:T(8,128)S(1)}, u32[]{:S(2)}, u32[]{:S(2)}) collective-permute-start(f32[4,16,256]{2,1,0:T(8,128)S(1)} %get-tuple-element.49), channel_id=1, source_target_pairs={{0,8},{1,9},{2,10},{3,11},{4,12},{5,13},{6,14},{7,15},{8,0},{9,1},... | collective-permute-start | bytes 196616 | tf_op jit(solution)/shard_map/ppermute | solution.py:376
  51.0 2.0 %collective-permute-start.12 = (f32[4,16,256]{2,1,0:T(8,128)S(1)}, f32[4,16,256]{2,1,0:T(8,128)S(1)}, u32[]{:S(2)}, u32[]{:S(2)}) collective-permute-start(f32[4,16,256]{2,1,0:T(8,128)S(1)} %get-tuple-element.49), channel_id=1, source_target_pairs={{0,2},{1,3},{2,0},{3,1},{4,6},{5,7},{6,4},{7,5},{8,10},{9,11},{10,... | collective-permute-start | bytes 196616 | tf_op jit(solution)/shard_map/ppermute | solution.py:371
  53.0 4.5 %collective-permute-done.9 = f32[4,16,256]{2,1,0:T(8,128)S(1)} collective-permute-done((f32[4,16,256]{2,1,0:T(8,128)S(1)}, f32[4,16,256]{2,1,0:T(8,128)S(1)}, u32[]{:S(2)}, u32[]{:S(2)}) %collective-permute-start.9) | collective-permute-done | bytes 65568 | tf_op jit(solution)/shard_map/ppermute | solution.py:376
  57.5 2.0 %collective-permute-start.13 = (f32[3,4,16,256]{3,2,1,0:T(8,128)S(1)}, f32[3,4,16,256]{3,2,1,0:T(8,128)S(1)}, u32[]{:S(2)}, u32[]{:S(2)}) collective-permute-start(f32[3,4,16,256]{3,2,1,0:T(8,128)S(1)} %pad_maximum_fusion.2), channel_id=1, source_target_pairs={{0,2},{1,3},{2,0},{3,1},{4,6},{5,7},{6,4},{7,5},{8,10},{9,11},{10,... | collective-permute-start | bytes 589832 | tf_op jit(solution)/shard_map/ppermute | solution.py:371
  59.6 1.4 %place.3 = (f32[4,16,16,256]{3,2,1,0:T(8,128)}, f32[1]{0:T(128)}) custom-call(s32[1]{0:T(128)} %bitcast.me_ref, f32[4,4,16,256]{3,2,1,0:T(8,128)S(1)} %pad_maximum_fusion.refs_0_, f32[4,8,128]{2,1,0:T(8,128)S(1)} %pad_maximum_fusion.4.refs_1_), custom_call_target="tpu_custom_call" | custom-call | tf_op jit(solution)/shard_map/place/pallas_call | solution.py:354
  61.0 3.4 %collective-permute-done.13 = f32[3,4,16,256]{3,2,1,0:T(8,128)S(1)} collective-permute-done((f32[3,4,16,256]{3,2,1,0:T(8,128)S(1)}, f32[3,4,16,256]{3,2,1,0:T(8,128)S(1)}, u32[]{:S(2)}, u32[]{:S(2)}) %collective-permute-start.13) | collective-permute-done | bytes 196640 | tf_op jit(solution)/shard_map/ppermute | solution.py:371
  64.7 1.1 %place.4.refs_1_ = f32[4,16,16,256]{3,2,1,0:T(8,128)} custom-call(s32[1]{0:T(128)} %bitcast.me_ref, f32[4,4,16,256]{3,2,1,0:T(8,128)S(1)} %collective-permute-done.15.refs_0_, f32[4,4,16,256]{3,2,1,0:T(8,128)S(1)} %pad_maximum_fusion.1.refs_1_, f32[4,16,16,256]{3,2,1,0:T(8,128)} %get-tuple-element.41.refs_2_), custom_call_target="tpu_custom_call", output_to_operand_aliasing={{}: (3, {})} | custom-call | tf_op jit(solution)/shard_map/place/pallas_call | solution.py:354
  66.3 0.8 %place.5 = f32[4,16,16,256]{3,2,1,0:T(8,128)} custom-call(s32[1]{0:T(128)} %bitcast.me_ref, f32[4,4,16,256]{3,2,1,0:T(8,128)S(1)} %collective-permute-done.14.refs_0_, f32[4,16,16,256]{3,2,1,0:T(8,128)} %place.4.refs_1_), custom_call_target="tpu_custom_call", output_to_operand_aliasing={{}: (2, {})} | custom-call | tf_op jit(solution)/shard_map/place/pallas_call | solution.py:354
  (53 shorter events, 1.5 us)
Async XLA Ops:
  0.6 2.6 %copy-start.6 = (s32[8,2]{0,1:T(2,128)S(1)}, s32[8,2]{0,1:T(2,128)}, u32[]{:S(2)}) copy-start(s32[8,2]{0,1:T(2,128)} %param.10) | copy-start | bytes 196
  0.6 2.9 %copy-start.2 = (f32[2,2,256,256]{3,2,1,0:T(8,128)S(1)}, f32[2,2,256,256]{3,2,1,0:T(8,128)}, u32[]{:S(2)}) copy-start(f32[2,2,256,256]{3,2,1,0:T(8,128)} %refs_1_.3) | copy-start | bytes 3145732
  1.9 11.4 %collective-permute-start = (f32[2,256,384]{2,1,0:T(8,128)S(1)}, f32[2,256,384]{2,1,0:T(8,128)S(1)}, u32[]{:S(2)}, u32[]{:S(2)}) collective-permute-start(f32[2,256,384]{2,1,0:T(8,128)S(1)} %slice.91), channel_id=1, source_target_pairs={{1,0},{2,1},{3,2},{4,3},{5,4},{6,5},{7,6},{8,7},{9,8},{10,9},{11,1... | collective-permute-start | bytes 2359304 | tf_op jit(solution)/shard_map/ppermute | solution.py:393
  3.5 1.1 %copy-start.3 = (bf16[6,256,256]{2,1,0:T(8,128)(2,1)S(1)}, bf16[6,256,256]{2,1,0:T(8,128)(2,1)}, u32[]{:S(2)}) copy-start(bf16[6,256,256]{2,1,0:T(8,128)(2,1)} %constant.51.clone.refs_3_) | copy-start | bytes 2359300
  4.6 8.7 %copy-start = (f32[2,512,384]{2,1,0:T(8,128)S(1)}, f32[2,512,384]{2,1,0:T(8,128)}, u32[]{:S(2)}) copy-start(f32[2,512,384]{2,1,0:T(8,128)} %refs_0_.3) | copy-start | bytes 4718596
  4.6 8.7 %copy-start.1 = (f32[8,256,256]{2,1,0:T(8,128)S(1)}, f32[8,256,256]{2,1,0:T(8,128)}, u32[]{:S(2)}) copy-start(f32[8,256,256]{2,1,0:T(8,128)} %refs_2_.3) | copy-start | bytes 6291460
  21.8 5.1 %collective-permute-start.1 = (f32[8,168,128]{2,1,0:T(8,128)S(1)}, f32[8,168,128]{2,1,0:T(8,128)S(1)}, u32[]{:S(2)}, u32[]{:S(2)}) collective-permute-start(f32[8,168,128]{2,1,0:T(8,128)S(1)} %get-tuple-element.33), channel_id=1, source_target_pairs={{0,1},{1,0},{2,3},{3,2},{4,5},{5,4},{6,7},{7,6},{8,9},{9,8},{10,11... | collective-permute-start | bytes 2064392 | tf_op jit(solution)/shard_map/ppermute | solution.py:371
  25.2 10.2 %collective-permute-start.3 = (f32[2,256,384]{2,1,0:T(8,128)S(1)}, f32[2,256,384]{2,1,0:T(8,128)S(1)}, u32[]{:S(2)}, u32[]{:S(2)}) collective-permute-start(f32[2,256,384]{2,1,0:T(8,128)S(1)} %get-tuple-element.34), channel_id=1, source_target_pairs={{3,7},{7,11},{11,15},{19,23},{23,27},{27,31}} | collective-permute-start | bytes 2359304 | tf_op jit(solution)/shard_map/ppermute | solution.py:399
  27.0 8.3 %collective-permute-start.4 = (f32[3,168,128]{2,1,0:T(8,128)S(1)}, f32[3,168,128]{2,1,0:T(8,128)S(1)}, u32[]{:S(2)}, u32[]{:S(2)}) collective-permute-start(f32[3,168,128]{2,1,0:T(8,128)S(1)} %slice_add_fusion), channel_id=1, source_target_pairs={{0,2},{1,3},{2,0},{3,1},{4,6},{5,7},{6,4},{7,5},{8,10},{9,11},{10,... | collective-permute-start | bytes 774152 | tf_op jit(solution)/shard_map/ppermute | solution.py:371
  29.2 12.9 %collective-permute-start.2 = (f32[168,128]{1,0:T(8,128)S(1)}, f32[168,128]{1,0:T(8,128)S(1)}, u32[]{:S(2)}, u32[]{:S(2)}) collective-permute-start(f32[168,128]{1,0:T(8,128)S(1)} %fusion.1), channel_id=1, source_target_pairs={{0,2},{1,3},{2,0},{3,1},{4,6},{5,7},{6,4},{7,5},{8,10},{9,11},{10,... | collective-permute-start | bytes 258056 | tf_op jit(solution)/shard_map/ppermute | solution.py:371
  35.4 7.8 %collective-permute-start.5 = (f32[168,128]{1,0:T(8,128)S(1)}, f32[168,128]{1,0:T(8,128)S(1)}, u32[]{:S(2)}, u32[]{:S(2)}) collective-permute-start(f32[168,128]{1,0:T(8,128)S(1)} %get-tuple-element.45), channel_id=1, source_target_pairs={{0,4},{1,5},{2,6},{3,7},{4,8},{5,9},{6,10},{7,11},{8,12},{9,13},{1... | collective-permute-start | bytes 258056 | tf_op jit(solution)/shard_map/ppermute | solution.py:376
  37.5 9.4 %collective-permute-start.6 = (f32[168,128]{1,0:T(8,128)S(1)}, f32[168,128]{1,0:T(8,128)S(1)}, u32[]{:S(2)}, u32[]{:S(2)}) collective-permute-start(f32[168,128]{1,0:T(8,128)S(1)} %get-tuple-element.47), channel_id=1, source_target_pairs={{0,8},{1,9},{2,10},{3,11},{4,12},{5,13},{6,14},{7,15},{8,0},{9,1},... | collective-permute-start | bytes 258056 | tf_op jit(solution)/shard_map/ppermute | solution.py:376
  40.4 6.5 %collective-permute-start.7 = (f32[168,128]{1,0:T(8,128)S(1)}, f32[168,128]{1,0:T(8,128)S(1)}, u32[]{:S(2)}, u32[]{:S(2)}) collective-permute-start(f32[168,128]{1,0:T(8,128)S(1)} %get-tuple-element.46), channel_id=1, source_target_pairs={{0,12},{1,13},{2,14},{3,15},{4,0},{5,1},{6,2},{7,3},{8,4},{9,5},{1... | collective-permute-start | bytes 258056 | tf_op jit(solution)/shard_map/ppermute | solution.py:376
  42.1 22.4 %copy-start.4 = (f32[2,512,384]{2,1,0:T(8,128)S(1)}, f32[2,512,384]{2,1,0:T(8,128)}, u32[]{:S(2)}) copy-start(f32[2,512,384]{2,1,0:T(8,128)} %get-tuple-element.37) | copy-start | bytes 4718596
  42.1 22.3 %collective-permute-start.11 = (f32[2,256,384]{2,1,0:T(8,128)S(1)}, f32[2,256,384]{2,1,0:T(8,128)S(1)}, u32[]{:S(2)}, u32[]{:S(2)}) collective-permute-start(f32[2,256,384]{2,1,0:T(8,128)S(1)} %broadcast_select_fusion), channel_id=1, source_target_pairs={{0,1},{1,2},{2,3},{3,0},{4,5},{5,6},{6,7},{7,4},{8,9},{9,10},{10,1... | collective-permute-start | bytes 2359304 | tf_op jit(solution)/shard_map/ppermute | solution.py:408
  47.1 5.9 %collective-permute-start.8 = (f32[4,16,256]{2,1,0:T(8,128)S(1)}, f32[4,16,256]{2,1,0:T(8,128)S(1)}, u32[]{:S(2)}, u32[]{:S(2)}) collective-permute-start(f32[4,16,256]{2,1,0:T(8,128)S(1)} %get-tuple-element.49), channel_id=1, source_target_pairs={{0,12},{1,13},{2,14},{3,15},{4,0},{5,1},{6,2},{7,3},{8,4},{9,5},{1... | collective-permute-start | bytes 196616 | tf_op jit(solution)/shard_map/ppermute | solution.py:376
  50.2 7.3 %collective-permute-start.9 = (f32[4,16,256]{2,1,0:T(8,128)S(1)}, f32[4,16,256]{2,1,0:T(8,128)S(1)}, u32[]{:S(2)}, u32[]{:S(2)}) collective-permute-start(f32[4,16,256]{2,1,0:T(8,128)S(1)} %get-tuple-element.49), channel_id=1, source_target_pairs={{0,8},{1,9},{2,10},{3,11},{4,12},{5,13},{6,14},{7,15},{8,0},{9,1},... | collective-permute-start | bytes 196616 | tf_op jit(solution)/shard_map/ppermute | solution.py:376
  51.0 6.5 %collective-permute-start.10 = (f32[4,16,256]{2,1,0:T(8,128)S(1)}, f32[4,16,256]{2,1,0:T(8,128)S(1)}, u32[]{:S(2)}, u32[]{:S(2)}) collective-permute-start(f32[4,16,256]{2,1,0:T(8,128)S(1)} %get-tuple-element.49), channel_id=1, source_target_pairs={{0,4},{1,5},{2,6},{3,7},{4,8},{5,9},{6,10},{7,11},{8,12},{9,13},{1... | collective-permute-start | bytes 196616 | tf_op jit(solution)/shard_map/ppermute | solution.py:376
  51.0 10.0 %collective-permute-start.12 = (f32[4,16,256]{2,1,0:T(8,128)S(1)}, f32[4,16,256]{2,1,0:T(8,128)S(1)}, u32[]{:S(2)}, u32[]{:S(2)}) collective-permute-start(f32[4,16,256]{2,1,0:T(8,128)S(1)} %get-tuple-element.49), channel_id=1, source_target_pairs={{0,2},{1,3},{2,0},{3,1},{4,6},{5,7},{6,4},{7,5},{8,10},{9,11},{10,... | collective-permute-start | bytes 196616 | tf_op jit(solution)/shard_map/ppermute | solution.py:371
  57.5 7.0 %collective-permute-start.13 = (f32[3,4,16,256]{3,2,1,0:T(8,128)S(1)}, f32[3,4,16,256]{3,2,1,0:T(8,128)S(1)}, u32[]{:S(2)}, u32[]{:S(2)}) collective-permute-start(f32[3,4,16,256]{3,2,1,0:T(8,128)S(1)} %pad_maximum_fusion.2), channel_id=1, source_target_pairs={{0,2},{1,3},{2,0},{3,1},{4,6},{5,7},{6,4},{7,5},{8,10},{9,11},{10,... | collective-permute-start | bytes 589832 | tf_op jit(solution)/shard_map/ppermute | solution.py:371
  59.5 5.2 %collective-permute-start.15 = (f32[4,4,16,256]{3,2,1,0:T(8,128)S(1)}, f32[4,4,16,256]{3,2,1,0:T(8,128)S(1)}, u32[]{:S(2)}, u32[]{:S(2)}) collective-permute-start(f32[4,4,16,256]{3,2,1,0:T(8,128)S(1)} %pad_maximum_fusion.refs_0_), channel_id=1, source_target_pairs={{0,1},{1,0},{2,3},{3,2},{4,5},{5,4},{6,7},{7,6},{8,9},{9,8},{10,11... | collective-permute-start | bytes 786440 | tf_op jit(solution)/shard_map/ppermute | solution.py:371
  64.6 2.4 %copy-start.5 = (f32[2,512,384]{2,1,0:T(8,128)}, f32[2,512,384]{2,1,0:T(8,128)S(1)}, u32[]{:S(2)}) copy-start(f32[2,512,384]{2,1,0:T(8,128)S(1)} %add_dynamic-update-slice_fusion) | copy-start | bytes 4718596
  64.6 1.6 %collective-permute-start.14 = (f32[4,4,16,256]{3,2,1,0:T(8,128)S(1)}, f32[4,4,16,256]{3,2,1,0:T(8,128)S(1)}, u32[]{:S(2)}, u32[]{:S(2)}) collective-permute-start(f32[4,4,16,256]{3,2,1,0:T(8,128)S(1)} %pad_maximum_fusion.1.refs_1_), channel_id=1, source_target_pairs={{0,1},{1,0},{2,3},{3,2},{4,5},{5,4},{6,7},{7,6},{8,9},{9,8},{10,11... | collective-permute-start | bytes 786440 | tf_op jit(solution)/shard_map/ppermute | solution.py:371

commit v6 on v5

--- a/solution.py
+++ b/solution.py
@@ -38,7 +38,7 @@
     return np.stack(tables + [tables[1].T, tables[3].T]).astype(ml_dtypes.bfloat16)
 
 
-def windows_kernel(first, amp_first, off_ref, *refs):
+def windows_kernel(first, amp_first, group_size, off_ref, *refs):
     object_ref, probe_hbm, amp_hbm, tab_hbm = refs[:4]
     if first:
         grad_out, pg_out, loss_out = refs[4:7]
@@ -55,10 +55,10 @@
     sub = lax.broadcasted_iota(jnp.int32, (1, 8, 1), 1)
 
     def amplitude_copies(group):
-        at = amp_first + group * GROUP
+        at = amp_first + group * group_size
         return [
             pltpu.make_async_copy(
-                amp_hbm.at[pl.ds(at, GROUP), :, pl.ds(q * LANES, LANES)], amp_s.at[group, q], sems.at[8 + 2 * group + q]
+                amp_hbm.at[pl.ds(at, group_size), :, pl.ds(q * LANES, LANES)], amp_s.at[group, q], sems.at[8 + 2 * group + q]
             )
             for q in range(2)
         ]
@@ -76,7 +76,7 @@
 
     @pl.when(k == 0)
     def _():
-        for copy in (*windows_in, table_in, *amplitude_copies(0), *amplitude_copies(1), *sums_in):
+        for copy in (*windows_in, table_in, *[c for i in range(amp_s.shape[0]) for c in amplitude_copies(i)], *sums_in):
             copy.start()
         if first:
             grad[...] = jnp.zeros_like(grad)
@@ -94,8 +94,8 @@
         return jnp.dot(a, b, preferred_element_type=F32)
 
     places = []
-    for g in range(GROUP):
-        r, c = off_ref[amp_first + k * GROUP + g, 0] - below_row, off_ref[amp_first + k * GROUP + g, 1]
+    for g in range(group_size):
+        r, c = off_ref[amp_first + k * group_size + g, 0] - below_row, off_ref[amp_first + k * group_size + g, 1]
         fine = lax.rem(r, 8)
         places.append((pl.multiple_of(r - fine, 8), fine, c))
 
@@ -189,7 +189,7 @@
             js = slice(j * h, (j + 1) * h)
             for m in range(2):
                 s_re = s_im = None
-                for g in range(GROUP):
+                for g in range(group_size):
                     g_re, g_im = far_s[g, j, :, m * n : m * n + h], far_s[g, j, :, m * n + h : (m + 1) * n]
                     o_re, o_im = win_s[g, 0, :, js], win_s[g, 1, :, js]
                     a, b = o_re * g_re + o_im * g_im, o_re * g_im - o_im * g_re
@@ -197,7 +197,7 @@
                 pg_ref[2 * m, :, :, js] += s_re.reshape(shards, rows, h)
                 pg_ref[2 * m + 1, :, :, js] += s_im.reshape(shards, rows, h)
             s = None
-            for g in range(GROUP):
+            for g in range(group_size):
                 o_re, o_im = win_s[g, 0, :, js], win_s[g, 1, :, js]
                 v = o_re * o_re + o_im * o_im
                 s = v if s is None else s + v
@@ -228,10 +228,10 @@
                 grad[d, pl.ds(base + below_row, n + 8), LANES * q : LANES * (q + 1)] += out[q].reshape(n + 8, LANES)
 
     for stage in (load, wave, columns, down, weigh, up, columns_back):
-        for g in range(GROUP):
+        for g in range(group_size):
             stage(g)
     sums()
-    for g in range(GROUP):
+    for g in range(group_size):
         scatter(g)
 
     @pl.when(k == pl.num_programs(0) - 1)
@@ -272,6 +272,7 @@
 def windows(first, shards, count, offs, object_field, probe, amplitude, amp_first, table, carried=()):
     n = probe.shape[-1]
     width = object_field.shape[2]
+    group_size = GROUP if first else count
     sums = (5, shards, n // shards, n)
     hbm, anywhere = pl.BlockSpec(memory_space=pltpu.HBM), pl.BlockSpec(memory_space=pl.ANY)
     inputs = (object_field, probe, amplitude, table, *carried)
@@ -289,24 +290,24 @@
         pltpu.VMEM((8, n), F32),
         pltpu.VMEM(probe.shape, F32),
         pltpu.VMEM(table.shape, BF16),
-        pltpu.VMEM((count // GROUP, 2, GROUP, n, LANES), F32),
-        pltpu.VMEM((GROUP, 2, n, n), F32),
-        pltpu.VMEM((GROUP, 2, 2 * n, n), BF16),
-        pltpu.VMEM((GROUP, 2, n, 2 * n), BF16),
-        pltpu.VMEM((GROUP, 2, n, 2 * n), F32),
+        pltpu.VMEM((count // group_size, 2, group_size, n, LANES), F32),
+        pltpu.VMEM((group_size, 2, n, n), F32),
+        pltpu.VMEM((group_size, 2, 2 * n, n), BF16),
+        pltpu.VMEM((group_size, 2, n, 2 * n), BF16),
+        pltpu.VMEM((group_size, 2, n, 2 * n), F32),
         pltpu.SemaphoreType.DMA((12,)),
     ]
     return pl.pallas_call(
-        functools.partial(windows_kernel, first, amp_first),
+        functools.partial(windows_kernel, first, amp_first, group_size),
         grid_spec=pltpu.PrefetchScalarGridSpec(
             num_scalar_prefetch=1,
-            grid=(count // GROUP,),
+            grid=(count // group_size,),
             in_specs=[anywhere] * len(inputs),
             out_specs=[anywhere] * len(shapes),
             scratch_shapes=scratch,
         ),
         out_shape=[jax.ShapeDtypeStruct(s, F32) for s in shapes],
-        compiler_params=pltpu.CompilerParams(vmem_limit_bytes=(48 if first else 20) << 20),
+        compiler_params=pltpu.CompilerParams(vmem_limit_bytes=(48 if first else 27) << 20),
         name="near" if first else "across",
     )(offs, *inputs)
 

time: 67.3 us -> 67.1 us (level)
  no operation moved by 1% of the time
where the time goes in v6:
time: 67.1 us; the launch traced here: 67 us
  starting transfers between devices  22.3 us (33%)
  waiting for transfers between devices  20.5 us (31%)
  Pallas kernels  20.1 us (30%)
  local copies, waits for them, and re-layouts  2.56 us (4%)
  between operations  0.95 us (1%)
    pallas_call x2, Pallas kernels, windows(): pl.pallas_call(functools.partial(windows_kernel, first, amp_first, group_...  16.8 us
    ppermute x7, waiting for transfers between devices, swap(): return lax.ppermute(x, 'row', [(i, i ^ bit) for i in range(size)])  11.3 us
    ppermute x7, starting transfers between devices, swap(): return lax.ppermute(x, 'row', [(i, i ^ bit) for i in range(size)])  10.1 us
    ppermute x6, starting transfers between devices, shift(): return lax.ppermute(x, 'row', [(i, (i + by) % size) for i in range(size)])  10.1 us
    ppermute x6, waiting for transfers between devices, shift(): return lax.ppermute(x, 'row', [(i, (i + by) % size) for i in range(size)])  9.23 us
    pallas_call x3, Pallas kernels, place(): pl.pallas_call(functools.partial(place_kernel, nears, scale), in_specs=in...  3.26 us
  transfers between devices with their start and end apart: 16, of which 7 were waited for; matrix products, arithmetic and copies ran while one was open for 1% of the time, Pallas kernels for 17%

profile of v6, /device:TPU:0, one launch (start us, length us, event | category | flops | bytes accessed | tf_op | source)
XLA Modules:
  0.0 67.0 jit_solution(5150495592978865410)
XLA Ops:
  0.7 1.3 %slice.91 = f32[2,256,384]{2,1,0:T(8,128)S(1)} slice(f32[2,512,384]{2,1,0:T(8,128)} %refs_0_.3), slice={[0:2], [0:256], [0:384]} | slice | bytes 1572864 | tf_op jit(solution)/shard_map/slice | solution.py:394
  1.9 1.3 %collective-permute-start = (f32[2,256,384]{2,1,0:T(8,128)S(1)}, f32[2,256,384]{2,1,0:T(8,128)S(1)}, u32[]{:S(2)}, u32[]{:S(2)}) collective-permute-start(f32[2,256,384]{2,1,0:T(8,128)S(1)} %slice.91), channel_id=1, source_target_pairs={{1,0},{2,1},{3,2},{4,3},{5,4},{6,5},{7,6},{8,7},{9,8},{10,9},{11,1... | collective-permute-start | bytes 2359304 | tf_op jit(solution)/shard_map/ppermute | solution.py:394
  3.5 1.1 %copy-done.3 = bf16[6,256,256]{2,1,0:T(8,128)(2,1)S(1)} copy-done((bf16[6,256,256]{2,1,0:T(8,128)(2,1)S(1)}, bf16[6,256,256]{2,1,0:T(8,128)(2,1)}, u32[]{:S(2)}) %copy-start.3) | copy-done | bytes 786456
  4.6 8.7 %near.1 = (f32[2,512,384]{2,1,0:T(8,128)S(1)}, f32[5,16,16,256]{3,2,1,0:T(8,128)S(1)}, f32[8,256]{1,0:T(8,128)S(1)}) custom-call(s32[9,2]{1,0:T(8,128)S(1)} %pad_add_fusion.off_ref, f32[2,512,384]{2,1,0:T(8,128)} %refs_0_.3, f32[2,2,256,256]{3,2,1,0:T(8,128)S(1)} %copy-done.2, f32[8,256,256]{2,1,0:T(8,128)} %refs_2_.3, bf16[6,256,256]{2,1,0:T(8,128)(2,1)S(1)} %copy-done.3), custom_call_target="tpu_custom_call" | custom-call | tf_op jit(solution)/shard_map/near/pallas_call | solution.py:300
  13.3 8.1 %across.1 = (f32[2,512,384]{2,1,0:T(8,128)}, f32[2,256,384]{2,1,0:T(8,128)S(1)}, f32[8,168,128]{2,1,0:T(8,128)S(1)}, f32[8,168,128]{2,1,0:T(8,128)S(1)}) custom-call(s32[9,2]{1,0:T(8,128)S(1)} %pad_add_fusion.off_ref, f32[2,512,384]{2,1,0:T(8,128)S(1)} %copy-done, f32[2,2,256,256]{3,2,1,0:T(8,128)S(1)} %copy-done.2, f32[8,256,256]{2,1,0:T(8,128)S(1)} %copy-done.1, ...), custom_call_target="tpu_custom_call" | custom-call | tf_op jit(solution)/shard_map/across/pallas_call | solution.py:300
  21.5 3.3 %collective-permute-start.1 = (f32[8,168,128]{2,1,0:T(8,128)S(1)}, f32[8,168,128]{2,1,0:T(8,128)S(1)}, u32[]{:S(2)}, u32[]{:S(2)}) collective-permute-start(f32[8,168,128]{2,1,0:T(8,128)S(1)} %get-tuple-element.33), channel_id=1, source_target_pairs={{0,1},{1,0},{2,3},{3,2},{4,5},{5,4},{6,7},{7,6},{8,9},{9,8},{10,11... | collective-permute-start | bytes 2064392 | tf_op jit(solution)/shard_map/ppermute | solution.py:372
  24.8 0.7 %collective-permute-start.3 = (f32[2,256,384]{2,1,0:T(8,128)S(1)}, f32[2,256,384]{2,1,0:T(8,128)S(1)}, u32[]{:S(2)}, u32[]{:S(2)}) collective-permute-start(f32[2,256,384]{2,1,0:T(8,128)S(1)} %get-tuple-element.34), channel_id=1, source_target_pairs={{3,7},{7,11},{11,15},{19,23},{23,27},{27,31}} | collective-permute-start | bytes 2359304 | tf_op jit(solution)/shard_map/ppermute | solution.py:400
  25.5 1.1 %collective-permute-done.1 = f32[8,168,128]{2,1,0:T(8,128)S(1)} collective-permute-done((f32[8,168,128]{2,1,0:T(8,128)S(1)}, f32[8,168,128]{2,1,0:T(8,128)S(1)}, u32[]{:S(2)}, u32[]{:S(2)}) %collective-permute-start.1) | collective-permute-done | bytes 688160 | tf_op jit(solution)/shard_map/ppermute | solution.py:372
  26.6 2.5 %collective-permute-start.4 = (f32[3,168,128]{2,1,0:T(8,128)S(1)}, f32[3,168,128]{2,1,0:T(8,128)S(1)}, u32[]{:S(2)}, u32[]{:S(2)}) collective-permute-start(f32[3,168,128]{2,1,0:T(8,128)S(1)} %slice_add_fusion), channel_id=1, source_target_pairs={{0,2},{1,3},{2,0},{3,1},{4,6},{5,7},{6,4},{7,5},{8,10},{9,11},{10,... | collective-permute-start | bytes 774152 | tf_op jit(solution)/shard_map/ppermute | solution.py:372
  29.2 6.2 %collective-permute-done.4 = f32[3,168,128]{2,1,0:T(8,128)S(1)} collective-permute-done((f32[3,168,128]{2,1,0:T(8,128)S(1)}, f32[3,168,128]{2,1,0:T(8,128)S(1)}, u32[]{:S(2)}, u32[]{:S(2)}) %collective-permute-start.4) | collective-permute-done | bytes 258080 | tf_op jit(solution)/shard_map/ppermute | solution.py:372
  35.5 1.6 %collective-permute-start.5 = (f32[168,128]{1,0:T(8,128)S(1)}, f32[168,128]{1,0:T(8,128)S(1)}, u32[]{:S(2)}, u32[]{:S(2)}) collective-permute-start(f32[168,128]{1,0:T(8,128)S(1)} %get-tuple-element.45), channel_id=1, source_target_pairs={{0,4},{1,5},{2,6},{3,7},{4,8},{5,9},{6,10},{7,11},{8,12},{9,13},{1... | collective-permute-start | bytes 258056 | tf_op jit(solution)/shard_map/ppermute | solution.py:377
  37.1 3.1 %collective-permute-start.6 = (f32[168,128]{1,0:T(8,128)S(1)}, f32[168,128]{1,0:T(8,128)S(1)}, u32[]{:S(2)}, u32[]{:S(2)}) collective-permute-start(f32[168,128]{1,0:T(8,128)S(1)} %get-tuple-element.47), channel_id=1, source_target_pairs={{0,8},{1,9},{2,10},{3,11},{4,12},{5,13},{6,14},{7,15},{8,0},{9,1},... | collective-permute-start | bytes 258056 | tf_op jit(solution)/shard_map/ppermute | solution.py:377
  40.2 1.5 %collective-permute-start.7 = (f32[168,128]{1,0:T(8,128)S(1)}, f32[168,128]{1,0:T(8,128)S(1)}, u32[]{:S(2)}, u32[]{:S(2)}) collective-permute-start(f32[168,128]{1,0:T(8,128)S(1)} %get-tuple-element.46), channel_id=1, source_target_pairs={{0,12},{1,13},{2,14},{3,15},{4,0},{5,1},{6,2},{7,3},{8,4},{9,5},{1... | collective-permute-start | bytes 258056 | tf_op jit(solution)/shard_map/ppermute | solution.py:377
  41.8 1.1 %collective-permute-done.5 = f32[168,128]{1,0:T(8,128)S(1)} collective-permute-done((f32[168,128]{1,0:T(8,128)S(1)}, f32[168,128]{1,0:T(8,128)S(1)}, u32[]{:S(2)}, u32[]{:S(2)}) %collective-permute-start.5) | collective-permute-done | bytes 86048 | tf_op jit(solution)/shard_map/ppermute | solution.py:377
  42.9 3.7 %collective-permute-done.6 = f32[168,128]{1,0:T(8,128)S(1)} collective-permute-done((f32[168,128]{1,0:T(8,128)S(1)}, f32[168,128]{1,0:T(8,128)S(1)}, u32[]{:S(2)}, u32[]{:S(2)}) %collective-permute-start.6) | collective-permute-done | bytes 86048 | tf_op jit(solution)/shard_map/ppermute | solution.py:377
  46.8 3.1 %collective-permute-start.8 = (f32[4,16,256]{2,1,0:T(8,128)S(1)}, f32[4,16,256]{2,1,0:T(8,128)S(1)}, u32[]{:S(2)}, u32[]{:S(2)}) collective-permute-start(f32[4,16,256]{2,1,0:T(8,128)S(1)} %get-tuple-element.49), channel_id=1, source_target_pairs={{0,12},{1,13},{2,14},{3,15},{4,0},{5,1},{6,2},{7,3},{8,4},{9,5},{1... | collective-permute-start | bytes 196616 | tf_op jit(solution)/shard_map/ppermute | solution.py:377
  49.8 0.9 %collective-permute-start.9 = (f32[4,16,256]{2,1,0:T(8,128)S(1)}, f32[4,16,256]{2,1,0:T(8,128)S(1)}, u32[]{:S(2)}, u32[]{:S(2)}) collective-permute-start(f32[4,16,256]{2,1,0:T(8,128)S(1)} %get-tuple-element.49), channel_id=1, source_target_pairs={{0,8},{1,9},{2,10},{3,11},{4,12},{5,13},{6,14},{7,15},{8,0},{9,1},... | collective-permute-start | bytes 196616 | tf_op jit(solution)/shard_map/ppermute | solution.py:377
  50.7 2.0 %collective-permute-start.12 = (f32[4,16,256]{2,1,0:T(8,128)S(1)}, f32[4,16,256]{2,1,0:T(8,128)S(1)}, u32[]{:S(2)}, u32[]{:S(2)}) collective-permute-start(f32[4,16,256]{2,1,0:T(8,128)S(1)} %get-tuple-element.49), channel_id=1, source_target_pairs={{0,2},{1,3},{2,0},{3,1},{4,6},{5,7},{6,4},{7,5},{8,10},{9,11},{10,... | collective-permute-start | bytes 196616 | tf_op jit(solution)/shard_map/ppermute | solution.py:372
  52.8 4.4 %collective-permute-done.9 = f32[4,16,256]{2,1,0:T(8,128)S(1)} collective-permute-done((f32[4,16,256]{2,1,0:T(8,128)S(1)}, f32[4,16,256]{2,1,0:T(8,128)S(1)}, u32[]{:S(2)}, u32[]{:S(2)}) %collective-permute-start.9) | collective-permute-done | bytes 65568 | tf_op jit(solution)/shard_map/ppermute | solution.py:377
  57.2 2.1 %collective-permute-start.13 = (f32[3,4,16,256]{3,2,1,0:T(8,128)S(1)}, f32[3,4,16,256]{3,2,1,0:T(8,128)S(1)}, u32[]{:S(2)}, u32[]{:S(2)}) collective-permute-start(f32[3,4,16,256]{3,2,1,0:T(8,128)S(1)} %pad_maximum_fusion.2), channel_id=1, source_target_pairs={{0,2},{1,3},{2,0},{3,1},{4,6},{5,7},{6,4},{7,5},{8,10},{9,11},{10,... | collective-permute-start | bytes 589832 | tf_op jit(solution)/shard_map/ppermute | solution.py:372
  59.4 1.4 %place.3 = (f32[4,16,16,256]{3,2,1,0:T(8,128)}, f32[1]{0:T(128)}) custom-call(s32[1]{0:T(128)} %bitcast.me_ref, f32[4,4,16,256]{3,2,1,0:T(8,128)S(1)} %pad_maximum_fusion.refs_0_, f32[4,8,128]{2,1,0:T(8,128)S(1)} %pad_maximum_fusion.4.refs_1_), custom_call_target="tpu_custom_call" | custom-call | tf_op jit(solution)/shard_map/place/pallas_call | solution.py:355
  60.8 3.6 %collective-permute-done.13 = f32[3,4,16,256]{3,2,1,0:T(8,128)S(1)} collective-permute-done((f32[3,4,16,256]{3,2,1,0:T(8,128)S(1)}, f32[3,4,16,256]{3,2,1,0:T(8,128)S(1)}, u32[]{:S(2)}, u32[]{:S(2)}) %collective-permute-start.13) | collective-permute-done | bytes 196640 | tf_op jit(solution)/shard_map/ppermute | solution.py:372
  64.7 1.1 %place.4.refs_1_ = f32[4,16,16,256]{3,2,1,0:T(8,128)} custom-call(s32[1]{0:T(128)} %bitcast.me_ref, f32[4,4,16,256]{3,2,1,0:T(8,128)S(1)} %collective-permute-done.15.refs_0_, f32[4,4,16,256]{3,2,1,0:T(8,128)S(1)} %pad_maximum_fusion.1.refs_1_, f32[4,16,16,256]{3,2,1,0:T(8,128)} %get-tuple-element.41.refs_2_), custom_call_target="tpu_custom_call", output_to_operand_aliasing={{}: (3, {})} | custom-call | tf_op jit(solution)/shard_map/place/pallas_call | solution.py:355
  66.2 0.8 %place.5 = f32[4,16,16,256]{3,2,1,0:T(8,128)} custom-call(s32[1]{0:T(128)} %bitcast.me_ref, f32[4,4,16,256]{3,2,1,0:T(8,128)S(1)} %collective-permute-done.14.refs_0_, f32[4,16,16,256]{3,2,1,0:T(8,128)} %place.4.refs_1_), custom_call_target="tpu_custom_call", output_to_operand_aliasing={{}: (2, {})} | custom-call | tf_op jit(solution)/shard_map/place/pallas_call | solution.py:355
  (53 shorter events, 1.5 us)
Async XLA Ops:
  0.6 2.6 %copy-start.6 = (s32[8,2]{0,1:T(2,128)S(1)}, s32[8,2]{0,1:T(2,128)}, u32[]{:S(2)}) copy-start(s32[8,2]{0,1:T(2,128)} %param.10) | copy-start | bytes 196
  0.6 2.9 %copy-start.2 = (f32[2,2,256,256]{3,2,1,0:T(8,128)S(1)}, f32[2,2,256,256]{3,2,1,0:T(8,128)}, u32[]{:S(2)}) copy-start(f32[2,2,256,256]{3,2,1,0:T(8,128)} %refs_1_.3) | copy-start | bytes 3145732
  1.9 11.4 %collective-permute-start = (f32[2,256,384]{2,1,0:T(8,128)S(1)}, f32[2,256,384]{2,1,0:T(8,128)S(1)}, u32[]{:S(2)}, u32[]{:S(2)}) collective-permute-start(f32[2,256,384]{2,1,0:T(8,128)S(1)} %slice.91), channel_id=1, source_target_pairs={{1,0},{2,1},{3,2},{4,3},{5,4},{6,5},{7,6},{8,7},{9,8},{10,9},{11,1... | collective-permute-start | bytes 2359304 | tf_op jit(solution)/shard_map/ppermute | solution.py:394
  3.5 1.1 %copy-start.3 = (bf16[6,256,256]{2,1,0:T(8,128)(2,1)S(1)}, bf16[6,256,256]{2,1,0:T(8,128)(2,1)}, u32[]{:S(2)}) copy-start(bf16[6,256,256]{2,1,0:T(8,128)(2,1)} %constant.51.clone.refs_3_) | copy-start | bytes 2359300
  4.6 8.7 %copy-start = (f32[2,512,384]{2,1,0:T(8,128)S(1)}, f32[2,512,384]{2,1,0:T(8,128)}, u32[]{:S(2)}) copy-start(f32[2,512,384]{2,1,0:T(8,128)} %refs_0_.3) | copy-start | bytes 4718596
  4.6 8.7 %copy-start.1 = (f32[8,256,256]{2,1,0:T(8,128)S(1)}, f32[8,256,256]{2,1,0:T(8,128)}, u32[]{:S(2)}) copy-start(f32[8,256,256]{2,1,0:T(8,128)} %refs_2_.3) | copy-start | bytes 6291460
  21.5 5.1 %collective-permute-start.1 = (f32[8,168,128]{2,1,0:T(8,128)S(1)}, f32[8,168,128]{2,1,0:T(8,128)S(1)}, u32[]{:S(2)}, u32[]{:S(2)}) collective-permute-start(f32[8,168,128]{2,1,0:T(8,128)S(1)} %get-tuple-element.33), channel_id=1, source_target_pairs={{0,1},{1,0},{2,3},{3,2},{4,5},{5,4},{6,7},{7,6},{8,9},{9,8},{10,11... | collective-permute-start | bytes 2064392 | tf_op jit(solution)/shard_map/ppermute | solution.py:372
  24.8 10.7 %collective-permute-start.3 = (f32[2,256,384]{2,1,0:T(8,128)S(1)}, f32[2,256,384]{2,1,0:T(8,128)S(1)}, u32[]{:S(2)}, u32[]{:S(2)}) collective-permute-start(f32[2,256,384]{2,1,0:T(8,128)S(1)} %get-tuple-element.34), channel_id=1, source_target_pairs={{3,7},{7,11},{11,15},{19,23},{23,27},{27,31}} | collective-permute-start | bytes 2359304 | tf_op jit(solution)/shard_map/ppermute | solution.py:400
  26.6 8.8 %collective-permute-start.4 = (f32[3,168,128]{2,1,0:T(8,128)S(1)}, f32[3,168,128]{2,1,0:T(8,128)S(1)}, u32[]{:S(2)}, u32[]{:S(2)}) collective-permute-start(f32[3,168,128]{2,1,0:T(8,128)S(1)} %slice_add_fusion), channel_id=1, source_target_pairs={{0,2},{1,3},{2,0},{3,1},{4,6},{5,7},{6,4},{7,5},{8,10},{9,11},{10,... | collective-permute-start | bytes 774152 | tf_op jit(solution)/shard_map/ppermute | solution.py:372
  29.1 12.8 %collective-permute-start.2 = (f32[168,128]{1,0:T(8,128)S(1)}, f32[168,128]{1,0:T(8,128)S(1)}, u32[]{:S(2)}, u32[]{:S(2)}) collective-permute-start(f32[168,128]{1,0:T(8,128)S(1)} %fusion.1), channel_id=1, source_target_pairs={{0,2},{1,3},{2,0},{3,1},{4,6},{5,7},{6,4},{7,5},{8,10},{9,11},{10,... | collective-permute-start | bytes 258056 | tf_op jit(solution)/shard_map/ppermute | solution.py:372
  35.5 7.4 %collective-permute-start.5 = (f32[168,128]{1,0:T(8,128)S(1)}, f32[168,128]{1,0:T(8,128)S(1)}, u32[]{:S(2)}, u32[]{:S(2)}) collective-permute-start(f32[168,128]{1,0:T(8,128)S(1)} %get-tuple-element.45), channel_id=1, source_target_pairs={{0,4},{1,5},{2,6},{3,7},{4,8},{5,9},{6,10},{7,11},{8,12},{9,13},{1... | collective-permute-start | bytes 258056 | tf_op jit(solution)/shard_map/ppermute | solution.py:377
  37.1 9.6 %collective-permute-start.6 = (f32[168,128]{1,0:T(8,128)S(1)}, f32[168,128]{1,0:T(8,128)S(1)}, u32[]{:S(2)}, u32[]{:S(2)}) collective-permute-start(f32[168,128]{1,0:T(8,128)S(1)} %get-tuple-element.47), channel_id=1, source_target_pairs={{0,8},{1,9},{2,10},{3,11},{4,12},{5,13},{6,14},{7,15},{8,0},{9,1},... | collective-permute-start | bytes 258056 | tf_op jit(solution)/shard_map/ppermute | solution.py:377
  40.2 6.5 %collective-permute-start.7 = (f32[168,128]{1,0:T(8,128)S(1)}, f32[168,128]{1,0:T(8,128)S(1)}, u32[]{:S(2)}, u32[]{:S(2)}) collective-permute-start(f32[168,128]{1,0:T(8,128)S(1)} %get-tuple-element.46), channel_id=1, source_target_pairs={{0,12},{1,13},{2,14},{3,15},{4,0},{5,1},{6,2},{7,3},{8,4},{9,5},{1... | collective-permute-start | bytes 258056 | tf_op jit(solution)/shard_map/ppermute | solution.py:377
  41.8 22.7 %copy-start.4 = (f32[2,512,384]{2,1,0:T(8,128)S(1)}, f32[2,512,384]{2,1,0:T(8,128)}, u32[]{:S(2)}) copy-start(f32[2,512,384]{2,1,0:T(8,128)} %get-tuple-element.37) | copy-start | bytes 4718596
  41.8 22.6 %collective-permute-start.11 = (f32[2,256,384]{2,1,0:T(8,128)S(1)}, f32[2,256,384]{2,1,0:T(8,128)S(1)}, u32[]{:S(2)}, u32[]{:S(2)}) collective-permute-start(f32[2,256,384]{2,1,0:T(8,128)S(1)} %broadcast_select_fusion), channel_id=1, source_target_pairs={{0,1},{1,2},{2,3},{3,0},{4,5},{5,6},{6,7},{7,4},{8,9},{9,10},{10,1... | collective-permute-start | bytes 2359304 | tf_op jit(solution)/shard_map/ppermute | solution.py:409
  46.8 6.0 %collective-permute-start.8 = (f32[4,16,256]{2,1,0:T(8,128)S(1)}, f32[4,16,256]{2,1,0:T(8,128)S(1)}, u32[]{:S(2)}, u32[]{:S(2)}) collective-permute-start(f32[4,16,256]{2,1,0:T(8,128)S(1)} %get-tuple-element.49), channel_id=1, source_target_pairs={{0,12},{1,13},{2,14},{3,15},{4,0},{5,1},{6,2},{7,3},{8,4},{9,5},{1... | collective-permute-start | bytes 196616 | tf_op jit(solution)/shard_map/ppermute | solution.py:377
  49.8 7.3 %collective-permute-start.9 = (f32[4,16,256]{2,1,0:T(8,128)S(1)}, f32[4,16,256]{2,1,0:T(8,128)S(1)}, u32[]{:S(2)}, u32[]{:S(2)}) collective-permute-start(f32[4,16,256]{2,1,0:T(8,128)S(1)} %get-tuple-element.49), channel_id=1, source_target_pairs={{0,8},{1,9},{2,10},{3,11},{4,12},{5,13},{6,14},{7,15},{8,0},{9,1},... | collective-permute-start | bytes 196616 | tf_op jit(solution)/shard_map/ppermute | solution.py:377
  50.7 6.5 %collective-permute-start.10 = (f32[4,16,256]{2,1,0:T(8,128)S(1)}, f32[4,16,256]{2,1,0:T(8,128)S(1)}, u32[]{:S(2)}, u32[]{:S(2)}) collective-permute-start(f32[4,16,256]{2,1,0:T(8,128)S(1)} %get-tuple-element.49), channel_id=1, source_target_pairs={{0,4},{1,5},{2,6},{3,7},{4,8},{5,9},{6,10},{7,11},{8,12},{9,13},{1... | collective-permute-start | bytes 196616 | tf_op jit(solution)/shard_map/ppermute | solution.py:377
  50.7 10.1 %collective-permute-start.12 = (f32[4,16,256]{2,1,0:T(8,128)S(1)}, f32[4,16,256]{2,1,0:T(8,128)S(1)}, u32[]{:S(2)}, u32[]{:S(2)}) collective-permute-start(f32[4,16,256]{2,1,0:T(8,128)S(1)} %get-tuple-element.49), channel_id=1, source_target_pairs={{0,2},{1,3},{2,0},{3,1},{4,6},{5,7},{6,4},{7,5},{8,10},{9,11},{10,... | collective-permute-start | bytes 196616 | tf_op jit(solution)/shard_map/ppermute | solution.py:372
  57.2 7.2 %collective-permute-start.13 = (f32[3,4,16,256]{3,2,1,0:T(8,128)S(1)}, f32[3,4,16,256]{3,2,1,0:T(8,128)S(1)}, u32[]{:S(2)}, u32[]{:S(2)}) collective-permute-start(f32[3,4,16,256]{3,2,1,0:T(8,128)S(1)} %pad_maximum_fusion.2), channel_id=1, source_target_pairs={{0,2},{1,3},{2,0},{3,1},{4,6},{5,7},{6,4},{7,5},{8,10},{9,11},{10,... | collective-permute-start | bytes 589832 | tf_op jit(solution)/shard_map/ppermute | solution.py:372
  59.3 5.4 %collective-permute-start.15 = (f32[4,4,16,256]{3,2,1,0:T(8,128)S(1)}, f32[4,4,16,256]{3,2,1,0:T(8,128)S(1)}, u32[]{:S(2)}, u32[]{:S(2)}) collective-permute-start(f32[4,4,16,256]{3,2,1,0:T(8,128)S(1)} %pad_maximum_fusion.refs_0_), channel_id=1, source_target_pairs={{0,1},{1,0},{2,3},{3,2},{4,5},{5,4},{6,7},{7,6},{8,9},{9,8},{10,11... | collective-permute-start | bytes 786440 | tf_op jit(solution)/shard_map/ppermute | solution.py:372
  64.6 2.4 %copy-start.5 = (f32[2,512,384]{2,1,0:T(8,128)}, f32[2,512,384]{2,1,0:T(8,128)S(1)}, u32[]{:S(2)}) copy-start(f32[2,512,384]{2,1,0:T(8,128)S(1)} %add_dynamic-update-slice_fusion) | copy-start | bytes 4718596
  64.6 1.6 %collective-permute-start.14 = (f32[4,4,16,256]{3,2,1,0:T(8,128)S(1)}, f32[4,4,16,256]{3,2,1,0:T(8,128)S(1)}, u32[]{:S(2)}, u32[]{:S(2)}) collective-permute-start(f32[4,4,16,256]{3,2,1,0:T(8,128)S(1)} %pad_maximum_fusion.1.refs_1_), channel_id=1, source_target_pairs={{0,1},{1,0},{2,3},{3,2},{4,5},{5,4},{6,7},{7,6},{8,9},{9,8},{10,11... | collective-permute-start | bytes 786440 | tf_op jit(solution)/shard_map/ppermute | solution.py:372

commit v7 on v6

--- a/solution.py
+++ b/solution.py
@@ -12,7 +12,6 @@
 
 F32, BF16 = jnp.float32, jnp.bfloat16
 LANES = 128
-GROUP = 2
 VMEM_MIB = 30
 
 
@@ -272,7 +271,7 @@
 def windows(first, shards, count, offs, object_field, probe, amplitude, amp_first, table, carried=()):
     n = probe.shape[-1]
     width = object_field.shape[2]
-    group_size = GROUP if first else count
+    group_size = count
     sums = (5, shards, n // shards, n)
     hbm, anywhere = pl.BlockSpec(memory_space=pltpu.HBM), pl.BlockSpec(memory_space=pl.ANY)
     inputs = (object_field, probe, amplitude, table, *carried)

time: 67.1 us -> 67 us (level)
  transfers between devices with their start and end apart: 16 -> 16, of which waited for: 7 -> 7; matrix products, arithmetic and copies ran while one was open for 1% -> 1% of each run, Pallas kernels for 17% -> 16%
where the time goes in v7:
time: 67 us; the launch traced here: 66.8 us
  starting transfers between devices  22.9 us (34%)
  waiting for transfers between devices  19.9 us (30%)
  Pallas kernels  19.8 us (30%)
  local copies, waits for them, and re-layouts  2.56 us (4%)
  between operations  0.95 us (1%)
    pallas_call x2, Pallas kernels, windows(): pl.pallas_call(functools.partial(windows_kernel, first, amp_first, group_...  16.5 us
    ppermute x7, waiting for transfers between devices, swap(): return lax.ppermute(x, 'row', [(i, i ^ bit) for i in range(size)])  11 us
    ppermute x7, starting transfers between devices, swap(): return lax.ppermute(x, 'row', [(i, i ^ bit) for i in range(size)])  10.6 us
    ppermute x6, starting transfers between devices, shift(): return lax.ppermute(x, 'row', [(i, (i + by) % size) for i in range(size)])  10.3 us
    ppermute x6, waiting for transfers between devices, shift(): return lax.ppermute(x, 'row', [(i, (i + by) % size) for i in range(size)])  8.87 us
    pallas_call x3, Pallas kernels, place(): pl.pallas_call(functools.partial(place_kernel, nears, scale), in_specs=in...  3.26 us
  transfers between devices with their start and end apart: 16, of which 7 were waited for; matrix products, arithmetic and copies ran while one was open for 1% of the time, Pallas kernels for 16%

profile of v7, /device:TPU:0, one launch (start us, length us, event | category | flops | bytes accessed | tf_op | source)
XLA Modules:
  0.0 66.8 jit_solution(9568403646904303178)
XLA Ops:
  0.7 1.3 %slice.91 = f32[2,256,384]{2,1,0:T(8,128)S(1)} slice(f32[2,512,384]{2,1,0:T(8,128)} %refs_0_.3), slice={[0:2], [0:256], [0:384]} | slice | bytes 1572864 | tf_op jit(solution)/shard_map/slice | solution.py:393
  1.9 1.3 %collective-permute-start = (f32[2,256,384]{2,1,0:T(8,128)S(1)}, f32[2,256,384]{2,1,0:T(8,128)S(1)}, u32[]{:S(2)}, u32[]{:S(2)}) collective-permute-start(f32[2,256,384]{2,1,0:T(8,128)S(1)} %slice.91), channel_id=1, source_target_pairs={{1,0},{2,1},{3,2},{4,3},{5,4},{6,5},{7,6},{8,7},{9,8},{10,9},{11,1... | collective-permute-start | bytes 2359304 | tf_op jit(solution)/shard_map/ppermute | solution.py:393
  3.5 1.1 %copy-done.3 = bf16[6,256,256]{2,1,0:T(8,128)(2,1)S(1)} copy-done((bf16[6,256,256]{2,1,0:T(8,128)(2,1)S(1)}, bf16[6,256,256]{2,1,0:T(8,128)(2,1)}, u32[]{:S(2)}) %copy-start.3) | copy-done | bytes 786456
  4.6 8.5 %near.1 = (f32[2,512,384]{2,1,0:T(8,128)S(1)}, f32[5,16,16,256]{3,2,1,0:T(8,128)S(1)}, f32[8,256]{1,0:T(8,128)S(1)}) custom-call(s32[9,2]{1,0:T(8,128)S(1)} %pad_add_fusion.off_ref, f32[2,512,384]{2,1,0:T(8,128)} %refs_0_.3, f32[2,2,256,256]{3,2,1,0:T(8,128)S(1)} %copy-done.2, f32[8,256,256]{2,1,0:T(8,128)} %refs_2_.3, bf16[6,256,256]{2,1,0:T(8,128)(2,1)S(1)} %copy-done.3), custom_call_target="tpu_custom_call" | custom-call | tf_op jit(solution)/shard_map/near/pallas_call | solution.py:299
  13.1 8.1 %across.1 = (f32[2,512,384]{2,1,0:T(8,128)}, f32[2,256,384]{2,1,0:T(8,128)S(1)}, f32[8,168,128]{2,1,0:T(8,128)S(1)}, f32[8,168,128]{2,1,0:T(8,128)S(1)}) custom-call(s32[9,2]{1,0:T(8,128)S(1)} %pad_add_fusion.off_ref, f32[2,512,384]{2,1,0:T(8,128)S(1)} %copy-done, f32[2,2,256,256]{3,2,1,0:T(8,128)S(1)} %copy-done.2, f32[8,256,256]{2,1,0:T(8,128)S(1)} %copy-done.1, ...), custom_call_target="tpu_custom_call" | custom-call | tf_op jit(solution)/shard_map/across/pallas_call | solution.py:299
  21.2 3.5 %collective-permute-start.1 = (f32[8,168,128]{2,1,0:T(8,128)S(1)}, f32[8,168,128]{2,1,0:T(8,128)S(1)}, u32[]{:S(2)}, u32[]{:S(2)}) collective-permute-start(f32[8,168,128]{2,1,0:T(8,128)S(1)} %get-tuple-element.33), channel_id=1, source_target_pairs={{0,1},{1,0},{2,3},{3,2},{4,5},{5,4},{6,7},{7,6},{8,9},{9,8},{10,11... | collective-permute-start | bytes 2064392 | tf_op jit(solution)/shard_map/ppermute | solution.py:371
  24.7 0.7 %collective-permute-start.3 = (f32[2,256,384]{2,1,0:T(8,128)S(1)}, f32[2,256,384]{2,1,0:T(8,128)S(1)}, u32[]{:S(2)}, u32[]{:S(2)}) collective-permute-start(f32[2,256,384]{2,1,0:T(8,128)S(1)} %get-tuple-element.34), channel_id=1, source_target_pairs={{3,7},{7,11},{11,15},{19,23},{23,27},{27,31}} | collective-permute-start | bytes 2359304 | tf_op jit(solution)/shard_map/ppermute | solution.py:399
  25.4 1.1 %collective-permute-done.1 = f32[8,168,128]{2,1,0:T(8,128)S(1)} collective-permute-done((f32[8,168,128]{2,1,0:T(8,128)S(1)}, f32[8,168,128]{2,1,0:T(8,128)S(1)}, u32[]{:S(2)}, u32[]{:S(2)}) %collective-permute-start.1) | collective-permute-done | bytes 688160 | tf_op jit(solution)/shard_map/ppermute | solution.py:371
  26.5 2.5 %collective-permute-start.4 = (f32[3,168,128]{2,1,0:T(8,128)S(1)}, f32[3,168,128]{2,1,0:T(8,128)S(1)}, u32[]{:S(2)}, u32[]{:S(2)}) collective-permute-start(f32[3,168,128]{2,1,0:T(8,128)S(1)} %slice_add_fusion), channel_id=1, source_target_pairs={{0,2},{1,3},{2,0},{3,1},{4,6},{5,7},{6,4},{7,5},{8,10},{9,11},{10,... | collective-permute-start | bytes 774152 | tf_op jit(solution)/shard_map/ppermute | solution.py:371
  29.1 6.1 %collective-permute-done.4 = f32[3,168,128]{2,1,0:T(8,128)S(1)} collective-permute-done((f32[3,168,128]{2,1,0:T(8,128)S(1)}, f32[3,168,128]{2,1,0:T(8,128)S(1)}, u32[]{:S(2)}, u32[]{:S(2)}) %collective-permute-start.4) | collective-permute-done | bytes 258080 | tf_op jit(solution)/shard_map/ppermute | solution.py:371
  35.3 1.8 %collective-permute-start.5 = (f32[168,128]{1,0:T(8,128)S(1)}, f32[168,128]{1,0:T(8,128)S(1)}, u32[]{:S(2)}, u32[]{:S(2)}) collective-permute-start(f32[168,128]{1,0:T(8,128)S(1)} %get-tuple-element.45), channel_id=1, source_target_pairs={{0,4},{1,5},{2,6},{3,7},{4,8},{5,9},{6,10},{7,11},{8,12},{9,13},{1... | collective-permute-start | bytes 258056 | tf_op jit(solution)/shard_map/ppermute | solution.py:376
  37.1 2.9 %collective-permute-start.6 = (f32[168,128]{1,0:T(8,128)S(1)}, f32[168,128]{1,0:T(8,128)S(1)}, u32[]{:S(2)}, u32[]{:S(2)}) collective-permute-start(f32[168,128]{1,0:T(8,128)S(1)} %get-tuple-element.47), channel_id=1, source_target_pairs={{0,8},{1,9},{2,10},{3,11},{4,12},{5,13},{6,14},{7,15},{8,0},{9,1},... | collective-permute-start | bytes 258056 | tf_op jit(solution)/shard_map/ppermute | solution.py:376
  40.0 1.7 %collective-permute-start.7 = (f32[168,128]{1,0:T(8,128)S(1)}, f32[168,128]{1,0:T(8,128)S(1)}, u32[]{:S(2)}, u32[]{:S(2)}) collective-permute-start(f32[168,128]{1,0:T(8,128)S(1)} %get-tuple-element.46), channel_id=1, source_target_pairs={{0,12},{1,13},{2,14},{3,15},{4,0},{5,1},{6,2},{7,3},{8,4},{9,5},{1... | collective-permute-start | bytes 258056 | tf_op jit(solution)/shard_map/ppermute | solution.py:376
  41.9 0.5 collective-permute-done.5
  42.4 4.1 %collective-permute-done.6 = f32[168,128]{1,0:T(8,128)S(1)} collective-permute-done((f32[168,128]{1,0:T(8,128)S(1)}, f32[168,128]{1,0:T(8,128)S(1)}, u32[]{:S(2)}, u32[]{:S(2)}) %collective-permute-start.6) | collective-permute-done | bytes 86048 | tf_op jit(solution)/shard_map/ppermute | solution.py:376
  46.6 3.3 %collective-permute-start.8 = (f32[4,16,256]{2,1,0:T(8,128)S(1)}, f32[4,16,256]{2,1,0:T(8,128)S(1)}, u32[]{:S(2)}, u32[]{:S(2)}) collective-permute-start(f32[4,16,256]{2,1,0:T(8,128)S(1)} %get-tuple-element.49), channel_id=1, source_target_pairs={{0,12},{1,13},{2,14},{3,15},{4,0},{5,1},{6,2},{7,3},{8,4},{9,5},{1... | collective-permute-start | bytes 196616 | tf_op jit(solution)/shard_map/ppermute | solution.py:376
  49.9 0.6 collective-permute-start.9
  50.5 2.1 %collective-permute-start.12 = (f32[4,16,256]{2,1,0:T(8,128)S(1)}, f32[4,16,256]{2,1,0:T(8,128)S(1)}, u32[]{:S(2)}, u32[]{:S(2)}) collective-permute-start(f32[4,16,256]{2,1,0:T(8,128)S(1)} %get-tuple-element.49), channel_id=1, source_target_pairs={{0,2},{1,3},{2,0},{3,1},{4,6},{5,7},{6,4},{7,5},{8,10},{9,11},{10,... | collective-permute-start | bytes 196616 | tf_op jit(solution)/shard_map/ppermute | solution.py:371
  52.7 4.3 %collective-permute-done.9 = f32[4,16,256]{2,1,0:T(8,128)S(1)} collective-permute-done((f32[4,16,256]{2,1,0:T(8,128)S(1)}, f32[4,16,256]{2,1,0:T(8,128)S(1)}, u32[]{:S(2)}, u32[]{:S(2)}) %collective-permute-start.9) | collective-permute-done | bytes 65568 | tf_op jit(solution)/shard_map/ppermute | solution.py:376
  57.0 2.2 %collective-permute-start.13 = (f32[3,4,16,256]{3,2,1,0:T(8,128)S(1)}, f32[3,4,16,256]{3,2,1,0:T(8,128)S(1)}, u32[]{:S(2)}, u32[]{:S(2)}) collective-permute-start(f32[3,4,16,256]{3,2,1,0:T(8,128)S(1)} %pad_maximum_fusion.2), channel_id=1, source_target_pairs={{0,2},{1,3},{2,0},{3,1},{4,6},{5,7},{6,4},{7,5},{8,10},{9,11},{10,... | collective-permute-start | bytes 589832 | tf_op jit(solution)/shard_map/ppermute | solution.py:371
  59.3 1.4 %place.3 = (f32[4,16,16,256]{3,2,1,0:T(8,128)}, f32[1]{0:T(128)}) custom-call(s32[1]{0:T(128)} %bitcast.me_ref, f32[4,4,16,256]{3,2,1,0:T(8,128)S(1)} %pad_maximum_fusion.refs_0_, f32[4,8,128]{2,1,0:T(8,128)S(1)} %pad_maximum_fusion.4.refs_1_), custom_call_target="tpu_custom_call" | custom-call | tf_op jit(solution)/shard_map/place/pallas_call | solution.py:354
  60.7 3.4 %collective-permute-done.13 = f32[3,4,16,256]{3,2,1,0:T(8,128)S(1)} collective-permute-done((f32[3,4,16,256]{3,2,1,0:T(8,128)S(1)}, f32[3,4,16,256]{3,2,1,0:T(8,128)S(1)}, u32[]{:S(2)}, u32[]{:S(2)}) %collective-permute-start.13) | collective-permute-done | bytes 196640 | tf_op jit(solution)/shard_map/ppermute | solution.py:371
  64.5 1.1 %place.4.refs_1_ = f32[4,16,16,256]{3,2,1,0:T(8,128)} custom-call(s32[1]{0:T(128)} %bitcast.me_ref, f32[4,4,16,256]{3,2,1,0:T(8,128)S(1)} %collective-permute-done.15.refs_0_, f32[4,4,16,256]{3,2,1,0:T(8,128)S(1)} %pad_maximum_fusion.1.refs_1_, f32[4,16,16,256]{3,2,1,0:T(8,128)} %get-tuple-element.41.refs_2_), custom_call_target="tpu_custom_call", output_to_operand_aliasing={{}: (3, {})} | custom-call | tf_op jit(solution)/shard_map/place/pallas_call | solution.py:354
  66.0 0.8 %place.5 = f32[4,16,16,256]{3,2,1,0:T(8,128)} custom-call(s32[1]{0:T(128)} %bitcast.me_ref, f32[4,4,16,256]{3,2,1,0:T(8,128)S(1)} %collective-permute-done.14.refs_0_, f32[4,16,16,256]{3,2,1,0:T(8,128)} %place.4.refs_1_), custom_call_target="tpu_custom_call", output_to_operand_aliasing={{}: (2, {})} | custom-call | tf_op jit(solution)/shard_map/place/pallas_call | solution.py:354
  (53 shorter events, 1.5 us)
Async XLA Ops:
  0.6 2.6 %copy-start.6 = (s32[8,2]{0,1:T(2,128)S(1)}, s32[8,2]{0,1:T(2,128)}, u32[]{:S(2)}) copy-start(s32[8,2]{0,1:T(2,128)} %param.10) | copy-start | bytes 196
  0.6 2.9 %copy-start.2 = (f32[2,2,256,256]{3,2,1,0:T(8,128)S(1)}, f32[2,2,256,256]{3,2,1,0:T(8,128)}, u32[]{:S(2)}) copy-start(f32[2,2,256,256]{3,2,1,0:T(8,128)} %refs_1_.3) | copy-start | bytes 3145732
  1.9 11.2 %collective-permute-start = (f32[2,256,384]{2,1,0:T(8,128)S(1)}, f32[2,256,384]{2,1,0:T(8,128)S(1)}, u32[]{:S(2)}, u32[]{:S(2)}) collective-permute-start(f32[2,256,384]{2,1,0:T(8,128)S(1)} %slice.91), channel_id=1, source_target_pairs={{1,0},{2,1},{3,2},{4,3},{5,4},{6,5},{7,6},{8,7},{9,8},{10,9},{11,1... | collective-permute-start | bytes 2359304 | tf_op jit(solution)/shard_map/ppermute | solution.py:393
  3.5 1.1 %copy-start.3 = (bf16[6,256,256]{2,1,0:T(8,128)(2,1)S(1)}, bf16[6,256,256]{2,1,0:T(8,128)(2,1)}, u32[]{:S(2)}) copy-start(bf16[6,256,256]{2,1,0:T(8,128)(2,1)} %constant.51.clone.refs_3_) | copy-start | bytes 2359300
  4.6 8.5 %copy-start = (f32[2,512,384]{2,1,0:T(8,128)S(1)}, f32[2,512,384]{2,1,0:T(8,128)}, u32[]{:S(2)}) copy-start(f32[2,512,384]{2,1,0:T(8,128)} %refs_0_.3) | copy-start | bytes 4718596
  4.6 8.5 %copy-start.1 = (f32[8,256,256]{2,1,0:T(8,128)S(1)}, f32[8,256,256]{2,1,0:T(8,128)}, u32[]{:S(2)}) copy-start(f32[8,256,256]{2,1,0:T(8,128)} %refs_2_.3) | copy-start | bytes 6291460
  21.2 5.3 %collective-permute-start.1 = (f32[8,168,128]{2,1,0:T(8,128)S(1)}, f32[8,168,128]{2,1,0:T(8,128)S(1)}, u32[]{:S(2)}, u32[]{:S(2)}) collective-permute-start(f32[8,168,128]{2,1,0:T(8,128)S(1)} %get-tuple-element.33), channel_id=1, source_target_pairs={{0,1},{1,0},{2,3},{3,2},{4,5},{5,4},{6,7},{7,6},{8,9},{9,8},{10,11... | collective-permute-start | bytes 2064392 | tf_op jit(solution)/shard_map/ppermute | solution.py:371
  24.7 10.6 %collective-permute-start.3 = (f32[2,256,384]{2,1,0:T(8,128)S(1)}, f32[2,256,384]{2,1,0:T(8,128)S(1)}, u32[]{:S(2)}, u32[]{:S(2)}) collective-permute-start(f32[2,256,384]{2,1,0:T(8,128)S(1)} %get-tuple-element.34), channel_id=1, source_target_pairs={{3,7},{7,11},{11,15},{19,23},{23,27},{27,31}} | collective-permute-start | bytes 2359304 | tf_op jit(solution)/shard_map/ppermute | solution.py:399
  26.5 8.7 %collective-permute-start.4 = (f32[3,168,128]{2,1,0:T(8,128)S(1)}, f32[3,168,128]{2,1,0:T(8,128)S(1)}, u32[]{:S(2)}, u32[]{:S(2)}) collective-permute-start(f32[3,168,128]{2,1,0:T(8,128)S(1)} %slice_add_fusion), channel_id=1, source_target_pairs={{0,2},{1,3},{2,0},{3,1},{4,6},{5,7},{6,4},{7,5},{8,10},{9,11},{10,... | collective-permute-start | bytes 774152 | tf_op jit(solution)/shard_map/ppermute | solution.py:371
  29.0 12.9 %collective-permute-start.2 = (f32[168,128]{1,0:T(8,128)S(1)}, f32[168,128]{1,0:T(8,128)S(1)}, u32[]{:S(2)}, u32[]{:S(2)}) collective-permute-start(f32[168,128]{1,0:T(8,128)S(1)} %fusion.1), channel_id=1, source_target_pairs={{0,2},{1,3},{2,0},{3,1},{4,6},{5,7},{6,4},{7,5},{8,10},{9,11},{10,... | collective-permute-start | bytes 258056 | tf_op jit(solution)/shard_map/ppermute | solution.py:371
  35.3 7.1 %collective-permute-start.5 = (f32[168,128]{1,0:T(8,128)S(1)}, f32[168,128]{1,0:T(8,128)S(1)}, u32[]{:S(2)}, u32[]{:S(2)}) collective-permute-start(f32[168,128]{1,0:T(8,128)S(1)} %get-tuple-element.45), channel_id=1, source_target_pairs={{0,4},{1,5},{2,6},{3,7},{4,8},{5,9},{6,10},{7,11},{8,12},{9,13},{1... | collective-permute-start | bytes 258056 | tf_op jit(solution)/shard_map/ppermute | solution.py:376
  37.1 9.4 %collective-permute-start.6 = (f32[168,128]{1,0:T(8,128)S(1)}, f32[168,128]{1,0:T(8,128)S(1)}, u32[]{:S(2)}, u32[]{:S(2)}) collective-permute-start(f32[168,128]{1,0:T(8,128)S(1)} %get-tuple-element.47), channel_id=1, source_target_pairs={{0,8},{1,9},{2,10},{3,11},{4,12},{5,13},{6,14},{7,15},{8,0},{9,1},... | collective-permute-start | bytes 258056 | tf_op jit(solution)/shard_map/ppermute | solution.py:376
  40.0 6.5 %collective-permute-start.7 = (f32[168,128]{1,0:T(8,128)S(1)}, f32[168,128]{1,0:T(8,128)S(1)}, u32[]{:S(2)}, u32[]{:S(2)}) collective-permute-start(f32[168,128]{1,0:T(8,128)S(1)} %get-tuple-element.46), channel_id=1, source_target_pairs={{0,12},{1,13},{2,14},{3,15},{4,0},{5,1},{6,2},{7,3},{8,4},{9,5},{1... | collective-permute-start | bytes 258056 | tf_op jit(solution)/shard_map/ppermute | solution.py:376
  41.8 22.4 %copy-start.4 = (f32[2,512,384]{2,1,0:T(8,128)S(1)}, f32[2,512,384]{2,1,0:T(8,128)}, u32[]{:S(2)}) copy-start(f32[2,512,384]{2,1,0:T(8,128)} %get-tuple-element.37) | copy-start | bytes 4718596
  41.8 22.3 %collective-permute-start.11 = (f32[2,256,384]{2,1,0:T(8,128)S(1)}, f32[2,256,384]{2,1,0:T(8,128)S(1)}, u32[]{:S(2)}, u32[]{:S(2)}) collective-permute-start(f32[2,256,384]{2,1,0:T(8,128)S(1)} %broadcast_select_fusion), channel_id=1, source_target_pairs={{0,1},{1,2},{2,3},{3,0},{4,5},{5,6},{6,7},{7,4},{8,9},{9,10},{10,1... | collective-permute-start | bytes 2359304 | tf_op jit(solution)/shard_map/ppermute | solution.py:408
  46.6 6.1 %collective-permute-start.8 = (f32[4,16,256]{2,1,0:T(8,128)S(1)}, f32[4,16,256]{2,1,0:T(8,128)S(1)}, u32[]{:S(2)}, u32[]{:S(2)}) collective-permute-start(f32[4,16,256]{2,1,0:T(8,128)S(1)} %get-tuple-element.49), channel_id=1, source_target_pairs={{0,12},{1,13},{2,14},{3,15},{4,0},{5,1},{6,2},{7,3},{8,4},{9,5},{1... | collective-permute-start | bytes 196616 | tf_op jit(solution)/shard_map/ppermute | solution.py:376
  49.9 7.1 %collective-permute-start.9 = (f32[4,16,256]{2,1,0:T(8,128)S(1)}, f32[4,16,256]{2,1,0:T(8,128)S(1)}, u32[]{:S(2)}, u32[]{:S(2)}) collective-permute-start(f32[4,16,256]{2,1,0:T(8,128)S(1)} %get-tuple-element.49), channel_id=1, source_target_pairs={{0,8},{1,9},{2,10},{3,11},{4,12},{5,13},{6,14},{7,15},{8,0},{9,1},... | collective-permute-start | bytes 196616 | tf_op jit(solution)/shard_map/ppermute | solution.py:376
  50.5 6.5 %collective-permute-start.10 = (f32[4,16,256]{2,1,0:T(8,128)S(1)}, f32[4,16,256]{2,1,0:T(8,128)S(1)}, u32[]{:S(2)}, u32[]{:S(2)}) collective-permute-start(f32[4,16,256]{2,1,0:T(8,128)S(1)} %get-tuple-element.49), channel_id=1, source_target_pairs={{0,4},{1,5},{2,6},{3,7},{4,8},{5,9},{6,10},{7,11},{8,12},{9,13},{1... | collective-permute-start | bytes 196616 | tf_op jit(solution)/shard_map/ppermute | solution.py:376
  50.5 10.2 %collective-permute-start.12 = (f32[4,16,256]{2,1,0:T(8,128)S(1)}, f32[4,16,256]{2,1,0:T(8,128)S(1)}, u32[]{:S(2)}, u32[]{:S(2)}) collective-permute-start(f32[4,16,256]{2,1,0:T(8,128)S(1)} %get-tuple-element.49), channel_id=1, source_target_pairs={{0,2},{1,3},{2,0},{3,1},{4,6},{5,7},{6,4},{7,5},{8,10},{9,11},{10,... | collective-permute-start | bytes 196616 | tf_op jit(solution)/shard_map/ppermute | solution.py:371
  57.0 7.1 %collective-permute-start.13 = (f32[3,4,16,256]{3,2,1,0:T(8,128)S(1)}, f32[3,4,16,256]{3,2,1,0:T(8,128)S(1)}, u32[]{:S(2)}, u32[]{:S(2)}) collective-permute-start(f32[3,4,16,256]{3,2,1,0:T(8,128)S(1)} %pad_maximum_fusion.2), channel_id=1, source_target_pairs={{0,2},{1,3},{2,0},{3,1},{4,6},{5,7},{6,4},{7,5},{8,10},{9,11},{10,... | collective-permute-start | bytes 589832 | tf_op jit(solution)/shard_map/ppermute | solution.py:371
  59.2 5.2 %collective-permute-start.15 = (f32[4,4,16,256]{3,2,1,0:T(8,128)S(1)}, f32[4,4,16,256]{3,2,1,0:T(8,128)S(1)}, u32[]{:S(2)}, u32[]{:S(2)}) collective-permute-start(f32[4,4,16,256]{3,2,1,0:T(8,128)S(1)} %pad_maximum_fusion.refs_0_), channel_id=1, source_target_pairs={{0,1},{1,0},{2,3},{3,2},{4,5},{5,4},{6,7},{7,6},{8,9},{9,8},{10,11... | collective-permute-start | bytes 786440 | tf_op jit(solution)/shard_map/ppermute | solution.py:371
  64.4 2.4 %copy-start.5 = (f32[2,512,384]{2,1,0:T(8,128)}, f32[2,512,384]{2,1,0:T(8,128)S(1)}, u32[]{:S(2)}) copy-start(f32[2,512,384]{2,1,0:T(8,128)S(1)} %add_dynamic-update-slice_fusion) | copy-start | bytes 4718596
  64.4 1.6 %collective-permute-start.14 = (f32[4,4,16,256]{3,2,1,0:T(8,128)S(1)}, f32[4,4,16,256]{3,2,1,0:T(8,128)S(1)}, u32[]{:S(2)}, u32[]{:S(2)}) collective-permute-start(f32[4,4,16,256]{3,2,1,0:T(8,128)S(1)} %pad_maximum_fusion.1.refs_1_), channel_id=1, source_target_pairs={{0,1},{1,0},{2,3},{3,2},{4,5},{5,4},{6,7},{7,6},{8,9},{9,8},{10,11... | collective-permute-start | bytes 786440 | tf_op jit(solution)/shard_map/ppermute | solution.py:371
